TPU v7x, 128 devices: a whole 4x4x4 slice. The times are simulated.
128 devices in a mesh: chan: 8 (over x, z_hi), space: 16 (over z_lo, y, core).
Axes of the slice: x: 4, y: 4, z: 4 (z_hi: 2, z_lo: 2; z = z_hi * 2 + z_lo), core: 2. Of those that a mesh axis runs over, the one named last changes fastest.
Arguments:
- volume: bfloat16 [128, 128, 8, 256], P(None, 'space', None, 'chan'), may hold values from -6 to 6
- first_filters: bfloat16 [3, 3, 3, 256, 256], P(None, None, None, None, 'chan'), may hold values from -0.078125 to 0.078125
- second_filters: bfloat16 [3, 3, 3, 256, 256], replicated, may hold values from -0.078125 to 0.078125
- out_grad: bfloat16 [128, 128, 8, 256], P('chan', 'space'), may hold values from -6 to 6
Outputs:
- act_grad: bfloat16 [128, 128, 8, 256], P('chan', 'space')
- filter_grad: float32 [3, 3, 3, 256, 256], replicated
All inputs are finite; a program needn't handle non-finite values.
Results may differ from a plain program's by a relative error of at most 0.0055.
Values may be sent and summed in bfloat16 or wider, within the bound.
No kernel may reach another device: no remote copies, remote signals or barrier semaphores. Data moves between devices by JAX's collectives and lax.ppermute only.
A program may use at most 128 MiB of HBM per device.

v0:
```python
import math

import jax
import jax.numpy as jnp
import numpy as np
from jax import lax
from jax.experimental import pallas as pl
from jax.experimental.pallas import tpu as pltpu
from jax.sharding import Mesh
from jax.sharding import PartitionSpec as P

BF = jnp.bfloat16
F32 = jnp.float32
C = 256
NZ = 8
BX, BY = 16, 8
HALF = 3456
SLOT = 3584
CHIPS = ("chan", "slab")
VMEM = pl.BlockSpec(memory_space=pltpu.VMEM)
SMEM = pl.BlockSpec(memory_space=pltpu.SMEM)


def params(limit=60 << 20):
    return pltpu.CompilerParams(vmem_limit_bytes=limit)


def cost(flops, moved):
    return pl.CostEstimate(flops=int(flops), bytes_accessed=int(moved), transcendentals=0)


def dot_t(a, b):
    return lax.dot_general(a, b, (((1,), (1,)), ((), ())), preferred_element_type=F32)


def dot_n(a, b):
    return lax.dot_general(a, b, (((1,), (0,)), ((), ())), preferred_element_type=F32)


def pack_kernel(pick_ref, vol_ref, out_ref, wide_ref):
    pick = pick_ref[...]
    for quad in range(2):
        for z in range(NZ):
            rows = jnp.concatenate([vol_ref[quad * 4 + j, z] for j in range(4)], axis=0)
            wide_ref[pl.ds(quad * 8 + z, 176, stride=16), :] = dot_t(pick, rows)
    out_ref[...] = wide_ref[...].astype(BF)


def neighbours(value):
    z = lax.broadcasted_iota(jnp.int32, value.shape, 1)
    before = jnp.where(z == 0, 0.0, pltpu.roll(value, 1, 1))
    after = jnp.where(z == NZ - 1, 0.0, pltpu.roll(value, NZ - 1, 1))
    return before.astype(BF), after.astype(BF)


def layers_kernel(
    place_ref, near_ref, low_ref, high_ref, mine_ref, other_ref, w2_ref,
    grad_ref, gxl_ref, gxh_ref, gyl_ref, gyh_ref,
    keep_ref, send_ref, d3_ref,
    v3_ref, a3_ref, w1_ref, acc_ref, og_ref, dt_ref, g_ref,
):
    chan, space, core = place_ref[0], place_ref[1], place_ref[2]

    def place_filters(d, carry):
        owner = lax.rem(chan - d + 8, 8)
        for stack, half in ((mine_ref, core), (other_ref, 1 - core)):
            at = pl.multiple_of(owner * 32 + half * 16, 16)
            for t in range(27):
                w1_ref[t // 3, pl.ds(at, 16), (t % 3) * C : (t % 3 + 1) * C] = stack[d, t]
        return carry

    lax.fori_loop(0, 8, place_filters, 0)

    row = lax.broadcasted_iota(jnp.int32, (1024, C), 0)
    col = lax.broadcasted_iota(jnp.int32, (1024, C), 1)
    same = ((row >> 7) == (col >> 5)) & ((row & 31) == (col & 31))
    for j in range(4):
        sel = (same & (((row >> 5) & 3) == j)).astype(F32).astype(BF)
        for b in range(4):
            y = b * 4 + j - 1
            if y < 0 or y >= 14:
                continue
            src = (low_ref, near_ref, near_ref, high_ref)[b]
            at = 8 if b == 2 else 0
            rows = jnp.concatenate(
                [src[c, :, at : at + 8, :].reshape(176, 128) for c in range(8)], axis=1
            )
            value = dot_n(rows, sel).reshape(22, NZ, C)
            before, after = neighbours(value)
            v3_ref[:, y * 8 : y * 8 + 8, 0:C] = before
            v3_ref[:, y * 8 : y * 8 + 8, C : 2 * C] = value.astype(BF)
            v3_ref[:, y * 8 : y * 8 + 8, 2 * C : 3 * C] = after

    def first(i, carry):
        x0 = i * 5
        for s in range(9):
            part = v3_ref[pl.ds(x0 + s // 3, 5), (s % 3) * 8 : (s % 3) * 8 + 96, :]
            part = dot_t(part.reshape(480, 3 * C), w1_ref[s])
            if s == 0:
                acc_ref[...] = part
            else:
                acc_ref[...] += part
        v = acc_ref[...]
        act = (v / (1.0 + jnp.exp(-v))).astype(BF)
        wide = act.astype(F32).reshape(60, NZ, C)
        before, after = neighbours(wide)
        a3_ref[pl.ds(x0, 5), :, 0:C] = before.reshape(5, 96, C)
        a3_ref[pl.ds(x0, 5), :, C : 2 * C] = act.reshape(5, 96, C)
        a3_ref[pl.ds(x0, 5), :, 2 * C : 3 * C] = after.reshape(5, 96, C)
        return carry

    lax.fori_loop(0, 4, first, 0)

    @pl.when(chan == 0)
    def _():
        a3_ref[0:2] = jnp.zeros((2, 96, 3 * C), BF)

    @pl.when(chan == 7)
    def _():
        a3_ref[18:20] = jnp.zeros((2, 96, 3 * C), BF)

    @pl.when(space == 0)
    def _():
        a3_ref[:, 0:16, :] = jnp.zeros((20, 16, 3 * C), BF)

    @pl.when(space == 15)
    def _():
        a3_ref[:, 80:96, :] = jnp.zeros((20, 16, 3 * C), BF)

    og_ref[1:17, 8:72, :] = grad_ref[...]
    og_ref[0:1, 8:72, :] = gxl_ref[...]
    og_ref[17:18, 8:72, :] = gxh_ref[...]
    og_ref[:, 0:8, :] = gyl_ref[...]
    og_ref[:, 72:80, :] = gyh_ref[...]

    def second(i, carry):
        x0 = i * 6
        for s in range(9):
            part = a3_ref[pl.ds(x0 + s // 3, 6), (s % 3) * 8 : (s % 3) * 8 + 80, :]
            part = dot_n(part.reshape(480, 3 * C), w2_ref[s])
            if s == 0:
                acc_ref[...] = part
            else:
                acc_ref[...] += part
        v = acc_ref[...]
        sig = 1.0 / (1.0 + jnp.exp(-v))
        og = og_ref[pl.ds(x0, 6)].reshape(480, C).astype(F32)
        delta = (og * sig * (1.0 + v * (1.0 - sig))).astype(BF)
        before, after = neighbours(delta.astype(F32).reshape(60, NZ, C))
        d3_ref[pl.ds(x0, 6), :, 0:C] = after.reshape(6, 80, C)
        d3_ref[pl.ds(x0, 6), :, C : 2 * C] = delta.reshape(6, 80, C)
        d3_ref[pl.ds(x0, 6), :, 2 * C : 3 * C] = before.reshape(6, 80, C)
        return carry

    lax.fori_loop(0, 3, second, 0)

    dt_ref[...] = d3_ref[1:17, 8:72, C : 2 * C].reshape(1024, C).T
    for s in range(9):
        part = a3_ref[1 + s // 3 : 17 + s // 3, (1 + s % 3) * 8 : (1 + s % 3) * 8 + 64, :]
        g = dot_n(dt_ref[...], part.reshape(1024, 3 * C)).astype(BF)
        for tz in range(3):
            t = 3 * s + tz
            tile = g[:, tz * C : (tz + 1) * C]
            for h in range(2):
                at = t * C + h * 128
                at += SLOT - HALF if at >= HALF else 0
                g_ref[at : at + 128, :] = tile[h * 128 : h * 128 + 128]
    zero = jnp.zeros((SLOT - HALF, C), BF)
    g_ref[HALF:SLOT, :] = zero
    g_ref[SLOT + HALF : 2 * SLOT, :] = zero
    keep_ref[...] = g_ref[pl.ds(pl.multiple_of(core * SLOT, 16), SLOT), :]
    send_ref[...] = g_ref[pl.ds(pl.multiple_of((1 - core) * SLOT, 16), SLOT), :]


def back_kernel(d3_ref, w2_ref, out_ref, acc_ref):
    def block(i, carry):
        x0 = i * 8
        for s in range(9):
            tx, ty = s // 3, s % 3
            part = d3_ref[pl.ds(x0 + 2 - tx, 8), (2 - ty) * 8 : (2 - ty) * 8 + 64, :]
            w = jnp.concatenate([w2_ref[s, k * C : (k + 1) * C, :] for k in range(3)], axis=1)
            part = dot_t(part.reshape(512, 3 * C), w)
            if s == 0:
                acc_ref[...] = part
            else:
                acc_ref[...] += part
        out_ref[pl.ds(x0, 8)] = acc_ref[...].astype(BF).reshape(8, 64, C)
        return carry

    lax.fori_loop(0, 2, block, 0)


def finish_kernel(place_ref, mine_ref, other_ref, out_ref, full_ref):
    core = place_ref[2]

    @pl.when(pl.program_id(0) == 0)
    def _():
        at = pl.multiple_of(core * HALF, 16)
        full_ref[pl.ds(at, HALF), :] = mine_ref[0:HALF, :]
        at = pl.multiple_of((1 - core) * HALF, 16)
        full_ref[pl.ds(at, HALF), :] = other_ref[0:HALF, :]

    row = lax.broadcasted_iota(jnp.int32, (C, C), 0)
    col = lax.broadcasted_iota(jnp.int32, (C, C), 1)
    unit = (row == col).astype(F32).astype(BF)
    at = pl.multiple_of(pl.program_id(0) * C, C)
    out_ref[0] = dot_t(unit, full_ref[pl.ds(at, C), :])


def border(count):
    up = [(i, i + 1) for i in range(count - 1)]
    return up, [(b, a) for a, b in up]


def local(volume, first_filters, second_filters, out_grad):
    chan, slab, core = (lax.axis_index(a) for a in ("chan", "slab", "core"))
    place = jnp.stack([chan, slab * 2 + core, core]).astype(jnp.int32)
    swap = [(0, 1), (1, 0)]
    up, down = border(16)
    xup, xdown = border(8)
    space = ("slab", "core")

    w1 = jnp.transpose(first_filters, (0, 1, 2, 4, 3)).reshape(27, 32, C)
    half = lax.dynamic_slice_in_dim(w1, core * 16, 16, axis=1)
    pieces = [half] + [
        lax.ppermute(half, "chan", [(i, (i + d) % 8) for i in range(8)]) for d in range(1, 8)
    ]

    og = out_grad.reshape(BX, BY * NZ, C)
    gxl = lax.ppermute(og[BX - 1 :], "chan", xup)
    gxh = lax.ppermute(og[:1], "chan", xdown)
    top = jnp.concatenate([gxl[:, 56:], og[:, 56:], gxh[:, 56:]], axis=0)
    bottom = jnp.concatenate([gxl[:, :8], og[:, :8], gxh[:, :8]], axis=0)
    gyl = lax.ppermute(top, space, up)
    gyh = lax.ppermute(bottom, space, down)

    pick = np.zeros((176, 128), np.float32)
    for c in range(8):
        for j in range(22):
            if 0 <= 16 * c - 3 + j < 128:
                pick[c * 22 + j, 16 * c - 3 + j] = 1.0
    packed = pl.pallas_call(
        pack_kernel,
        out_shape=jax.ShapeDtypeStruct((176 * 16, 128), BF),
        in_specs=[VMEM, VMEM],
        out_specs=VMEM,
        scratch_shapes=[pltpu.VMEM((176 * 16, 128), F32)],
        compiler_params=params(),
        cost_estimate=cost(16 * 176 * 128 * 256, 3 << 20),
        name="pack",
    )(jnp.asarray(pick, BF), jnp.transpose(volume, (1, 2, 3, 0)))
    near = lax.all_to_all(packed.reshape(8, 352, 128), "chan", 0, 0, tiled=True)
    near = near.reshape(8, 22, 16, 128)
    low = lax.ppermute(near[:, :, 8:], space, up)
    high = lax.ppermute(near[:, :, :8], space, down)

    mine = jnp.stack(pieces)
    other = lax.ppermute(mine, "core", swap)

    w2 = second_filters.reshape(9, 3 * C, C)
    keep, send, d3 = pl.pallas_call(
        layers_kernel,
        out_shape=(
            jax.ShapeDtypeStruct((SLOT, C), BF),
            jax.ShapeDtypeStruct((SLOT, C), BF),
            jax.ShapeDtypeStruct((18, 80, 3 * C), BF),
        ),
        in_specs=[SMEM] + [VMEM] * 11,
        out_specs=(VMEM, VMEM, VMEM),
        scratch_shapes=[
            pltpu.VMEM((22, 112, 3 * C), BF),
            pltpu.VMEM((20, 96, 3 * C), BF),
            pltpu.VMEM((9, C, 3 * C), BF),
            pltpu.VMEM((480, C), F32),
            pltpu.VMEM((18, 80, C), BF),
            pltpu.VMEM((C, 1024), BF),
            pltpu.VMEM((2 * SLOT, C), BF),
        ],
        compiler_params=params(),
        cost_estimate=cost(16e9, 20 << 20),
        name="layers",
    )(place, near, low, high, mine, other, w2, og, gxl, gxh, gyl, gyh)

    received = lax.ppermute(send, "core", swap)
    act_grad = pl.pallas_call(
        back_kernel,
        out_shape=jax.ShapeDtypeStruct((BX, BY * NZ, C), BF),
        in_specs=[VMEM, VMEM],
        out_specs=VMEM,
        scratch_shapes=[pltpu.VMEM((512, C), F32)],
        compiler_params=params(),
        cost_estimate=cost(3.6e9, 7 << 20),
        name="back",
    )(d3, w2)

    both = (keep.astype(F32) + received.astype(F32)).astype(BF).reshape(64, 56, C)
    shares = lax.all_to_all(both, CHIPS, 0, 0, tiled=True)
    scale = 1.0 / math.sqrt(128 * 128 * NZ)
    share = (jnp.sum(shares.astype(F32), axis=0) * scale).astype(BF)
    spread = lax.optimization_barrier(jnp.broadcast_to(share[None], (64, 56, C)))
    ours = lax.all_to_all(spread, CHIPS, 0, 0, tiled=True).reshape(SLOT, C)
    theirs = lax.ppermute(ours, "core", swap)
    whole = pl.BlockSpec((SLOT, C), lambda t: (0, 0))
    filter_grad = pl.pallas_call(
        finish_kernel,
        grid=(27,),
        out_shape=jax.ShapeDtypeStruct((27, C, C), F32),
        in_specs=[SMEM, whole, whole],
        out_specs=pl.BlockSpec((1, C, C), lambda t: (t, 0, 0)),
        scratch_shapes=[pltpu.VMEM((2 * HALF, C), BF)],
        compiler_params=params(),
        cost_estimate=cost(1e9, 11 << 20),
        name="finish",
    )(place, ours, theirs)
    return (
        act_grad.reshape(BX, BY, NZ, C),
        filter_grad.reshape(3, 3, 3, C, C),
    )


def solution(mesh):
    cells = Mesh(mesh.devices.reshape(8, 8, 2), ("chan", "slab", "core"))
    space = ("slab", "core")
    placed = (
        P(None, space, None, "chan"),
        P(None, None, None, None, "chan"),
        P(),
        P("chan", space, None, None),
    )
    return jax.shard_map(
        local,
        mesh=cells,
        in_specs=placed,
        out_specs=(P("chan", space, None, None), P()),
        check_vma=False,
    )
```

profile of v0, /device:TPU:1, one launch (start us, length us, event | category | flops | bytes accessed | tf_op | source)
XLA Modules:
  0.0 201.5 jit_solution(11616928952212595146)
XLA Ops:
  0.6 1.0 bitcast_dynamic-update-slice_fusion.7
  1.6 4.5 %collective-permute-start.2 = (bf16[27,16,256]{2,1,0:T(8,128)(2,1)S(1)}, bf16[27,16,256]{2,1,0:T(8,128)(2,1)S(1)}, u32[]{:S(2)}, u32[]{:S(2)}) collective-permute-start(bf16[27,16,256]{2,1,0:T(8,128)(2,1)S(1)} %get-tuple-element.9), channel_id=1, source_target_pairs={{0,16},{16,32},{32,48},{48,64},{64,80},{80,96},{96,112},{112,0},{1... | collective-permute-start | bytes 663560 | tf_op jit(solution)/shard_map/ppermute | solution.py:226
  6.1 2.5 %collective-permute-start.7 = (bf16[27,16,256]{2,1,0:T(8,128)(2,1)S(1)}, bf16[27,16,256]{2,1,0:T(8,128)(2,1)S(1)}, u32[]{:S(2)}, u32[]{:S(2)}) collective-permute-start(bf16[27,16,256]{2,1,0:T(8,128)(2,1)S(1)} %get-tuple-element.9), channel_id=1, source_target_pairs={{0,96},{16,112},{32,0},{48,16},{64,32},{80,48},{96,64},{112,80},{1... | collective-permute-start | bytes 663560 | tf_op jit(solution)/shard_map/ppermute | solution.py:226
  8.6 0.5 collective-permute-start.6
  9.1 2.2 %collective-permute-start.5 = (bf16[27,16,256]{2,1,0:T(8,128)(2,1)S(1)}, bf16[27,16,256]{2,1,0:T(8,128)(2,1)S(1)}, u32[]{:S(2)}, u32[]{:S(2)}) collective-permute-start(bf16[27,16,256]{2,1,0:T(8,128)(2,1)S(1)} %get-tuple-element.9), channel_id=1, source_target_pairs={{0,64},{16,80},{32,96},{48,112},{64,0},{80,16},{96,32},{112,48},{1... | collective-permute-start | bytes 663560 | tf_op jit(solution)/shard_map/ppermute | solution.py:226
  11.4 1.1 collective-permute-start.4
  12.5 1.0 collective-permute-done.2
  13.5 0.7 collective-permute-start.3
  14.2 17.2 %collective-permute-done.3 = bf16[27,16,256]{2,1,0:T(8,128)(2,1)S(1)} collective-permute-done((bf16[27,16,256]{2,1,0:T(8,128)(2,1)S(1)}, bf16[27,16,256]{2,1,0:T(8,128)(2,1)S(1)}, u32[]{:S(2)}, u32[]{:S(2)}) %collective-permute-start.3) | collective-permute-done | bytes 221216 | tf_op jit(solution)/shard_map/ppermute | solution.py:226
  31.5 0.0 collective-permute-start.8
  31.5 0.0 collective-permute-done.4
  31.5 0.0 collective-permute-done.5
  31.6 0.0 collective-permute-done.6
  31.6 0.0 collective-permute-done.7
  31.6 7.8 %collective-permute-done.8 = bf16[27,16,256]{2,1,0:T(8,128)(2,1)S(1)} collective-permute-done((bf16[27,16,256]{2,1,0:T(8,128)(2,1)S(1)}, bf16[27,16,256]{2,1,0:T(8,128)(2,1)S(1)}, u32[]{:S(2)}, u32[]{:S(2)}) %collective-permute-start.8) | collective-permute-done | bytes 221216 | tf_op jit(solution)/shard_map/ppermute | solution.py:226
  39.5 0.0 copy-start.3
  39.5 1.4 collective-permute-start.9
  40.9 2.7 %pack.1 = bf16[2816,128]{1,0:T(8,128)(2,1)} custom-call(bf16[176,128]{1,0:T(8,128)(2,1)} %constant.26.clone.pick_ref, bf16[8,8,32,128]{3,2,1,0:T(8,128)(2,1)} %bitcast.42), custom_call_target="tpu_custom_call" | custom-call | flops 92274688 | bytes 3145728 | tf_op jit(solution)/shard_map/pack/pallas_call | solution.py:242
  43.6 3.5 %all-to-all-start = ((bf16[8,352,128]{2,1,0:T(8,128)(2,1)}), bf16[8,352,128]{2,1,0:T(8,128)(2,1)S(1)}, u32[]{:S(2)}, u32[]{:S(2)}) async-start(bf16[8,352,128]{2,1,0:T(8,128)(2,1)} %bitcast.41), calls=%async_computation | async-start | bytes 1441792 | tf_op jit(solution)/shard_map/all_to_all | solution.py:252
  47.1 0.8 slice_bitcast_fusion
  47.9 1.3 collective-permute-start.11
  49.2 5.5 %collective-permute-start.10 = (bf16[1,64,256]{2,1,0:T(8,128)(2,1)S(1)}, bf16[1,64,256]{2,1,0:T(8,128)(2,1)S(1)}, u32[]{:S(2)}, u32[]{:S(2)}) collective-permute-start(bf16[1,64,256]{2,1,0:T(8,128)(2,1)S(1)} %get-tuple-element.15), channel_id=1, source_target_pairs={{0,16},{16,32},{32,48},{48,64},{64,80},{80,96},{96,112},{1,17},{17... | collective-permute-start | bytes 98312 | tf_op jit(solution)/shard_map/ppermute | solution.py:230
  54.7 0.9 fusion.1
  55.6 4.8 %collective-permute-done.11.gxh_ref = bf16[1,64,256]{2,1,0:T(8,128)(2,1)S(1)} collective-permute-done((bf16[1,64,256]{2,1,0:T(8,128)(2,1)S(1)}, bf16[1,64,256]{2,1,0:T(8,128)(2,1)S(1)}, u32[]{:S(2)}, u32[]{:S(2)}) %collective-permute-start.11) | collective-permute-done | bytes 32800 | tf_op jit(solution)/shard_map/ppermute | solution.py:231
  60.4 0.0 copy-start.4
  60.4 0.0 all-to-all-done
  60.4 0.0 copy-start.1
  60.4 0.1 fusion
  60.5 0.0 copy-done.3
  60.5 2.4 %collective-permute-start.1 = (bf16[8,22,8,128]{3,2,1,0:T(8,128)(2,1)S(1)}, bf16[8,22,8,128]{3,2,1,0:T(8,128)(2,1)S(1)}, u32[]{:S(2)}, u32[]{:S(2)}) collective-permute-start(bf16[8,22,8,128]{3,2,1,0:T(8,128)(2,1)S(1)} %get-tuple-element.10), channel_id=1, source_target_pairs={{1,0},{2,1},{3,2},{4,3},{5,4},{6,5},{7,6},{8,7},{9,8},{10,9},{11,1... | collective-permute-start | bytes 1081352 | tf_op jit(solution)/shard_map/ppermute | solution.py:255
  62.9 3.2 %collective-permute-start = (bf16[8,22,8,128]{3,2,1,0:T(8,128)(2,1)S(1)}, bf16[8,22,8,128]{3,2,1,0:T(8,128)(2,1)S(1)}, u32[]{:S(2)}, u32[]{:S(2)}) collective-permute-start(bf16[8,22,8,128]{3,2,1,0:T(8,128)(2,1)S(1)} %get-tuple-element.11), channel_id=1, source_target_pairs={{0,1},{1,2},{2,3},{3,4},{4,5},{5,6},{6,7},{7,8},{8,9},{9,10},{10,1... | collective-permute-start | bytes 1081352 | tf_op jit(solution)/shard_map/ppermute | solution.py:254
  66.1 0.0 collective-permute-done.10.gxl_ref
  66.1 0.0 copy-start.5
  66.2 2.3 %collective-permute-start.12 = (bf16[18,8,256]{2,1,0:T(8,128)(2,1)S(1)}, bf16[18,8,256]{2,1,0:T(8,128)(2,1)S(1)}, u32[]{:S(2)}, u32[]{:S(2)}) collective-permute-start(bf16[18,8,256]{2,1,0:T(8,128)(2,1)S(1)} %pad_maximum_fusion), channel_id=1, source_target_pairs={{0,1},{1,2},{2,3},{3,4},{4,5},{5,6},{6,7},{7,8},{8,9},{9,10},{10,1... | collective-permute-start | bytes 221192 | tf_op jit(solution)/shard_map/ppermute | solution.py:234
  68.5 2.0 collective-permute-start.13
  70.5 0.6 pad_add_fusion.place_ref
  71.1 0.1 collective-permute-done.12.gyl_ref
  71.2 0.0 copy-start.8
  71.2 3.0 %collective-permute-done.13.gyh_ref = bf16[18,8,256]{2,1,0:T(8,128)(2,1)S(1)} collective-permute-done((bf16[18,8,256]{2,1,0:T(8,128)(2,1)S(1)}, bf16[18,8,256]{2,1,0:T(8,128)(2,1)S(1)}, u32[]{:S(2)}, u32[]{:S(2)}) %collective-permute-start.13) | collective-permute-done | bytes 73760 | tf_op jit(solution)/shard_map/ppermute | solution.py:235
  74.2 0.0 collective-permute-done.1.high_ref
  74.2 0.0 collective-permute-done.low_ref
  74.2 0.0 copy-start.7
  74.2 0.0 collective-permute-done.9.other_ref
  74.2 0.0 copy-done.4
  74.3 0.0 copy-done.1
  74.3 0.0 copy-done.5
  74.3 0.0 copy-done.8
  74.3 0.6 copy-done.9
  74.8 0.2 copy-done.6
  75.0 0.0 copy-done.7
  75.1 26.8 %layers.1 = (bf16[3584,256]{1,0:T(8,128)(2,1)}, bf16[3584,256]{1,0:T(8,128)(2,1)}, bf16[18,80,768]{2,1,0:T(8,128)(2,1)}) custom-call(s32[3]{0:T(128)} %pad_add_fusion.place_ref, bf16[8,22,16,128]{3,2,1,0:T(8,128)(2,1)} %bitcast.40, bf16[8,22,8,128]{3,2,1,0:T(8,128)(2,1)} %copy-done.7, bf16[8,22,8,128]{3,2,1,0:T(8,128)(2,1)} %copy-done.6, ...), custom_call_target="tpu_custom_call" | custom-call | flops 16000000000 | bytes 20971520 | tf_op jit(solution)/shard_map/layers/pallas_call | solution.py:261
  101.8 0.0 collective-permute-start.14
  101.8 4.0 %collective-permute-done.14 = bf16[3584,256]{1,0:T(8,128)(2,1)S(1)} collective-permute-done((bf16[3584,256]{1,0:T(8,128)(2,1)}, bf16[3584,256]{1,0:T(8,128)(2,1)S(1)}, u32[]{:S(2)}, u32[]{:S(2)}) %collective-permute-start.14) | collective-permute-done | bytes 1835040 | tf_op jit(solution)/shard_map/ppermute | solution.py:284
  105.8 2.0 %add_convert_fusion = bf16[3584,256]{1,0:T(8,128)(2,1)S(1)} fusion(bf16[3584,256]{1,0:T(8,128)(2,1)S(1)} %collective-permute-done.14, bf16[3584,256]{1,0:T(8,128)(2,1)} %get-tuple-element.6), kind=kLoop, calls=%fused_computation.1 | loop fusion | flops 3670016 | bytes 5505024 | tf_op jit(solution)/shard_map/convert_element_type | solution.py:296
  107.9 35.2 %all_to_all.15 = bf16[64,56,256]{2,1,0:T(8,128)(2,1)S(1)} all-to-all(bf16[64,56,256]{2,1,0:T(8,128)(2,1)S(1)} %bitcast.37), channel_id=1, replica_groups=mesh['chan'=8,'slab'=8,'core'=2] {'chan','slab'}, dimensions={0} | all-to-all | bytes 3670016 | tf_op jit(solution)/shard_map/all_to_all | solution.py:297
  143.1 0.3 convert_reduce_fusion
  143.3 0.1 broadcast_in_dim.2
  143.5 30.0 %all_to_all.16 = bf16[64,56,256]{2,1,0:T(8,128)(2,1)S(1)} all-to-all(bf16[64,56,256]{2,1,0:T(8,128)(2,1)S(1)} %broadcast_in_dim.2), channel_id=1, replica_groups=mesh['chan'=8,'slab'=8,'core'=2] {'chan','slab'}, dimensions={0} | all-to-all | bytes 3670016 | tf_op jit(solution)/shard_map/all_to_all | solution.py:301
  173.5 3.9 %collective-permute-start.15 = (bf16[3584,256]{1,0:T(8,128)(2,1)S(1)}, bf16[3584,256]{1,0:T(8,128)(2,1)S(1)}, u32[]{:S(2)}, u32[]{:S(2)}) collective-permute-start(bf16[3584,256]{1,0:T(8,128)(2,1)S(1)} %bitcast.35), channel_id=1, source_target_pairs={{0,1},{1,0},{2,3},{3,2},{4,5},{5,4},{6,7},{7,6},{8,9},{9,8},{10,11... | collective-permute-start | bytes 5505032 | tf_op jit(solution)/shard_map/ppermute | solution.py:302
  177.4 7.5 %back.1 = bf16[16,64,256]{2,1,0:T(8,128)(2,1)} custom-call(bf16[18,80,768]{2,1,0:T(8,128)(2,1)} %get-tuple-element.5.d3_ref, bf16[9,768,256]{2,1,0:T(8,128)(2,1)} %bitcast.47), custom_call_target="tpu_custom_call" | custom-call | flops 3600000000 | bytes 7340032 | tf_op jit(solution)/shard_map/back/pallas_call | solution.py:285
  184.9 0.0 copy-done
  184.9 0.0 collective-permute-done.15.other_ref
  184.9 1.2 copy-done.2
  186.1 15.4 %finish.1 = f32[27,256,256]{2,1,0:T(8,128)} custom-call(s32[3]{0:T(128)} %pad_add_fusion.place_ref, bf16[3584,256]{1,0:T(8,128)(2,1)} %bitcast.36, bf16[3584,256]{1,0:T(8,128)(2,1)} %copy-done.2), custom_call_target="tpu_custom_call" | custom-call | flops 1000000000 | bytes 11534336 | tf_op jit(solution)/shard_map/finish/pallas_call | solution.py:304
  (16 shorter events, 0.2 us)
Async XLA Ops:
  1.6 11.8 %collective-permute-start.2 = (bf16[27,16,256]{2,1,0:T(8,128)(2,1)S(1)}, bf16[27,16,256]{2,1,0:T(8,128)(2,1)S(1)}, u32[]{:S(2)}, u32[]{:S(2)}) collective-permute-start(bf16[27,16,256]{2,1,0:T(8,128)(2,1)S(1)} %get-tuple-element.9), channel_id=1, source_target_pairs={{0,16},{16,32},{32,48},{48,64},{64,80},{80,96},{96,112},{112,0},{1... | collective-permute-start | bytes 663560 | tf_op jit(solution)/shard_map/ppermute | solution.py:226
  6.1 25.5 %collective-permute-start.7 = (bf16[27,16,256]{2,1,0:T(8,128)(2,1)S(1)}, bf16[27,16,256]{2,1,0:T(8,128)(2,1)S(1)}, u32[]{:S(2)}, u32[]{:S(2)}) collective-permute-start(bf16[27,16,256]{2,1,0:T(8,128)(2,1)S(1)} %get-tuple-element.9), channel_id=1, source_target_pairs={{0,96},{16,112},{32,0},{48,16},{64,32},{80,48},{96,64},{112,80},{1... | collective-permute-start | bytes 663560 | tf_op jit(solution)/shard_map/ppermute | solution.py:226
  8.6 23.0 %collective-permute-start.6 = (bf16[27,16,256]{2,1,0:T(8,128)(2,1)S(1)}, bf16[27,16,256]{2,1,0:T(8,128)(2,1)S(1)}, u32[]{:S(2)}, u32[]{:S(2)}) collective-permute-start(bf16[27,16,256]{2,1,0:T(8,128)(2,1)S(1)} %get-tuple-element.9), channel_id=1, source_target_pairs={{0,80},{16,96},{32,112},{48,0},{64,16},{80,32},{96,48},{112,64},{1... | collective-permute-start | bytes 663560 | tf_op jit(solution)/shard_map/ppermute | solution.py:226
  9.1 22.4 %collective-permute-start.5 = (bf16[27,16,256]{2,1,0:T(8,128)(2,1)S(1)}, bf16[27,16,256]{2,1,0:T(8,128)(2,1)S(1)}, u32[]{:S(2)}, u32[]{:S(2)}) collective-permute-start(bf16[27,16,256]{2,1,0:T(8,128)(2,1)S(1)} %get-tuple-element.9), channel_id=1, source_target_pairs={{0,64},{16,80},{32,96},{48,112},{64,0},{80,16},{96,32},{112,48},{1... | collective-permute-start | bytes 663560 | tf_op jit(solution)/shard_map/ppermute | solution.py:226
  11.4 20.1 %collective-permute-start.4 = (bf16[27,16,256]{2,1,0:T(8,128)(2,1)S(1)}, bf16[27,16,256]{2,1,0:T(8,128)(2,1)S(1)}, u32[]{:S(2)}, u32[]{:S(2)}) collective-permute-start(bf16[27,16,256]{2,1,0:T(8,128)(2,1)S(1)} %get-tuple-element.9), channel_id=1, source_target_pairs={{0,48},{16,64},{32,80},{48,96},{64,112},{80,0},{96,16},{112,32},{1... | collective-permute-start | bytes 663560 | tf_op jit(solution)/shard_map/ppermute | solution.py:226
  13.5 18.0 %collective-permute-start.3 = (bf16[27,16,256]{2,1,0:T(8,128)(2,1)S(1)}, bf16[27,16,256]{2,1,0:T(8,128)(2,1)S(1)}, u32[]{:S(2)}, u32[]{:S(2)}) collective-permute-start(bf16[27,16,256]{2,1,0:T(8,128)(2,1)S(1)} %get-tuple-element.9), channel_id=1, source_target_pairs={{0,32},{16,48},{32,64},{48,80},{64,96},{80,112},{96,0},{112,16},{1... | collective-permute-start | bytes 663560 | tf_op jit(solution)/shard_map/ppermute | solution.py:226
  31.5 8.0 %collective-permute-start.8 = (bf16[27,16,256]{2,1,0:T(8,128)(2,1)S(1)}, bf16[27,16,256]{2,1,0:T(8,128)(2,1)S(1)}, u32[]{:S(2)}, u32[]{:S(2)}) collective-permute-start(bf16[27,16,256]{2,1,0:T(8,128)(2,1)S(1)} %get-tuple-element.9), channel_id=1, source_target_pairs={{0,112},{16,0},{32,16},{48,32},{64,48},{80,64},{96,80},{112,96},{1... | collective-permute-start | bytes 663560 | tf_op jit(solution)/shard_map/ppermute | solution.py:226
  39.5 21.0 %copy-start.3 = (bf16[8,27,16,256]{3,2,1,0:T(8,128)(2,1)}, bf16[8,27,16,256]{3,2,1,0:T(8,128)(2,1)S(1)}, u32[]{:S(2)}) copy-start(bf16[8,27,16,256]{3,2,1,0:T(8,128)(2,1)S(1)} %bitcast_dynamic-update-slice_fusion.mine_ref) | copy-start | bytes 5308420
  39.5 34.7 %collective-permute-start.9 = (bf16[8,27,16,256]{3,2,1,0:T(8,128)(2,1)S(1)}, bf16[8,27,16,256]{3,2,1,0:T(8,128)(2,1)}, u32[]{:S(2)}, u32[]{:S(2)}) collective-permute-start(bf16[8,27,16,256]{3,2,1,0:T(8,128)(2,1)S(1)} %bitcast_dynamic-update-slice_fusion.mine_ref), channel_id=1, source_target_pairs={{0,1},{1,0},{2,3},{3,2},{4,5},{5,4},{6,7},{7,6},{8,9},{9,8},{10,11... | collective-permute-start | bytes 5308424 | tf_op jit(solution)/shard_map/ppermute | solution.py:258
  43.6 16.8 %all-to-all-start = ((bf16[8,352,128]{2,1,0:T(8,128)(2,1)}), bf16[8,352,128]{2,1,0:T(8,128)(2,1)S(1)}, u32[]{:S(2)}, u32[]{:S(2)}) async-start(bf16[8,352,128]{2,1,0:T(8,128)(2,1)} %bitcast.41), calls=%async_computation | async-start | bytes 1441792 | tf_op jit(solution)/shard_map/all_to_all | solution.py:252
  47.9 12.5 %collective-permute-start.11 = (bf16[1,64,256]{2,1,0:T(8,128)(2,1)S(1)}, bf16[1,64,256]{2,1,0:T(8,128)(2,1)S(1)}, u32[]{:S(2)}, u32[]{:S(2)}) collective-permute-start(bf16[1,64,256]{2,1,0:T(8,128)(2,1)S(1)} %get-tuple-element.14), channel_id=1, source_target_pairs={{16,0},{32,16},{48,32},{64,48},{80,64},{96,80},{112,96},{17,1},{33... | collective-permute-start | bytes 98312 | tf_op jit(solution)/shard_map/ppermute | solution.py:231
  49.2 16.9 %collective-permute-start.10 = (bf16[1,64,256]{2,1,0:T(8,128)(2,1)S(1)}, bf16[1,64,256]{2,1,0:T(8,128)(2,1)S(1)}, u32[]{:S(2)}, u32[]{:S(2)}) collective-permute-start(bf16[1,64,256]{2,1,0:T(8,128)(2,1)S(1)} %get-tuple-element.15), channel_id=1, source_target_pairs={{0,16},{16,32},{32,48},{48,64},{64,80},{80,96},{96,112},{1,17},{17... | collective-permute-start | bytes 98312 | tf_op jit(solution)/shard_map/ppermute | solution.py:230
  60.4 13.9 %copy-start.4 = (bf16[1,64,256]{2,1,0:T(8,128)(2,1)}, bf16[1,64,256]{2,1,0:T(8,128)(2,1)S(1)}, u32[]{:S(2)}) copy-start(bf16[1,64,256]{2,1,0:T(8,128)(2,1)S(1)} %collective-permute-done.11.gxh_ref) | copy-start | bytes 98308
  60.4 13.9 %copy-start.1 = (bf16[8,352,128]{2,1,0:T(8,128)(2,1)}, bf16[8,352,128]{2,1,0:T(8,128)(2,1)S(1)}, u32[]{:S(2)}) copy-start(bf16[8,352,128]{2,1,0:T(8,128)(2,1)S(1)} %all-to-all-done) | copy-start | bytes 2162692
  60.5 13.7 %collective-permute-start.1 = (bf16[8,22,8,128]{3,2,1,0:T(8,128)(2,1)S(1)}, bf16[8,22,8,128]{3,2,1,0:T(8,128)(2,1)S(1)}, u32[]{:S(2)}, u32[]{:S(2)}) collective-permute-start(bf16[8,22,8,128]{3,2,1,0:T(8,128)(2,1)S(1)} %get-tuple-element.10), channel_id=1, source_target_pairs={{1,0},{2,1},{3,2},{4,3},{5,4},{6,5},{7,6},{8,7},{9,8},{10,9},{11,1... | collective-permute-start | bytes 1081352 | tf_op jit(solution)/shard_map/ppermute | solution.py:255
  62.9 11.3 %collective-permute-start = (bf16[8,22,8,128]{3,2,1,0:T(8,128)(2,1)S(1)}, bf16[8,22,8,128]{3,2,1,0:T(8,128)(2,1)S(1)}, u32[]{:S(2)}, u32[]{:S(2)}) collective-permute-start(bf16[8,22,8,128]{3,2,1,0:T(8,128)(2,1)S(1)} %get-tuple-element.11), channel_id=1, source_target_pairs={{0,1},{1,2},{2,3},{3,4},{4,5},{5,6},{6,7},{7,8},{8,9},{9,10},{10,1... | collective-permute-start | bytes 1081352 | tf_op jit(solution)/shard_map/ppermute | solution.py:254
  66.1 8.1 %copy-start.5 = (bf16[1,64,256]{2,1,0:T(8,128)(2,1)}, bf16[1,64,256]{2,1,0:T(8,128)(2,1)S(1)}, u32[]{:S(2)}) copy-start(bf16[1,64,256]{2,1,0:T(8,128)(2,1)S(1)} %collective-permute-done.10.gxl_ref) | copy-start | bytes 98308
  66.2 5.1 %collective-permute-start.12 = (bf16[18,8,256]{2,1,0:T(8,128)(2,1)S(1)}, bf16[18,8,256]{2,1,0:T(8,128)(2,1)S(1)}, u32[]{:S(2)}, u32[]{:S(2)}) collective-permute-start(bf16[18,8,256]{2,1,0:T(8,128)(2,1)S(1)} %pad_maximum_fusion), channel_id=1, source_target_pairs={{0,1},{1,2},{2,3},{3,4},{4,5},{5,6},{6,7},{7,8},{8,9},{9,10},{10,1... | collective-permute-start | bytes 221192 | tf_op jit(solution)/shard_map/ppermute | solution.py:234
  68.5 5.7 %collective-permute-start.13 = (bf16[18,8,256]{2,1,0:T(8,128)(2,1)S(1)}, bf16[18,8,256]{2,1,0:T(8,128)(2,1)S(1)}, u32[]{:S(2)}, u32[]{:S(2)}) collective-permute-start(bf16[18,8,256]{2,1,0:T(8,128)(2,1)S(1)} %pad_maximum_fusion.1), channel_id=1, source_target_pairs={{1,0},{2,1},{3,2},{4,3},{5,4},{6,5},{7,6},{8,7},{9,8},{10,9},{11,1... | collective-permute-start | bytes 221192 | tf_op jit(solution)/shard_map/ppermute | solution.py:235
  71.2 3.0 %copy-start.8 = (bf16[18,8,256]{2,1,0:T(8,128)(2,1)}, bf16[18,8,256]{2,1,0:T(8,128)(2,1)S(1)}, u32[]{:S(2)}) copy-start(bf16[18,8,256]{2,1,0:T(8,128)(2,1)S(1)} %collective-permute-done.12.gyl_ref) | copy-start | bytes 221188
  74.2 0.6 copy-start.9
  74.2 0.8 copy-start.6
  74.2 0.9 copy-start.7
  101.8 4.0 %collective-permute-start.14 = (bf16[3584,256]{1,0:T(8,128)(2,1)}, bf16[3584,256]{1,0:T(8,128)(2,1)S(1)}, u32[]{:S(2)}, u32[]{:S(2)}) collective-permute-start(bf16[3584,256]{1,0:T(8,128)(2,1)} %get-tuple-element.7), channel_id=1, source_target_pairs={{0,1},{1,0},{2,3},{3,2},{4,5},{5,4},{6,7},{7,6},{8,9},{9,8},{10,11... | collective-permute-start | bytes 5505032 | tf_op jit(solution)/shard_map/ppermute | solution.py:284
  173.5 11.4 %copy-start = (bf16[64,56,256]{2,1,0:T(8,128)(2,1)}, bf16[64,56,256]{2,1,0:T(8,128)(2,1)S(1)}, u32[]{:S(2)}) copy-start(bf16[64,56,256]{2,1,0:T(8,128)(2,1)S(1)} %all_to_all.16) | copy-start | bytes 5505028
  173.5 11.4 %collective-permute-start.15 = (bf16[3584,256]{1,0:T(8,128)(2,1)S(1)}, bf16[3584,256]{1,0:T(8,128)(2,1)S(1)}, u32[]{:S(2)}, u32[]{:S(2)}) collective-permute-start(bf16[3584,256]{1,0:T(8,128)(2,1)S(1)} %bitcast.35), channel_id=1, source_target_pairs={{0,1},{1,0},{2,3},{3,2},{4,5},{5,4},{6,7},{7,6},{8,9},{9,8},{10,11... | collective-permute-start | bytes 5505032 | tf_op jit(solution)/shard_map/ppermute | solution.py:302
  184.9 1.2 copy-start.2
where the time goes:
time: 202 us
  blocking collectives  65.2 us (32%)
  Pallas kernels  52.3 us (26%)
  waiting for transfers between devices  38 us (19%)
  starting transfers between devices  37.1 us (18%)
  local copies, waits for them, and re-layouts  5.06 us (3%)
  other arithmetic  2.93 us (1%)
    all_to_all x1, blocking collectives, local(): shares = lax.all_to_all(both, CHIPS, 0, 0, tiled=True)  35.2 us
    all_to_all x1, blocking collectives, local(): ours = lax.all_to_all(spread, CHIPS, 0, 0, tiled=True).reshape(SLOT, C)  30 us
    pallas_call x1, Pallas kernels, local(): pl.pallas_call(layers_kernel, out_shape=(jax.ShapeDtypeStruct((SLOT, C),...  26.8 us
    ppermute x7, waiting for transfers between devices, local(): lax.ppermute(half, 'chan', [(i, (i + d) % 8) for i in range(8)])  26.1 us
    pallas_call x1, Pallas kernels, local(): pl.pallas_call(finish_kernel, grid=(27,), out_shape=jax.ShapeDtypeStruct(...  15.4 us
    ppermute x7, starting transfers between devices, local(): lax.ppermute(half, 'chan', [(i, (i + d) % 8) for i in range(8)])  11.6 us
    pallas_call x1, Pallas kernels, local(): pl.pallas_call(back_kernel, out_shape=jax.ShapeDtypeStruct((BX, BY * NZ,...  7.5 us
    ppermute x1, starting transfers between devices, local(): gxl = lax.ppermute(og[BX - 1:], 'chan', xup)  5.49 us
  transfers between devices with their start and end apart: 17, of which 7 were waited for; matrix products, arithmetic and copies ran while one was open for 1% of the time, Pallas kernels for 5%

commit v1 on v0

--- a/solution.py
+++ b/solution.py
@@ -21,8 +21,8 @@
 SMEM = pl.BlockSpec(memory_space=pltpu.SMEM)
 
 
-def params(limit=60 << 20):
-    return pltpu.CompilerParams(vmem_limit_bytes=limit)
+def params(mib):
+    return pltpu.CompilerParams(vmem_limit_bytes=mib << 20)
 
 
 def cost(flops, moved):
@@ -53,26 +53,10 @@
     return before.astype(BF), after.astype(BF)
 
 
-def layers_kernel(
-    place_ref, near_ref, low_ref, high_ref, mine_ref, other_ref, w2_ref,
-    grad_ref, gxl_ref, gxh_ref, gyl_ref, gyh_ref,
-    keep_ref, send_ref, d3_ref,
-    v3_ref, a3_ref, w1_ref, acc_ref, og_ref, dt_ref, g_ref,
-):
-    chan, space, core = place_ref[0], place_ref[1], place_ref[2]
-
-    def place_filters(d, carry):
-        owner = lax.rem(chan - d + 8, 8)
-        for stack, half in ((mine_ref, core), (other_ref, 1 - core)):
-            at = pl.multiple_of(owner * 32 + half * 16, 16)
-            for t in range(27):
-                w1_ref[t // 3, pl.ds(at, 16), (t % 3) * C : (t % 3 + 1) * C] = stack[d, t]
-        return carry
-
-    lax.fori_loop(0, 8, place_filters, 0)
-
+def unpack_kernel(place_ref, near_ref, low_ref, high_ref, v3_ref):
+    core = place_ref[2]
     row = lax.broadcasted_iota(jnp.int32, (1024, C), 0)
-    col = lax.broadcasted_iota(jnp.int32, (1024, C), 1)
+    col = lax.broadcasted_iota(jnp.int32, (1024, C), 1) ^ (core * 128)
     same = ((row >> 7) == (col >> 5)) & ((row & 31) == (col & 31))
     for j in range(4):
         sel = (same & (((row >> 5) & 3) == j)).astype(F32).astype(BF)
@@ -91,11 +75,31 @@
             v3_ref[:, y * 8 : y * 8 + 8, C : 2 * C] = value.astype(BF)
             v3_ref[:, y * 8 : y * 8 + 8, 2 * C : 3 * C] = after
 
+
+def turn_kernel(pieces_ref, out_ref):
+    def turn(s, carry):
+        for k in range(3):
+            rows = jnp.concatenate([pieces_ref[c, 3 * s + k] for c in range(8)], axis=0)
+            out_ref[3 * s + k] = rows.T
+        return carry
+
+    lax.fori_loop(0, 9, turn, 0)
+
+
+def layers_kernel(
+    place_ref, v3_ref, mine_ref, other_ref, w2_ref,
+    grad_ref, gxl_ref, gxh_ref, gyl_ref, gyh_ref,
+    keep_ref, send_ref, d3_ref,
+    a3_ref, acc_ref, og_ref, dt_ref, g_ref,
+):
+    chan, space, core = place_ref[0], place_ref[1], place_ref[2]
+
     def first(i, carry):
         x0 = i * 5
         for s in range(9):
             part = v3_ref[pl.ds(x0 + s // 3, 5), (s % 3) * 8 : (s % 3) * 8 + 96, :]
-            part = dot_t(part.reshape(480, 3 * C), w1_ref[s])
+            w = [h[3 * s + k] for k in range(3) for h in (mine_ref, other_ref)]
+            part = dot_n(part.reshape(480, 3 * C), jnp.concatenate(w, axis=0))
             if s == 0:
                 acc_ref[...] = part
             else:
@@ -172,22 +176,26 @@
     send_ref[...] = g_ref[pl.ds(pl.multiple_of((1 - core) * SLOT, 16), SLOT), :]
 
 
+def flip_kernel(w_ref, out_ref):
+    def turn(s, carry):
+        for k in range(3):
+            out_ref[s, k * C : (k + 1) * C, :] = w_ref[s, k * C : (k + 1) * C, :].T
+        return carry
+
+    lax.fori_loop(0, 9, turn, 0)
+
+
 def back_kernel(d3_ref, w2_ref, out_ref, acc_ref):
-    def block(i, carry):
-        x0 = i * 8
-        for s in range(9):
-            tx, ty = s // 3, s % 3
-            part = d3_ref[pl.ds(x0 + 2 - tx, 8), (2 - ty) * 8 : (2 - ty) * 8 + 64, :]
-            w = jnp.concatenate([w2_ref[s, k * C : (k + 1) * C, :] for k in range(3)], axis=1)
-            part = dot_t(part.reshape(512, 3 * C), w)
-            if s == 0:
-                acc_ref[...] = part
-            else:
-                acc_ref[...] += part
-        out_ref[pl.ds(x0, 8)] = acc_ref[...].astype(BF).reshape(8, 64, C)
-        return carry
-
-    lax.fori_loop(0, 2, block, 0)
+    for s in range(9):
+        tx, ty = s // 3, s % 3
+        part = d3_ref[2 - tx : 18 - tx, (2 - ty) * 8 : (2 - ty) * 8 + 64, :]
+        part = dot_n(part.reshape(1024, 3 * C), w2_ref[s])
+        if s == 0:
+            acc_ref[...] = part
+        elif s < 8:
+            acc_ref[...] += part
+        else:
+            out_ref[...] = (acc_ref[...] + part).astype(BF).reshape(BX, 64, C)
 
 
 def finish_kernel(place_ref, mine_ref, other_ref, out_ref, full_ref):
@@ -203,8 +211,9 @@
     row = lax.broadcasted_iota(jnp.int32, (C, C), 0)
     col = lax.broadcasted_iota(jnp.int32, (C, C), 1)
     unit = (row == col).astype(F32).astype(BF)
-    at = pl.multiple_of(pl.program_id(0) * C, C)
-    out_ref[0] = dot_t(unit, full_ref[pl.ds(at, C), :])
+    for k in range(3):
+        at = pl.multiple_of(pl.program_id(0) * 3 * C + k * C, C)
+        out_ref[k] = dot_t(unit, full_ref[pl.ds(at, C), :])
 
 
 def border(count):
@@ -220,41 +229,60 @@
     xup, xdown = border(8)
     space = ("slab", "core")
 
-    w1 = jnp.transpose(first_filters, (0, 1, 2, 4, 3)).reshape(27, 32, C)
-    half = lax.dynamic_slice_in_dim(w1, core * 16, 16, axis=1)
-    pieces = [half] + [
-        lax.ppermute(half, "chan", [(i, (i + d) % 8) for i in range(8)]) for d in range(1, 8)
-    ]
-
-    og = out_grad.reshape(BX, BY * NZ, C)
-    gxl = lax.ppermute(og[BX - 1 :], "chan", xup)
-    gxh = lax.ppermute(og[:1], "chan", xdown)
-    top = jnp.concatenate([gxl[:, 56:], og[:, 56:], gxh[:, 56:]], axis=0)
-    bottom = jnp.concatenate([gxl[:, :8], og[:, :8], gxh[:, :8]], axis=0)
-    gyl = lax.ppermute(top, space, up)
-    gyh = lax.ppermute(bottom, space, down)
-
     pick = np.zeros((176, 128), np.float32)
     for c in range(8):
         for j in range(22):
             if 0 <= 16 * c - 3 + j < 128:
                 pick[c * 22 + j, 16 * c - 3 + j] = 1.0
+    og = out_grad.reshape(BX, BY * NZ, C)
+    gxl = lax.ppermute(og[BX - 1 :], "chan", xup)
+    gxh = lax.ppermute(og[:1], "chan", xdown)
     packed = pl.pallas_call(
         pack_kernel,
         out_shape=jax.ShapeDtypeStruct((176 * 16, 128), BF),
         in_specs=[VMEM, VMEM],
         out_specs=VMEM,
         scratch_shapes=[pltpu.VMEM((176 * 16, 128), F32)],
-        compiler_params=params(),
+        compiler_params=params(12),
         cost_estimate=cost(16 * 176 * 128 * 256, 3 << 20),
         name="pack",
     )(jnp.asarray(pick, BF), jnp.transpose(volume, (1, 2, 3, 0)))
     near = lax.all_to_all(packed.reshape(8, 352, 128), "chan", 0, 0, tiled=True)
+
+    w1 = jnp.transpose(first_filters, (0, 1, 2, 4, 3)).reshape(27, 32, C)
+    half = lax.dynamic_slice_in_dim(w1, core * 128, 128, axis=2)
+    spread = jnp.broadcast_to(half.reshape(1, 864, 128), (8, 864, 128))
+    spread, near = lax.optimization_barrier((spread, near))
+    pieces = lax.all_to_all(spread, "chan", 0, 0, tiled=True)
+
+    top = jnp.concatenate([gxl[:, 56:], og[:, 56:], gxh[:, 56:]], axis=0)
+    bottom = jnp.concatenate([gxl[:, :8], og[:, :8], gxh[:, :8]], axis=0)
+    gyl = lax.ppermute(top, space, up)
+    gyh = lax.ppermute(bottom, space, down)
+    near, gyl, gyh = lax.optimization_barrier((near, gyl, gyh))
     near = near.reshape(8, 22, 16, 128)
     low = lax.ppermute(near[:, :, 8:], space, up)
     high = lax.ppermute(near[:, :, :8], space, down)
-
-    mine = jnp.stack(pieces)
+    v3 = pl.pallas_call(
+        unpack_kernel,
+        out_shape=jax.ShapeDtypeStruct((22, 112, 3 * C), BF),
+        in_specs=[SMEM, VMEM, VMEM, VMEM],
+        out_specs=VMEM,
+        compiler_params=params(24),
+        cost_estimate=cost(1.5e9, 6 << 20),
+        name="unpack",
+    )(place, near, low, high)
+    v3, pieces = lax.optimization_barrier((v3, pieces))
+
+    mine = pl.pallas_call(
+        turn_kernel,
+        out_shape=jax.ShapeDtypeStruct((27, 128, C), BF),
+        in_specs=[VMEM],
+        out_specs=VMEM,
+        compiler_params=params(12),
+        cost_estimate=cost(1e9, 4 << 20),
+        name="turn",
+    )(pieces.reshape(8, 27, 32, 128))
     other = lax.ppermute(mine, "core", swap)
 
     w2 = second_filters.reshape(9, 3 * C, C)
@@ -265,36 +293,44 @@
             jax.ShapeDtypeStruct((SLOT, C), BF),
             jax.ShapeDtypeStruct((18, 80, 3 * C), BF),
         ),
-        in_specs=[SMEM] + [VMEM] * 11,
+        in_specs=[SMEM] + [VMEM] * 9,
         out_specs=(VMEM, VMEM, VMEM),
         scratch_shapes=[
-            pltpu.VMEM((22, 112, 3 * C), BF),
             pltpu.VMEM((20, 96, 3 * C), BF),
-            pltpu.VMEM((9, C, 3 * C), BF),
             pltpu.VMEM((480, C), F32),
             pltpu.VMEM((18, 80, C), BF),
             pltpu.VMEM((C, 1024), BF),
             pltpu.VMEM((2 * SLOT, C), BF),
         ],
-        compiler_params=params(),
+        compiler_params=params(44),
         cost_estimate=cost(16e9, 20 << 20),
         name="layers",
-    )(place, near, low, high, mine, other, w2, og, gxl, gxh, gyl, gyh)
-
+    )(place, v3, mine, other, w2, og, gxl, gxh, gyl, gyh)
+
+    w2_back = pl.pallas_call(
+        flip_kernel,
+        out_shape=jax.ShapeDtypeStruct((9, 3 * C, C), BF),
+        in_specs=[VMEM],
+        out_specs=VMEM,
+        compiler_params=params(12),
+        cost_estimate=cost(1e9, 7 << 20),
+        name="flip",
+    )(w2)
     received = lax.ppermute(send, "core", swap)
     act_grad = pl.pallas_call(
         back_kernel,
         out_shape=jax.ShapeDtypeStruct((BX, BY * NZ, C), BF),
         in_specs=[VMEM, VMEM],
         out_specs=VMEM,
-        scratch_shapes=[pltpu.VMEM((512, C), F32)],
-        compiler_params=params(),
+        scratch_shapes=[pltpu.VMEM((1024, C), F32)],
+        compiler_params=params(16),
         cost_estimate=cost(3.6e9, 7 << 20),
         name="back",
-    )(d3, w2)
+    )(d3, w2_back)
 
     both = (keep.astype(F32) + received.astype(F32)).astype(BF).reshape(64, 56, C)
     shares = lax.all_to_all(both, CHIPS, 0, 0, tiled=True)
+    shares, act_grad = lax.optimization_barrier((shares, act_grad))
     scale = 1.0 / math.sqrt(128 * 128 * NZ)
     share = (jnp.sum(shares.astype(F32), axis=0) * scale).astype(BF)
     spread = lax.optimization_barrier(jnp.broadcast_to(share[None], (64, 56, C)))
@@ -303,12 +339,12 @@
     whole = pl.BlockSpec((SLOT, C), lambda t: (0, 0))
     filter_grad = pl.pallas_call(
         finish_kernel,
-        grid=(27,),
+        grid=(9,),
         out_shape=jax.ShapeDtypeStruct((27, C, C), F32),
         in_specs=[SMEM, whole, whole],
-        out_specs=pl.BlockSpec((1, C, C), lambda t: (t, 0, 0)),
+        out_specs=pl.BlockSpec((3, C, C), lambda t: (t, 0, 0)),
         scratch_shapes=[pltpu.VMEM((2 * HALF, C), BF)],
-        compiler_params=params(),
+        compiler_params=params(20),
         cost_estimate=cost(1e9, 11 << 20),
         name="finish",
     )(place, ours, theirs)

time: 202 us -> 177 us (0.88)
  blocking collectives: 65.2 us -> 29.7 us
  starting transfers between devices: 37.1 us -> 51.2 us
  Pallas kernels: 52.3 us -> 39.5 us
  local copies, waits for them, and re-layouts: 5.06 us -> 10.3 us
  waiting for transfers between devices: 38 us -> 40.6 us
    all_to_all x1 -> x0, blocking collectives: 35.2 us -> none  [local(): shares = lax.all_to_all(both, CHIPS, 0, 0, tiled=True)]
    ppermute x7 -> x0, waiting for transfers between devices: 26.1 us -> none  [local(): lax.ppermute(half, 'chan', [(i, (i + d) % 8) for i in range(8)])]
    all_to_all x0 -> x2, starting transfers between devices: none -> 19.8 us  [the longest x1 16.2 us: local(): shares = lax.all_to_all(both, CHIPS, 0, 0, tiled=True)]
    all_to_all x0 -> x2, waiting for transfers between devices: none -> 16.9 us  [the longest x1 16.9 us: local(): shares = lax.all_to_all(both, CHIPS, 0, 0, tiled=True)]
    ppermute x7 -> x0, starting transfers between devices: 11.6 us -> none  [local(): lax.ppermute(half, 'chan', [(i, (i + d) % 8) for i in range(8)])]
    all_to_all x1, waiting for transfers between devices: 0.01 us -> 5.61 us  [local(): near = lax.all_to_all(packed.reshape(8, 352, 128), 'chan', 0, 0, tiled=True)]
    pallas_call x1, Pallas kernels: 26.8 us -> 21.4 us  [local(): pl.pallas_call(layers_kernel, out_shape=(jax.ShapeDtypeStruct((SLOT, C),...]
    ppermute x1, waiting for transfers between devices: 4.77 us -> 0.01 us  [local(): gxh = lax.ppermute(og[:1], 'chan', xdown)]
  transfers between devices with their start and end apart: 17 -> 12, of which waited for: 7 -> 8; matrix products, arithmetic and copies ran while one was open for 1% -> 2% of each run, Pallas kernels for 5% -> 5%
where the time goes in v1:
time: 177 us; the launch traced here: 176 us
  starting transfers between devices  51.2 us (29%)
  waiting for transfers between devices  40.6 us (23%)
  Pallas kernels  39.5 us (22%)
  blocking collectives  29.7 us (17%)
  local copies, waits for them, and re-layouts  10.3 us (6%)
  other arithmetic  3.66 us (2%)
    all_to_all x1, blocking collectives, local(): ours = lax.all_to_all(spread, CHIPS, 0, 0, tiled=True).reshape(SLOT, C)  29.7 us
    pallas_call x1, Pallas kernels, local(): pl.pallas_call(layers_kernel, out_shape=(jax.ShapeDtypeStruct((SLOT, C),...  21.4 us
    all_to_all x1, waiting for transfers between devices, local(): shares = lax.all_to_all(both, CHIPS, 0, 0, tiled=True)  16.9 us
    all_to_all x1, starting transfers between devices, local(): shares = lax.all_to_all(both, CHIPS, 0, 0, tiled=True)  16.2 us
    all_to_all x1, starting transfers between devices, local(): near = lax.all_to_all(packed.reshape(8, 352, 128), 'chan', 0, 0, tiled=True)  8.17 us
    unnamed x20, local copies, waits for them, and re-layouts  7.01 us
    pallas_call x1, Pallas kernels, local(): pl.pallas_call(finish_kernel, grid=(9,), out_shape=jax.ShapeDtypeStruct((...  6.72 us
    all_to_all x1, waiting for transfers between devices, local(): near = lax.all_to_all(packed.reshape(8, 352, 128), 'chan', 0, 0, tiled=True)  5.61 us
  transfers between devices with their start and end apart: 12, of which 8 were waited for; matrix products, arithmetic and copies ran while one was open for 2% of the time, Pallas kernels for 5%

profile of v1, /device:TPU:1, one launch (start us, length us, event | category | flops | bytes accessed | tf_op | source)
XLA Modules:
  0.0 175.8 jit_solution(14782619008942068807)
XLA Ops:
  0.6 0.0 copy-start
  0.6 0.0 copy-start.2
  0.7 1.1 copy-done.2
  1.7 0.0 copy-start.4
  1.7 0.8 copy-done.4
  2.5 0.0 copy-start.3
  2.5 1.6 pack.1
  4.2 8.2 %all-to-all-start = ((bf16[8,352,128]{2,1,0:T(8,128)(2,1)}), bf16[8,352,128]{2,1,0:T(8,128)(2,1)S(1)}, u32[]{:S(2)}, u32[]{:S(2)}) async-start(bf16[8,352,128]{2,1,0:T(8,128)(2,1)} %bitcast.7), calls=%async_computation | async-start | bytes 1441792 | tf_op jit(solution)/shard_map/all_to_all | solution.py:250
  12.3 0.0 copy-done.3
  12.3 0.6 slice_bitcast_fusion.1
  13.0 4.9 %collective-permute-start = (bf16[1,64,256]{2,1,0:T(8,128)(2,1)}, bf16[1,64,256]{2,1,0:T(8,128)(2,1)S(1)}, u32[]{:S(2)}, u32[]{:S(2)}) collective-permute-start(bf16[1,64,256]{2,1,0:T(8,128)(2,1)} %get-tuple-element.30), channel_id=1, source_target_pairs={{0,16},{16,32},{32,48},{48,64},{64,80},{80,96},{96,112},{1,17},{17... | collective-permute-start | bytes 98312 | tf_op jit(solution)/shard_map/ppermute | solution.py:238
  17.8 1.3 collective-permute-start.1
  19.1 0.0 copy-done
  19.2 5.6 %all-to-all-done = bf16[8,352,128]{2,1,0:T(8,128)(2,1)S(1)} async-done(((bf16[8,352,128]{2,1,0:T(8,128)(2,1)}), bf16[8,352,128]{2,1,0:T(8,128)(2,1)S(1)}, u32[]{:S(2)}, u32[]{:S(2)}) %all-to-all-start) | async-done | bytes 720928 | tf_op jit(solution)/shard_map/all_to_all | solution.py:250
  24.8 1.5 broadcast_in_dim.14
  26.3 3.6 %all-to-all-start.1 = ((bf16[8,864,128]{2,1,0:T(8,128)(2,1)}), bf16[8,864,128]{2,1,0:T(8,128)(2,1)S(1)}, u32[]{:S(2)}, u32[]{:S(2)}) async-start(bf16[8,864,128]{2,1,0:T(8,128)(2,1)} %broadcast_in_dim.14), calls=%async_computation.1 | async-start | bytes 3538944 | tf_op jit(solution)/shard_map/all_to_all | solution.py:256
  29.9 0.0 collective-permute-done.gxl_ref
  29.9 0.0 collective-permute-done.1.gxh_ref
  30.0 4.6 %collective-permute-start.2 = (bf16[18,8,256]{2,1,0:T(8,128)(2,1)S(1)}, bf16[18,8,256]{2,1,0:T(8,128)(2,1)S(1)}, u32[]{:S(2)}, u32[]{:S(2)}) collective-permute-start(bf16[18,8,256]{2,1,0:T(8,128)(2,1)S(1)} %pad_maximum_fusion), channel_id=1, source_target_pairs={{0,1},{1,2},{2,3},{3,4},{4,5},{5,6},{6,7},{7,8},{8,9},{9,10},{10,1... | collective-permute-start | bytes 221192 | tf_op jit(solution)/shard_map/ppermute | solution.py:260
  34.6 1.9 %collective-permute-start.3 = (bf16[18,8,256]{2,1,0:T(8,128)(2,1)S(1)}, bf16[18,8,256]{2,1,0:T(8,128)(2,1)S(1)}, u32[]{:S(2)}, u32[]{:S(2)}) collective-permute-start(bf16[18,8,256]{2,1,0:T(8,128)(2,1)S(1)} %pad_maximum_fusion.1), channel_id=1, source_target_pairs={{1,0},{2,1},{3,2},{4,3},{5,4},{6,5},{7,6},{8,7},{9,8},{10,9},{11,1... | collective-permute-start | bytes 221192 | tf_op jit(solution)/shard_map/ppermute | solution.py:261
  36.5 0.0 collective-permute-done.2.gyl_ref
  36.5 0.0 copy-start.5
  36.5 0.6 copy-done.5
  37.2 3.4 %collective-permute-done.3.gyh_ref = bf16[18,8,256]{2,1,0:T(8,128)(2,1)S(1)} collective-permute-done((bf16[18,8,256]{2,1,0:T(8,128)(2,1)S(1)}, bf16[18,8,256]{2,1,0:T(8,128)(2,1)S(1)}, u32[]{:S(2)}, u32[]{:S(2)}) %collective-permute-start.3) | collective-permute-done | bytes 73760 | tf_op jit(solution)/shard_map/ppermute | solution.py:261
  40.5 0.0 copy-start.7
  40.5 0.6 copy-done.7
  41.2 1.0 fusion
  42.2 1.9 %collective-permute-start.5 = (bf16[8,22,8,128]{3,2,1,0:T(8,128)(2,1)}, bf16[8,22,8,128]{3,2,1,0:T(8,128)(2,1)}, u32[]{:S(2)}, u32[]{:S(2)}) collective-permute-start(bf16[8,22,8,128]{3,2,1,0:T(8,128)(2,1)} %get-tuple-element.26), channel_id=1, source_target_pairs={{1,0},{2,1},{3,2},{4,3},{5,4},{6,5},{7,6},{8,7},{9,8},{10,9},{11,1... | collective-permute-start | bytes 1081352 | tf_op jit(solution)/shard_map/ppermute | solution.py:265
  44.1 3.6 %collective-permute-start.4 = (bf16[8,22,8,128]{3,2,1,0:T(8,128)(2,1)}, bf16[8,22,8,128]{3,2,1,0:T(8,128)(2,1)}, u32[]{:S(2)}, u32[]{:S(2)}) collective-permute-start(bf16[8,22,8,128]{3,2,1,0:T(8,128)(2,1)} %get-tuple-element.27), channel_id=1, source_target_pairs={{0,1},{1,2},{2,3},{3,4},{4,5},{5,6},{6,7},{7,8},{8,9},{9,10},{10,1... | collective-permute-start | bytes 1081352 | tf_op jit(solution)/shard_map/ppermute | solution.py:264
  47.7 0.1 pad_add_fusion.place_ref
  47.8 3.6 %collective-permute-done.5.high_ref = bf16[8,22,8,128]{3,2,1,0:T(8,128)(2,1)} collective-permute-done((bf16[8,22,8,128]{3,2,1,0:T(8,128)(2,1)}, bf16[8,22,8,128]{3,2,1,0:T(8,128)(2,1)}, u32[]{:S(2)}, u32[]{:S(2)}) %collective-permute-start.5) | collective-permute-done | bytes 360480 | tf_op jit(solution)/shard_map/ppermute | solution.py:265
  51.4 1.0 collective-permute-done.4.low_ref
  52.4 2.8 %unpack.1.v3_ref = bf16[22,112,768]{2,1,0:T(8,128)(2,1)S(1)} custom-call(s32[3]{0:T(128)S(1)} %pad_add_fusion.place_ref, bf16[8,22,16,128]{3,2,1,0:T(8,128)(2,1)S(1)} %bitcast.27, bf16[8,22,8,128]{3,2,1,0:T(8,128)(2,1)} %collective-permute-done.4.low_ref, bf16[8,22,8,128]{3,2,1,0:T(8,128)(2,1)} %collective-permute-done.5.high_ref), custom_call_target="tpu_custom_call" | custom-call | flops 1500000000 | bytes 6291456 | tf_op jit(solution)/shard_map/unpack/pallas_call | solution.py:266
  55.2 0.0 copy-start.9
  55.2 1.9 %copy-done.9 = bf16[22,112,768]{2,1,0:T(8,128)(2,1)} copy-done((bf16[22,112,768]{2,1,0:T(8,128)(2,1)}, bf16[22,112,768]{2,1,0:T(8,128)(2,1)S(1)}, u32[]{:S(2)}) %copy-start.9) | copy-done | bytes 3784728
  57.0 0.0 all-to-all-done.1
  57.0 0.0 copy-start.6
  57.0 0.0 copy-start.8
  57.0 0.9 turn.1.mine_ref
  58.0 0.5 collective-permute-start.6
  58.5 3.3 %collective-permute-done.6.other_ref = bf16[27,128,256]{2,1,0:T(8,128)(2,1)S(1)} collective-permute-done((bf16[27,128,256]{2,1,0:T(8,128)(2,1)S(1)}, bf16[27,128,256]{2,1,0:T(8,128)(2,1)S(1)}, u32[]{:S(2)}, u32[]{:S(2)}) %collective-permute-start.6) | collective-permute-done | bytes 1769504 | tf_op jit(solution)/shard_map/ppermute | solution.py:286
  61.8 0.0 copy-done.6
  61.8 0.0 copy-done.8
  61.8 21.4 %layers.1 = (bf16[3584,256]{1,0:T(8,128)(2,1)S(1)}, bf16[3584,256]{1,0:T(8,128)(2,1)S(1)}, bf16[18,80,768]{2,1,0:T(8,128)(2,1)S(1)}) custom-call(s32[3]{0:T(128)S(1)} %pad_add_fusion.place_ref, bf16[22,112,768]{2,1,0:T(8,128)(2,1)} %copy-done.9, bf16[27,128,256]{2,1,0:T(8,128)(2,1)S(1)} %turn.1.mine_ref, ...), custom_call_target="tpu_custom_call" | custom-call | flops 16000000000 | bytes 20971520 | tf_op jit(solution)/shard_map/layers/pallas_call | solution.py:289
  83.2 0.5 collective-permute-start.7
  83.7 3.4 %collective-permute-done.7 = bf16[3584,256]{1,0:T(8,128)(2,1)S(1)} collective-permute-done((bf16[3584,256]{1,0:T(8,128)(2,1)S(1)}, bf16[3584,256]{1,0:T(8,128)(2,1)S(1)}, u32[]{:S(2)}, u32[]{:S(2)}) %collective-permute-start.7) | collective-permute-done | bytes 1835040 | tf_op jit(solution)/shard_map/ppermute | solution.py:319
  87.1 1.8 %add_convert_fusion = bf16[3584,256]{1,0:T(8,128)(2,1)} fusion(bf16[3584,256]{1,0:T(8,128)(2,1)S(1)} %collective-permute-done.7, bf16[3584,256]{1,0:T(8,128)(2,1)S(1)} %get-tuple-element.21), kind=kLoop, calls=%fused_computation.1 | loop fusion | flops 3670016 | bytes 5505024 | tf_op jit(solution)/shard_map/convert_element_type | solution.py:331
  88.9 16.2 %all-to-all-start.2 = ((bf16[64,56,256]{2,1,0:T(8,128)(2,1)}), bf16[64,56,256]{2,1,0:T(8,128)(2,1)}, u32[]{:S(2)}, u32[]{:S(2)}) async-start(bf16[64,56,256]{2,1,0:T(8,128)(2,1)} %bitcast.32), calls=%async_computation.2 | async-start | bytes 3670016 | tf_op jit(solution)/shard_map/all_to_all | solution.py:332
  105.1 0.0 copy-start.1
  105.1 2.0 %copy-done.1 = bf16[3,3,3,256,256]{4,3,2,1,0:T(8,128)(2,1)S(1)} copy-done((bf16[3,3,3,256,256]{4,3,2,1,0:T(8,128)(2,1)S(1)}, bf16[3,3,3,256,256]{4,3,2,1,0:T(8,128)(2,1)}, u32[]{:S(2)}) %copy-start.1) | copy-done | bytes 3538968
  107.1 1.4 flip.1.w2_ref
  108.5 4.6 %back.1 = bf16[16,64,256]{2,1,0:T(8,128)(2,1)} custom-call(bf16[18,80,768]{2,1,0:T(8,128)(2,1)S(1)} %get-tuple-element.23.d3_ref, bf16[9,768,256]{2,1,0:T(8,128)(2,1)S(1)} %flip.1.w2_ref), custom_call_target="tpu_custom_call" | custom-call | flops 3600000000 | bytes 7340032 | tf_op jit(solution)/shard_map/back/pallas_call | solution.py:320
  113.1 16.9 %all-to-all-done.2 = bf16[64,56,256]{2,1,0:T(8,128)(2,1)} async-done(((bf16[64,56,256]{2,1,0:T(8,128)(2,1)}), bf16[64,56,256]{2,1,0:T(8,128)(2,1)}, u32[]{:S(2)}, u32[]{:S(2)}) %all-to-all-start.2) | async-done | bytes 1835040 | tf_op jit(solution)/shard_map/all_to_all | solution.py:332
  130.0 1.8 %convert_reduce_fusion = f32[56,256]{1,0:T(8,128)S(1)} fusion(bf16[64,56,256]{2,1,0:T(8,128)(2,1)} %all-to-all-done.2), kind=kLoop, calls=%fused_computation | loop fusion | flops 1820672 | bytes 1892352 | tf_op jit(solution)/shard_map/reduce_sum | solution.py:335
  131.8 0.1 broadcast_in_dim.15
  131.9 29.7 %all_to_all.20 = bf16[64,56,256]{2,1,0:T(8,128)(2,1)S(1)} all-to-all(bf16[64,56,256]{2,1,0:T(8,128)(2,1)S(1)} %broadcast_in_dim.15), channel_id=1, replica_groups=mesh['chan'=8,'slab'=8,'core'=2] {'chan','slab'}, dimensions={0} | all-to-all | bytes 3670016 | tf_op jit(solution)/shard_map/all_to_all | solution.py:337
  161.7 4.0 %collective-permute-start.8 = (bf16[3584,256]{1,0:T(8,128)(2,1)S(1)}, bf16[3584,256]{1,0:T(8,128)(2,1)S(1)}, u32[]{:S(2)}, u32[]{:S(2)}) collective-permute-start(bf16[3584,256]{1,0:T(8,128)(2,1)S(1)} %bitcast.22), channel_id=1, source_target_pairs={{0,1},{1,0},{2,3},{3,2},{4,5},{5,4},{6,7},{7,6},{8,9},{9,8},{10,11... | collective-permute-start | bytes 5505032 | tf_op jit(solution)/shard_map/ppermute | solution.py:338
  165.7 3.4 %collective-permute-done.8.other_ref = bf16[3584,256]{1,0:T(8,128)(2,1)S(1)} collective-permute-done((bf16[3584,256]{1,0:T(8,128)(2,1)S(1)}, bf16[3584,256]{1,0:T(8,128)(2,1)S(1)}, u32[]{:S(2)}, u32[]{:S(2)}) %collective-permute-start.8) | collective-permute-done | bytes 1835040 | tf_op jit(solution)/shard_map/ppermute | solution.py:338
  169.1 6.7 %finish.1 = f32[27,256,256]{2,1,0:T(8,128)} custom-call(s32[3]{0:T(128)S(1)} %pad_add_fusion.place_ref, bf16[3584,256]{1,0:T(8,128)(2,1)S(1)} %bitcast.23, bf16[3584,256]{1,0:T(8,128)(2,1)S(1)} %collective-permute-done.8.other_ref), custom_call_target="tpu_custom_call" | custom-call | flops 1000000000 | bytes 11534336 | tf_op jit(solution)/shard_map/finish/pallas_call | solution.py:340
  (7 shorter events, 0.1 us)
Async XLA Ops:
  0.6 18.5 %copy-start = (bf16[3,3,3,256,32]{3,4,2,1,0:T(8,128)(2,1)S(1)}, bf16[3,3,3,256,32]{3,4,2,1,0:T(8,128)(2,1)}, u32[]{:S(2)}) copy-start(bf16[3,3,3,256,32]{3,4,2,1,0:T(8,128)(2,1)} %param.6) | copy-start | bytes 1327108
  0.6 1.1 copy-start.2
  1.7 0.8 copy-start.4
  2.5 9.8 %copy-start.3 = (bf16[16,8,8,256]{3,2,1,0:T(8,128)(2,1)S(1)}, bf16[16,8,8,256]{3,2,1,0:T(8,128)(2,1)}, u32[]{:S(2)}) copy-start(bf16[16,8,8,256]{3,2,1,0:T(8,128)(2,1)} %param.8) | copy-start | bytes 1572868
  4.2 20.6 %all-to-all-start = ((bf16[8,352,128]{2,1,0:T(8,128)(2,1)}), bf16[8,352,128]{2,1,0:T(8,128)(2,1)S(1)}, u32[]{:S(2)}, u32[]{:S(2)}) async-start(bf16[8,352,128]{2,1,0:T(8,128)(2,1)} %bitcast.7), calls=%async_computation | async-start | bytes 1441792 | tf_op jit(solution)/shard_map/all_to_all | solution.py:250
  13.0 16.9 %collective-permute-start = (bf16[1,64,256]{2,1,0:T(8,128)(2,1)}, bf16[1,64,256]{2,1,0:T(8,128)(2,1)S(1)}, u32[]{:S(2)}, u32[]{:S(2)}) collective-permute-start(bf16[1,64,256]{2,1,0:T(8,128)(2,1)} %get-tuple-element.30), channel_id=1, source_target_pairs={{0,16},{16,32},{32,48},{48,64},{64,80},{80,96},{96,112},{1,17},{17... | collective-permute-start | bytes 98312 | tf_op jit(solution)/shard_map/ppermute | solution.py:238
  17.8 12.1 %collective-permute-start.1 = (bf16[1,64,256]{2,1,0:T(8,128)(2,1)}, bf16[1,64,256]{2,1,0:T(8,128)(2,1)S(1)}, u32[]{:S(2)}, u32[]{:S(2)}) collective-permute-start(bf16[1,64,256]{2,1,0:T(8,128)(2,1)} %get-tuple-element.31), channel_id=1, source_target_pairs={{16,0},{32,16},{48,32},{64,48},{80,64},{96,80},{112,96},{17,1},{33... | collective-permute-start | bytes 98312 | tf_op jit(solution)/shard_map/ppermute | solution.py:239
  26.3 30.7 %all-to-all-start.1 = ((bf16[8,864,128]{2,1,0:T(8,128)(2,1)}), bf16[8,864,128]{2,1,0:T(8,128)(2,1)S(1)}, u32[]{:S(2)}, u32[]{:S(2)}) async-start(bf16[8,864,128]{2,1,0:T(8,128)(2,1)} %broadcast_in_dim.14), calls=%async_computation.1 | async-start | bytes 3538944 | tf_op jit(solution)/shard_map/all_to_all | solution.py:256
  30.0 6.5 %collective-permute-start.2 = (bf16[18,8,256]{2,1,0:T(8,128)(2,1)S(1)}, bf16[18,8,256]{2,1,0:T(8,128)(2,1)S(1)}, u32[]{:S(2)}, u32[]{:S(2)}) collective-permute-start(bf16[18,8,256]{2,1,0:T(8,128)(2,1)S(1)} %pad_maximum_fusion), channel_id=1, source_target_pairs={{0,1},{1,2},{2,3},{3,4},{4,5},{5,6},{6,7},{7,8},{8,9},{9,10},{10,1... | collective-permute-start | bytes 221192 | tf_op jit(solution)/shard_map/ppermute | solution.py:260
  34.6 6.0 %collective-permute-start.3 = (bf16[18,8,256]{2,1,0:T(8,128)(2,1)S(1)}, bf16[18,8,256]{2,1,0:T(8,128)(2,1)S(1)}, u32[]{:S(2)}, u32[]{:S(2)}) collective-permute-start(bf16[18,8,256]{2,1,0:T(8,128)(2,1)S(1)} %pad_maximum_fusion.1), channel_id=1, source_target_pairs={{1,0},{2,1},{3,2},{4,3},{5,4},{6,5},{7,6},{8,7},{9,8},{10,9},{11,1... | collective-permute-start | bytes 221192 | tf_op jit(solution)/shard_map/ppermute | solution.py:261
  36.5 0.6 copy-start.5
  40.5 0.6 copy-start.7
  42.2 9.2 %collective-permute-start.5 = (bf16[8,22,8,128]{3,2,1,0:T(8,128)(2,1)}, bf16[8,22,8,128]{3,2,1,0:T(8,128)(2,1)}, u32[]{:S(2)}, u32[]{:S(2)}) collective-permute-start(bf16[8,22,8,128]{3,2,1,0:T(8,128)(2,1)} %get-tuple-element.26), channel_id=1, source_target_pairs={{1,0},{2,1},{3,2},{4,3},{5,4},{6,5},{7,6},{8,7},{9,8},{10,9},{11,1... | collective-permute-start | bytes 1081352 | tf_op jit(solution)/shard_map/ppermute | solution.py:265
  44.1 8.3 %collective-permute-start.4 = (bf16[8,22,8,128]{3,2,1,0:T(8,128)(2,1)}, bf16[8,22,8,128]{3,2,1,0:T(8,128)(2,1)}, u32[]{:S(2)}, u32[]{:S(2)}) collective-permute-start(bf16[8,22,8,128]{3,2,1,0:T(8,128)(2,1)} %get-tuple-element.27), channel_id=1, source_target_pairs={{0,1},{1,2},{2,3},{3,4},{4,5},{5,6},{6,7},{7,8},{8,9},{9,10},{10,1... | collective-permute-start | bytes 1081352 | tf_op jit(solution)/shard_map/ppermute | solution.py:264
  55.2 1.9 %copy-start.9 = (bf16[22,112,768]{2,1,0:T(8,128)(2,1)}, bf16[22,112,768]{2,1,0:T(8,128)(2,1)S(1)}, u32[]{:S(2)}) copy-start(bf16[22,112,768]{2,1,0:T(8,128)(2,1)S(1)} %unpack.1.v3_ref) | copy-start | bytes 11354116
  57.0 4.8 %copy-start.6 = (bf16[18,8,256]{2,1,0:T(8,128)(2,1)S(1)}, bf16[18,8,256]{2,1,0:T(8,128)(2,1)}, u32[]{:S(2)}) copy-start(bf16[18,8,256]{2,1,0:T(8,128)(2,1)} %copy-done.5) | copy-start | bytes 221188
  57.0 4.8 %copy-start.8 = (bf16[18,8,256]{2,1,0:T(8,128)(2,1)S(1)}, bf16[18,8,256]{2,1,0:T(8,128)(2,1)}, u32[]{:S(2)}) copy-start(bf16[18,8,256]{2,1,0:T(8,128)(2,1)} %copy-done.7) | copy-start | bytes 221188
  58.0 3.8 %collective-permute-start.6 = (bf16[27,128,256]{2,1,0:T(8,128)(2,1)S(1)}, bf16[27,128,256]{2,1,0:T(8,128)(2,1)S(1)}, u32[]{:S(2)}, u32[]{:S(2)}) collective-permute-start(bf16[27,128,256]{2,1,0:T(8,128)(2,1)S(1)} %turn.1.mine_ref), channel_id=1, source_target_pairs={{0,1},{1,0},{2,3},{3,2},{4,5},{5,4},{6,7},{7,6},{8,9},{9,8},{10,11... | collective-permute-start | bytes 5308424 | tf_op jit(solution)/shard_map/ppermute | solution.py:286
  83.2 3.9 %collective-permute-start.7 = (bf16[3584,256]{1,0:T(8,128)(2,1)S(1)}, bf16[3584,256]{1,0:T(8,128)(2,1)S(1)}, u32[]{:S(2)}, u32[]{:S(2)}) collective-permute-start(bf16[3584,256]{1,0:T(8,128)(2,1)S(1)} %get-tuple-element.22), channel_id=1, source_target_pairs={{0,1},{1,0},{2,3},{3,2},{4,5},{5,4},{6,7},{7,6},{8,9},{9,8},{10,11... | collective-permute-start | bytes 5505032 | tf_op jit(solution)/shard_map/ppermute | solution.py:319
  88.9 41.1 %all-to-all-start.2 = ((bf16[64,56,256]{2,1,0:T(8,128)(2,1)}), bf16[64,56,256]{2,1,0:T(8,128)(2,1)}, u32[]{:S(2)}, u32[]{:S(2)}) async-start(bf16[64,56,256]{2,1,0:T(8,128)(2,1)} %bitcast.32), calls=%async_computation.2 | async-start | bytes 3670016 | tf_op jit(solution)/shard_map/all_to_all | solution.py:332
  105.1 2.0 %copy-start.1 = (bf16[3,3,3,256,256]{4,3,2,1,0:T(8,128)(2,1)S(1)}, bf16[3,3,3,256,256]{4,3,2,1,0:T(8,128)(2,1)}, u32[]{:S(2)}) copy-start(bf16[3,3,3,256,256]{4,3,2,1,0:T(8,128)(2,1)} %param.7) | copy-start | bytes 10616836
  161.7 7.4 %collective-permute-start.8 = (bf16[3584,256]{1,0:T(8,128)(2,1)S(1)}, bf16[3584,256]{1,0:T(8,128)(2,1)S(1)}, u32[]{:S(2)}, u32[]{:S(2)}) collective-permute-start(bf16[3584,256]{1,0:T(8,128)(2,1)S(1)} %bitcast.22), channel_id=1, source_target_pairs={{0,1},{1,0},{2,3},{3,2},{4,5},{5,4},{6,7},{7,6},{8,9},{9,8},{10,11... | collective-permute-start | bytes 5505032 | tf_op jit(solution)/shard_map/ppermute | solution.py:338

commit v2 on v1

--- a/solution.py
+++ b/solution.py
@@ -1,8 +1,8 @@
+import functools
 import math
 
 import jax
 import jax.numpy as jnp
-import numpy as np
 from jax import lax
 from jax.experimental import pallas as pl
 from jax.experimental.pallas import tpu as pltpu
@@ -14,8 +14,11 @@
 C = 256
 NZ = 8
 BX, BY = 16, 8
-HALF = 3456
-SLOT = 3584
+TAPS = 14
+SLOT = TAPS * C
+VOL = 352
+STRAIGHT = 15
+QUARTER = (27 - STRAIGHT) // 4
 CHIPS = ("chan", "slab")
 VMEM = pl.BlockSpec(memory_space=pltpu.VMEM)
 SMEM = pl.BlockSpec(memory_space=pltpu.SMEM)
@@ -37,13 +40,25 @@
     return lax.dot_general(a, b, (((1,), (0,)), ((), ())), preferred_element_type=F32)
 
 
-def pack_kernel(pick_ref, vol_ref, out_ref, wide_ref):
-    pick = pick_ref[...]
+def pack_kernel(place_ref, vol_ref, filters_ref, out_ref, straight_ref, wide_ref):
+    row = lax.broadcasted_iota(jnp.int32, (176, 128), 0)
+    col = lax.broadcasted_iota(jnp.int32, (176, 128), 1)
+    c = sum((row >= 22 * n).astype(jnp.int32) for n in range(1, 8))
+    pick = (col == row - 6 * c - 3).astype(F32).astype(BF)
     for quad in range(2):
         for z in range(NZ):
             rows = jnp.concatenate([vol_ref[quad * 4 + j, z] for j in range(4)], axis=0)
-            wide_ref[pl.ds(quad * 8 + z, 176, stride=16), :] = dot_t(pick, rows)
-    out_ref[...] = wide_ref[...].astype(BF)
+            wide_ref[quad, pl.ds(z, 176, stride=8), :] = dot_t(pick, rows)
+    lanes = pl.ds(pl.multiple_of(place_ref[2] * 128, 128), 128)
+    mine = pl.ds(STRAIGHT + QUARTER * place_ref[3], QUARTER)
+    quarter = filters_ref[mine, :, lanes].reshape(QUARTER * 32, 128)
+    straight = filters_ref[0:STRAIGHT, :, lanes].reshape(STRAIGHT * 32, 128)
+    for c in range(8):
+        for quad in range(2):
+            part = wide_ref[quad, c * 176 : c * 176 + 176, :]
+            out_ref[c, quad * 176 : quad * 176 + 176, :] = part.astype(BF)
+        out_ref[c, VOL : VOL + QUARTER * 32, :] = quarter
+        straight_ref[c] = straight
 
 
 def neighbours(value):
@@ -65,10 +80,8 @@
             if y < 0 or y >= 14:
                 continue
             src = (low_ref, near_ref, near_ref, high_ref)[b]
-            at = 8 if b == 2 else 0
-            rows = jnp.concatenate(
-                [src[c, :, at : at + 8, :].reshape(176, 128) for c in range(8)], axis=1
-            )
+            at = 176 if b == 2 else 0
+            rows = jnp.concatenate([src[c, at : at + 176, :] for c in range(8)], axis=1)
             value = dot_n(rows, sel).reshape(22, NZ, C)
             before, after = neighbours(value)
             v3_ref[:, y * 8 : y * 8 + 8, 0:C] = before
@@ -76,14 +89,20 @@
             v3_ref[:, y * 8 : y * 8 + 8, 2 * C : 3 * C] = after
 
 
-def turn_kernel(pieces_ref, out_ref):
-    def turn(s, carry):
-        for k in range(3):
-            rows = jnp.concatenate([pieces_ref[c, 3 * s + k] for c in range(8)], axis=0)
-            out_ref[3 * s + k] = rows.T
-        return carry
-
-    lax.fori_loop(0, 9, turn, 0)
+def turn_kernel(place_ref, near_ref, q1_ref, q2_ref, q3_ref, straight_ref, out_ref):
+    def turn(t, carry):
+        at = pl.ds(pl.multiple_of(t * 32, 32), 32)
+        rows = jnp.concatenate([straight_ref[c, at, :] for c in range(8)], axis=0)
+        out_ref[t] = rows.T
+        return carry
+
+    lax.fori_loop(0, STRAIGHT, turn, 0)
+    for d, ref in enumerate((near_ref, q1_ref, q2_ref, q3_ref)):
+        first = STRAIGHT + QUARTER * lax.rem(place_ref[3] - d + 4, 4)
+        for k in range(QUARTER):
+            at = k * 32 + (VOL if d == 0 else 0)
+            rows = jnp.concatenate([ref[c, at : at + 32, :] for c in range(8)], axis=0)
+            out_ref[first + k] = rows.T
 
 
 def layers_kernel(
@@ -164,14 +183,8 @@
         g = dot_n(dt_ref[...], part.reshape(1024, 3 * C)).astype(BF)
         for tz in range(3):
             t = 3 * s + tz
-            tile = g[:, tz * C : (tz + 1) * C]
-            for h in range(2):
-                at = t * C + h * 128
-                at += SLOT - HALF if at >= HALF else 0
-                g_ref[at : at + 128, :] = tile[h * 128 : h * 128 + 128]
-    zero = jnp.zeros((SLOT - HALF, C), BF)
-    g_ref[HALF:SLOT, :] = zero
-    g_ref[SLOT + HALF : 2 * SLOT, :] = zero
+            g_ref[t * C : (t + 1) * C, :] = g[:, tz * C : (tz + 1) * C]
+    g_ref[27 * C : 28 * C, :] = jnp.zeros((C, C), BF)
     keep_ref[...] = g_ref[pl.ds(pl.multiple_of(core * SLOT, 16), SLOT), :]
     send_ref[...] = g_ref[pl.ds(pl.multiple_of((1 - core) * SLOT, 16), SLOT), :]
 
@@ -198,22 +211,28 @@
             out_ref[...] = (acc_ref[...] + part).astype(BF).reshape(BX, 64, C)
 
 
-def finish_kernel(place_ref, mine_ref, other_ref, out_ref, full_ref):
-    core = place_ref[2]
-
-    @pl.when(pl.program_id(0) == 0)
-    def _():
-        at = pl.multiple_of(core * HALF, 16)
-        full_ref[pl.ds(at, HALF), :] = mine_ref[0:HALF, :]
-        at = pl.multiple_of((1 - core) * HALF, 16)
-        full_ref[pl.ds(at, HALF), :] = other_ref[0:HALF, :]
-
-    row = lax.broadcasted_iota(jnp.int32, (C, C), 0)
-    col = lax.broadcasted_iota(jnp.int32, (C, C), 1)
-    unit = (row == col).astype(F32).astype(BF)
-    for k in range(3):
-        at = pl.multiple_of(pl.program_id(0) * 3 * C + k * C, C)
-        out_ref[k] = dot_t(unit, full_ref[pl.ds(at, C), :])
+def finish_kernel(own, place_ref, sums_ref, *refs):
+    out_ref, tile_ref, sems = refs[-3:]
+    half = place_ref[2] if own else 1 - place_ref[2]
+    count = TAPS - half
+
+    def copy(t):
+        return pltpu.make_async_copy(
+            tile_ref.at[t], out_ref.at[half * TAPS + t], sems.at[t]
+        )
+
+    def turn(t, carry):
+        at = pl.multiple_of(t * C, C)
+        tile_ref[t] = sums_ref[pl.ds(at, C), :].T.astype(F32)
+        copy(t).start()
+        return carry
+
+    def wait(t, carry):
+        copy(t).wait()
+        return carry
+
+    lax.fori_loop(0, count, turn, 0)
+    lax.fori_loop(0, count, wait, 0)
 
 
 def border(count):
@@ -223,69 +242,87 @@
 
 def local(volume, first_filters, second_filters, out_grad):
     chan, slab, core = (lax.axis_index(a) for a in ("chan", "slab", "core"))
-    place = jnp.stack([chan, slab * 2 + core, core]).astype(jnp.int32)
+    along_y = lax.rem(slab, 4)
+    place = jnp.stack([chan, slab * 2 + core, core, along_y]).astype(jnp.int32)
     swap = [(0, 1), (1, 0)]
     up, down = border(16)
     xup, xdown = border(8)
     space = ("slab", "core")
 
-    pick = np.zeros((176, 128), np.float32)
-    for c in range(8):
-        for j in range(22):
-            if 0 <= 16 * c - 3 + j < 128:
-                pick[c * 22 + j, 16 * c - 3 + j] = 1.0
     og = out_grad.reshape(BX, BY * NZ, C)
     gxl = lax.ppermute(og[BX - 1 :], "chan", xup)
     gxh = lax.ppermute(og[:1], "chan", xdown)
-    packed = pl.pallas_call(
+
+    packed, straight = pl.pallas_call(
         pack_kernel,
-        out_shape=jax.ShapeDtypeStruct((176 * 16, 128), BF),
-        in_specs=[VMEM, VMEM],
-        out_specs=VMEM,
-        scratch_shapes=[pltpu.VMEM((176 * 16, 128), F32)],
-        compiler_params=params(12),
+        out_shape=(
+            jax.ShapeDtypeStruct((8, VOL + QUARTER * 32, 128), BF),
+            jax.ShapeDtypeStruct((8, STRAIGHT * 32, 128), BF),
+        ),
+        in_specs=[SMEM, VMEM, VMEM],
+        out_specs=(VMEM, VMEM),
+        scratch_shapes=[pltpu.VMEM((2, 8 * 176, 128), F32)],
+        compiler_params=params(16),
         cost_estimate=cost(16 * 176 * 128 * 256, 3 << 20),
         name="pack",
-    )(jnp.asarray(pick, BF), jnp.transpose(volume, (1, 2, 3, 0)))
-    near = lax.all_to_all(packed.reshape(8, 352, 128), "chan", 0, 0, tiled=True)
-
-    w1 = jnp.transpose(first_filters, (0, 1, 2, 4, 3)).reshape(27, 32, C)
-    half = lax.dynamic_slice_in_dim(w1, core * 128, 128, axis=2)
-    spread = jnp.broadcast_to(half.reshape(1, 864, 128), (8, 864, 128))
-    spread, near = lax.optimization_barrier((spread, near))
-    pieces = lax.all_to_all(spread, "chan", 0, 0, tiled=True)
+    )(
+        place,
+        jnp.transpose(volume, (1, 2, 3, 0)),
+        jnp.transpose(first_filters, (0, 1, 2, 4, 3)).reshape(27, 32, C),
+    )
+    near = lax.all_to_all(packed, "chan", 0, 0, tiled=True)
+
+    w2 = second_filters.reshape(9, 3 * C, C)
+    near, gxl, gxh, straight = lax.optimization_barrier((near, gxl, gxh, straight))
+    straight = lax.all_to_all(straight, "chan", 0, 0, tiled=True)
+    quarters = [
+        lax.ppermute(
+            near[:, VOL:],
+            "slab",
+            [(z + y, z + (y + d) % 4) for z in (0, 4) for y in range(4)],
+        )
+        for d in range(1, 4)
+    ]
 
     top = jnp.concatenate([gxl[:, 56:], og[:, 56:], gxh[:, 56:]], axis=0)
     bottom = jnp.concatenate([gxl[:, :8], og[:, :8], gxh[:, :8]], axis=0)
     gyl = lax.ppermute(top, space, up)
     gyh = lax.ppermute(bottom, space, down)
-    near, gyl, gyh = lax.optimization_barrier((near, gyl, gyh))
-    near = near.reshape(8, 22, 16, 128)
-    low = lax.ppermute(near[:, :, 8:], space, up)
-    high = lax.ppermute(near[:, :, :8], space, down)
+    low = lax.ppermute(near[:, 176:VOL], space, up)
+    high = lax.ppermute(near[:, :176], space, down)
+    w2_back = pl.pallas_call(
+        flip_kernel,
+        out_shape=jax.ShapeDtypeStruct((9, 3 * C, C), BF),
+        in_specs=[VMEM],
+        out_specs=VMEM,
+        compiler_params=params(12),
+        cost_estimate=cost(1e9, 7 << 20),
+        name="flip",
+    )(w2)
+    w2_back, gyl, gyh, low, high, straight = lax.optimization_barrier(
+        (w2_back, gyl, gyh, low, high, straight)
+    )
     v3 = pl.pallas_call(
         unpack_kernel,
         out_shape=jax.ShapeDtypeStruct((22, 112, 3 * C), BF),
         in_specs=[SMEM, VMEM, VMEM, VMEM],
         out_specs=VMEM,
-        compiler_params=params(24),
+        compiler_params=params(16),
         cost_estimate=cost(1.5e9, 6 << 20),
         name="unpack",
     )(place, near, low, high)
-    v3, pieces = lax.optimization_barrier((v3, pieces))
 
     mine = pl.pallas_call(
         turn_kernel,
         out_shape=jax.ShapeDtypeStruct((27, 128, C), BF),
-        in_specs=[VMEM],
+        in_specs=[SMEM] + [VMEM] * 5,
         out_specs=VMEM,
         compiler_params=params(12),
         cost_estimate=cost(1e9, 4 << 20),
         name="turn",
-    )(pieces.reshape(8, 27, 32, 128))
+    )(place, near, *quarters, straight)
     other = lax.ppermute(mine, "core", swap)
 
-    w2 = second_filters.reshape(9, 3 * C, C)
     keep, send, d3 = pl.pallas_call(
         layers_kernel,
         out_shape=(
@@ -302,20 +339,11 @@
             pltpu.VMEM((C, 1024), BF),
             pltpu.VMEM((2 * SLOT, C), BF),
         ],
-        compiler_params=params(44),
+        compiler_params=params(30),
         cost_estimate=cost(16e9, 20 << 20),
         name="layers",
     )(place, v3, mine, other, w2, og, gxl, gxh, gyl, gyh)
 
-    w2_back = pl.pallas_call(
-        flip_kernel,
-        out_shape=jax.ShapeDtypeStruct((9, 3 * C, C), BF),
-        in_specs=[VMEM],
-        out_specs=VMEM,
-        compiler_params=params(12),
-        cost_estimate=cost(1e9, 7 << 20),
-        name="flip",
-    )(w2)
     received = lax.ppermute(send, "core", swap)
     act_grad = pl.pallas_call(
         back_kernel,
@@ -328,26 +356,31 @@
         name="back",
     )(d3, w2_back)
 
+    received, act_grad = lax.optimization_barrier((received, act_grad))
     both = (keep.astype(F32) + received.astype(F32)).astype(BF).reshape(64, 56, C)
     shares = lax.all_to_all(both, CHIPS, 0, 0, tiled=True)
-    shares, act_grad = lax.optimization_barrier((shares, act_grad))
     scale = 1.0 / math.sqrt(128 * 128 * NZ)
     share = (jnp.sum(shares.astype(F32), axis=0) * scale).astype(BF)
     spread = lax.optimization_barrier(jnp.broadcast_to(share[None], (64, 56, C)))
     ours = lax.all_to_all(spread, CHIPS, 0, 0, tiled=True).reshape(SLOT, C)
     theirs = lax.ppermute(ours, "core", swap)
-    whole = pl.BlockSpec((SLOT, C), lambda t: (0, 0))
-    filter_grad = pl.pallas_call(
-        finish_kernel,
-        grid=(9,),
-        out_shape=jax.ShapeDtypeStruct((27, C, C), F32),
-        in_specs=[SMEM, whole, whole],
-        out_specs=pl.BlockSpec((3, C, C), lambda t: (t, 0, 0)),
-        scratch_shapes=[pltpu.VMEM((2 * HALF, C), BF)],
-        compiler_params=params(20),
-        cost_estimate=cost(1e9, 11 << 20),
-        name="finish",
-    )(place, ours, theirs)
+    anywhere = pl.BlockSpec(memory_space=pl.ANY)
+
+    def finish(own, *operands):
+        return pl.pallas_call(
+            functools.partial(finish_kernel, own),
+            out_shape=jax.ShapeDtypeStruct((27, C, C), F32),
+            in_specs=[SMEM, VMEM] + [anywhere] * (len(operands) - 2),
+            out_specs=anywhere,
+            scratch_shapes=[pltpu.VMEM((TAPS, C, C), F32), pltpu.SemaphoreType.DMA((TAPS,))],
+            input_output_aliases={2: 0} if len(operands) > 2 else {},
+            compiler_params=params(12),
+            cost_estimate=cost(1e9, 5 << 20),
+            name="finish",
+        )(*operands)
+
+    filter_grad = finish(True, place, ours)
+    filter_grad = finish(False, place, theirs, filter_grad)
     return (
         act_grad.reshape(BX, BY, NZ, C),
         filter_grad.reshape(3, 3, 3, C, C),

time: 177 us -> 168 us (0.949)
  blocking collectives: 29.7 us -> 65.6 us
  waiting for transfers between devices: 40.6 us -> 14.8 us
  starting transfers between devices: 51.2 us -> 41.2 us
  Pallas kernels: 39.5 us -> 36.4 us
  other arithmetic: 3.66 us -> 0.89 us
  local copies, waits for them, and re-layouts: 10.3 us -> 8.08 us
    all_to_all x0 -> x1, blocking collectives: none -> 35.8 us  [local(): shares = lax.all_to_all(both, CHIPS, 0, 0, tiled=True)]
    all_to_all x3 -> x2, waiting for transfers between devices: 22.5 us -> 6.06 us  [the longest x1 6.06 us: local(): near = lax.all_to_all(packed, 'chan', 0, 0, tiled=True)]
    all_to_all x3 -> x2, starting transfers between devices: 28 us -> 13.3 us  [the longest x1 8.17 us: local(): near = lax.all_to_all(packed, 'chan', 0, 0, tiled=True)]
    ppermute x2 -> x5, starting transfers between devices: 5.55 us -> 10.4 us  [the longest x3 4.87 us: local(): lax.ppermute(near[:, VOL:], 'slab', [(z + y, z + (y + d) % 4) for z in (0...]
    ppermute x1, waiting for transfers between devices: 3.41 us -> 0.01 us  [local(): received = lax.ppermute(send, 'core', swap)]
    ppermute x1, waiting for transfers between devices: 3.39 us -> 0.01 us  [local(): gyh = lax.ppermute(bottom, space, down)]
    pallas_call x1, Pallas kernels: 21.4 us -> 18.8 us  [local(): pl.pallas_call(layers_kernel, out_shape=(jax.ShapeDtypeStruct((SLOT, C),...]
    ppermute x1, waiting for transfers between devices: 3.41 us -> 0.88 us  [local(): theirs = lax.ppermute(ours, 'core', swap)]
  transfers between devices with their start and end apart: 12 -> 14, of which waited for: 8 -> 6; matrix products, arithmetic and copies ran while one was open for 2% -> 0% of each run, Pallas kernels for 5% -> 6%
where the time goes in v2:
time: 168 us
  blocking collectives  65.6 us (39%)
  starting transfers between devices  41.2 us (25%)
  Pallas kernels  36.4 us (22%)
  waiting for transfers between devices  14.8 us (9%)
  local copies, waits for them, and re-layouts  8.08 us (5%)
    all_to_all x1, blocking collectives, local(): shares = lax.all_to_all(both, CHIPS, 0, 0, tiled=True)  35.8 us
    all_to_all x1, blocking collectives, local(): ours = lax.all_to_all(spread, CHIPS, 0, 0, tiled=True).reshape(SLOT, C)  29.7 us
    pallas_call x1, Pallas kernels, local(): pl.pallas_call(layers_kernel, out_shape=(jax.ShapeDtypeStruct((SLOT, C),...  18.8 us
    all_to_all x1, starting transfers between devices, local(): near = lax.all_to_all(packed, 'chan', 0, 0, tiled=True)  8.17 us
    unnamed x22, local copies, waits for them, and re-layouts  7.21 us
    all_to_all x1, waiting for transfers between devices, local(): near = lax.all_to_all(packed, 'chan', 0, 0, tiled=True)  6.06 us
    ppermute x1, starting transfers between devices, local(): gxl = lax.ppermute(og[BX - 1:], 'chan', xup)  5.49 us
    all_to_all x1, starting transfers between devices, local(): straight = lax.all_to_all(straight, 'chan', 0, 0, tiled=True)  5.13 us
  transfers between devices with their start and end apart: 14, of which 6 were waited for; matrix products, arithmetic and copies ran while one was open for 0% of the time, Pallas kernels for 6%

profile of v2, /device:TPU:1, one launch (start us, length us, event | category | flops | bytes accessed | tf_op | source)
XLA Modules:
  0.0 167.9 jit_solution(1296096556869965624)
XLA Ops:
  0.6 0.1 pad_add_fusion.place_ref
  0.7 0.0 copy-start.4
  0.7 1.0 copy-done.4
  1.8 0.0 copy-start.5
  1.8 1.0 copy-done.5
  2.8 0.0 copy-start.6
  2.8 2.4 %pack.1 = (bf16[8,448,128]{2,1,0:T(8,128)(2,1)}, bf16[8,480,128]{2,1,0:T(8,128)(2,1)}) custom-call(s32[4]{0:T(128)S(1)} %pad_add_fusion.place_ref, bf16[8,8,32,128]{3,2,1,0:T(8,128)(2,1)S(1)} %bitcast.22, bf16[27,32,256]{2,1,0:T(8,128)(2,1)S(1)} %bitcast.23), custom_call_target="tpu_custom_call" | custom-call | flops 92274688 | bytes 3145728 | tf_op jit(solution)/shard_map/pack/pallas_call | solution.py:256
  5.2 8.2 %all-to-all-start = ((bf16[8,448,128]{2,1,0:T(8,128)(2,1)}), bf16[8,448,128]{2,1,0:T(8,128)(2,1)S(1)}, u32[]{:S(2)}, u32[]{:S(2)}) async-start(bf16[8,448,128]{2,1,0:T(8,128)(2,1)} %get-tuple-element.19), calls=%async_computation | async-start | bytes 1835008 | tf_op jit(solution)/shard_map/all_to_all | solution.py:273
  13.4 0.0 copy-done.6
  13.4 1.3 collective-permute-start.1
  14.7 5.5 %collective-permute-start = (bf16[1,64,256]{2,1,0:T(8,128)(2,1)S(1)}, bf16[1,64,256]{2,1,0:T(8,128)(2,1)S(1)}, u32[]{:S(2)}, u32[]{:S(2)}) collective-permute-start(bf16[1,64,256]{2,1,0:T(8,128)(2,1)S(1)} %get-tuple-element.41), channel_id=1, source_target_pairs={{0,16},{16,32},{32,48},{48,64},{64,80},{80,96},{96,112},{1,17},{17... | collective-permute-start | bytes 98312 | tf_op jit(solution)/shard_map/ppermute | solution.py:253
  20.2 0.0 collective-permute-done.1.gxh_ref
  20.2 1.4 collective-permute-done.gxl_ref
  21.6 6.1 %all-to-all-done.near_ref = bf16[8,448,128]{2,1,0:T(8,128)(2,1)S(1)} async-done(((bf16[8,448,128]{2,1,0:T(8,128)(2,1)}), bf16[8,448,128]{2,1,0:T(8,128)(2,1)S(1)}, u32[]{:S(2)}, u32[]{:S(2)}) %all-to-all-start) | async-done | bytes 917536 | tf_op jit(solution)/shard_map/all_to_all | solution.py:273
  27.7 5.1 %all-to-all-start.1 = ((bf16[8,480,128]{2,1,0:T(8,128)(2,1)}), bf16[8,480,128]{2,1,0:T(8,128)(2,1)S(1)}, u32[]{:S(2)}, u32[]{:S(2)}) async-start(bf16[8,480,128]{2,1,0:T(8,128)(2,1)} %get-tuple-element.24), calls=%async_computation.1 | async-start | bytes 1966080 | tf_op jit(solution)/shard_map/all_to_all | solution.py:277
  32.8 4.2 %collective-permute-start.2 = (bf16[18,8,256]{2,1,0:T(8,128)(2,1)S(1)}, bf16[18,8,256]{2,1,0:T(8,128)(2,1)S(1)}, u32[]{:S(2)}, u32[]{:S(2)}) collective-permute-start(bf16[18,8,256]{2,1,0:T(8,128)(2,1)S(1)} %pad_maximum_fusion), channel_id=1, source_target_pairs={{0,1},{1,2},{2,3},{3,4},{4,5},{5,6},{6,7},{7,8},{8,9},{9,10},{10,1... | collective-permute-start | bytes 221192 | tf_op jit(solution)/shard_map/ppermute | solution.py:289
  37.1 1.9 %collective-permute-start.5 = (bf16[8,176,128]{2,1,0:T(8,128)(2,1)S(1)}, bf16[8,176,128]{2,1,0:T(8,128)(2,1)S(1)}, u32[]{:S(2)}, u32[]{:S(2)}) collective-permute-start(bf16[8,176,128]{2,1,0:T(8,128)(2,1)S(1)} %get-tuple-element.36), channel_id=1, source_target_pairs={{1,0},{2,1},{3,2},{4,3},{5,4},{6,5},{7,6},{8,7},{9,8},{10,9},{11,1... | collective-permute-start | bytes 1081352 | tf_op jit(solution)/shard_map/ppermute | solution.py:292
  39.0 3.6 %collective-permute-start.4 = (bf16[8,176,128]{2,1,0:T(8,128)(2,1)S(1)}, bf16[8,176,128]{2,1,0:T(8,128)(2,1)S(1)}, u32[]{:S(2)}, u32[]{:S(2)}) collective-permute-start(bf16[8,176,128]{2,1,0:T(8,128)(2,1)S(1)} %get-tuple-element.37), channel_id=1, source_target_pairs={{0,1},{1,2},{2,3},{3,4},{4,5},{5,6},{6,7},{7,8},{8,9},{9,10},{10,1... | collective-permute-start | bytes 1081352 | tf_op jit(solution)/shard_map/ppermute | solution.py:291
  42.7 1.9 %collective-permute-start.3 = (bf16[18,8,256]{2,1,0:T(8,128)(2,1)S(1)}, bf16[18,8,256]{2,1,0:T(8,128)(2,1)S(1)}, u32[]{:S(2)}, u32[]{:S(2)}) collective-permute-start(bf16[18,8,256]{2,1,0:T(8,128)(2,1)S(1)} %pad_maximum_fusion.1), channel_id=1, source_target_pairs={{1,0},{2,1},{3,2},{4,3},{5,4},{6,5},{7,6},{8,7},{9,8},{10,9},{11,1... | collective-permute-start | bytes 221192 | tf_op jit(solution)/shard_map/ppermute | solution.py:290
  44.6 0.7 slice.53
  45.3 3.9 %collective-permute-start.8 = (bf16[8,96,128]{2,1,0:T(8,128)(2,1)}, bf16[8,96,128]{2,1,0:T(8,128)(2,1)S(1)}, u32[]{:S(2)}, u32[]{:S(2)}) collective-permute-start(bf16[8,96,128]{2,1,0:T(8,128)(2,1)} %slice.53), channel_id=1, source_target_pairs={{0,6},{2,0},{4,2},{6,4},{8,14},{10,8},{12,10},{14,12},{1,7},{3,1},... | collective-permute-start | bytes 589832 | tf_op jit(solution)/shard_map/ppermute | solution.py:279
  49.2 0.0 collective-permute-done.2.gyl_ref
  49.2 0.0 collective-permute-start.7
  49.2 0.0 collective-permute-done.3.gyh_ref
  49.2 0.0 copy-start.9
  49.3 0.6 copy-done.9
  49.9 0.9 collective-permute-start.6
  50.8 0.0 copy-start
  50.8 2.0 %copy-done = bf16[3,3,3,256,256]{4,3,2,1,0:T(8,128)(2,1)S(1)} copy-done((bf16[3,3,3,256,256]{4,3,2,1,0:T(8,128)(2,1)S(1)}, bf16[3,3,3,256,256]{4,3,2,1,0:T(8,128)(2,1)}, u32[]{:S(2)}) %copy-start) | copy-done | bytes 3538968
  52.8 1.4 flip.1.w2_ref
  54.2 0.0 copy-start.2
  54.2 1.8 %copy-done.2 = bf16[9,768,256]{2,1,0:T(8,128)(2,1)} copy-done((bf16[9,768,256]{2,1,0:T(8,128)(2,1)}, bf16[9,768,256]{2,1,0:T(8,128)(2,1)S(1)}, u32[]{:S(2)}) %copy-start.2) | copy-done | bytes 3538968
  56.0 0.0 collective-permute-done.5.high_ref
  56.0 0.0 collective-permute-done.4.low_ref
  56.0 0.0 copy-start.7
  56.0 0.7 copy-done.7
  56.8 0.0 all-to-all-done.1.straight_ref
  56.8 1.5 collective-permute-done.8.q3_ref
  58.3 0.0 collective-permute-done.7.q2_ref
  58.3 3.5 %collective-permute-done.6.q1_ref = bf16[8,96,128]{2,1,0:T(8,128)(2,1)S(1)} collective-permute-done((bf16[8,96,128]{2,1,0:T(8,128)(2,1)}, bf16[8,96,128]{2,1,0:T(8,128)(2,1)S(1)}, u32[]{:S(2)}, u32[]{:S(2)}) %collective-permute-start.6) | collective-permute-done | bytes 196640 | tf_op jit(solution)/shard_map/ppermute | solution.py:279
  61.8 1.8 %turn.1.mine_ref = bf16[27,128,256]{2,1,0:T(8,128)(2,1)S(1)} custom-call(s32[4]{0:T(128)S(1)} %pad_add_fusion.place_ref, bf16[8,448,128]{2,1,0:T(8,128)(2,1)S(1)} %all-to-all-done.near_ref, bf16[8,96,128]{2,1,0:T(8,128)(2,1)S(1)} %collective-permute-done.6.q1_ref, bf16[8,96,128]{2,1,0:T(8,128)(2,1)S(1)} %collective-permute-done.7.q2_ref, ...), custom_call_target="tpu_custom_call" | custom-call | flops 1000000000 | bytes 4194304 | tf_op jit(solution)/shard_map/turn/pallas_call | solution.py:315
  63.6 0.0 copy-start.1
  63.6 0.0 copy-start.10
  63.6 0.1 collective-permute-start.9
  63.7 0.0 copy-done.8
  63.7 2.2 %unpack.1.v3_ref = bf16[22,112,768]{2,1,0:T(8,128)(2,1)S(1)} custom-call(s32[4]{0:T(128)S(1)} %pad_add_fusion.place_ref, bf16[8,448,128]{2,1,0:T(8,128)(2,1)S(1)} %all-to-all-done.near_ref, bf16[8,176,128]{2,1,0:T(8,128)(2,1)S(1)} %copy-done.8, bf16[8,176,128]{2,1,0:T(8,128)(2,1)S(1)} %collective-permute-done.5.high_ref), custom_call_target="tpu_custom_call" | custom-call | flops 1500000000 | bytes 6291456 | tf_op jit(solution)/shard_map/unpack/pallas_call | solution.py:305
  66.0 0.0 copy-start.3
  66.0 1.4 collective-permute-done.9.other_ref
  67.4 0.0 copy-done.1
  67.4 0.0 copy-done.10
  67.4 18.8 %layers.1 = (bf16[3584,256]{1,0:T(8,128)(2,1)S(1)}, bf16[3584,256]{1,0:T(8,128)(2,1)S(1)}, bf16[18,80,768]{2,1,0:T(8,128)(2,1)S(1)}) custom-call(s32[4]{0:T(128)S(1)} %pad_add_fusion.place_ref, bf16[22,112,768]{2,1,0:T(8,128)(2,1)S(1)} %unpack.1.v3_ref, bf16[27,128,256]{2,1,0:T(8,128)(2,1)S(1)} %turn.1.mine_ref, ...), custom_call_target="tpu_custom_call" | custom-call | flops 16000000000 | bytes 20971520 | tf_op jit(solution)/shard_map/layers/pallas_call | solution.py:326
  86.2 0.4 collective-permute-start.10
  86.6 0.0 copy-done.3
  86.6 4.6 %back.1 = bf16[16,64,256]{2,1,0:T(8,128)(2,1)} custom-call(bf16[18,80,768]{2,1,0:T(8,128)(2,1)S(1)} %get-tuple-element.31.d3_ref, bf16[9,768,256]{2,1,0:T(8,128)(2,1)S(1)} %copy-done.3), custom_call_target="tpu_custom_call" | custom-call | flops 3600000000 | bytes 7340032 | tf_op jit(solution)/shard_map/back/pallas_call | solution.py:348
  91.2 0.0 collective-permute-done.10
  91.2 0.5 add_convert_fusion
  91.7 35.8 %all_to_all.20 = bf16[64,56,256]{2,1,0:T(8,128)(2,1)S(1)} all-to-all(bf16[64,56,256]{2,1,0:T(8,128)(2,1)S(1)} %bitcast.27), channel_id=1, replica_groups=mesh['chan'=8,'slab'=8,'core'=2] {'chan','slab'}, dimensions={0} | all-to-all | bytes 3670016 | tf_op jit(solution)/shard_map/all_to_all | solution.py:361
  127.6 0.3 convert_reduce_fusion
  127.8 0.1 broadcast_in_dim.2
  128.0 29.7 %all_to_all.21 = bf16[64,56,256]{2,1,0:T(8,128)(2,1)S(1)} all-to-all(bf16[64,56,256]{2,1,0:T(8,128)(2,1)S(1)} %broadcast_in_dim.2), channel_id=1, replica_groups=mesh['chan'=8,'slab'=8,'core'=2] {'chan','slab'}, dimensions={0} | all-to-all | bytes 3670016 | tf_op jit(solution)/shard_map/all_to_all | solution.py:365
  157.7 4.0 %collective-permute-start.11 = (bf16[3584,256]{1,0:T(8,128)(2,1)S(1)}, bf16[3584,256]{1,0:T(8,128)(2,1)S(1)}, u32[]{:S(2)}, u32[]{:S(2)}) collective-permute-start(bf16[3584,256]{1,0:T(8,128)(2,1)S(1)} %bitcast.18), channel_id=1, source_target_pairs={{0,1},{1,0},{2,3},{3,2},{4,5},{5,4},{6,7},{7,6},{8,9},{9,8},{10,11... | collective-permute-start | bytes 5505032 | tf_op jit(solution)/shard_map/ppermute | solution.py:366
  161.8 2.5 %finish.2.refs_0_ = f32[27,256,256]{2,1,0:T(8,128)} custom-call(s32[4]{0:T(128)S(1)} %pad_add_fusion.place_ref, bf16[3584,256]{1,0:T(8,128)(2,1)S(1)} %bitcast.19), custom_call_target="tpu_custom_call" | custom-call | flops 1000000000 | bytes 5242880 | tf_op jit(solution)/shard_map/finish/pallas_call | solution.py:370
  164.3 0.9 collective-permute-done.11.sums_ref
  165.2 2.6 %finish.3 = f32[27,256,256]{2,1,0:T(8,128)} custom-call(s32[4]{0:T(128)S(1)} %pad_add_fusion.place_ref, bf16[3584,256]{1,0:T(8,128)(2,1)S(1)} %collective-permute-done.11.sums_ref, f32[27,256,256]{2,1,0:T(8,128)} %finish.2.refs_0_), custom_call_target="tpu_custom_call", output_to_operand_aliasing={{}: (2, {})} | custom-call | flops 1000000000 | bytes 5242880 | tf_op jit(solution)/shard_map/finish/pallas_call | solution.py:370
  (8 shorter events, 0.1 us)
Async XLA Ops:
  0.7 1.0 copy-start.4
  1.8 1.0 copy-start.5
  2.8 10.6 %copy-start.6 = (bf16[16,8,8,256]{3,2,1,0:T(8,128)(2,1)S(1)}, bf16[16,8,8,256]{3,2,1,0:T(8,128)(2,1)}, u32[]{:S(2)}) copy-start(bf16[16,8,8,256]{3,2,1,0:T(8,128)(2,1)} %param.7) | copy-start | bytes 1572868
  5.2 22.5 %all-to-all-start = ((bf16[8,448,128]{2,1,0:T(8,128)(2,1)}), bf16[8,448,128]{2,1,0:T(8,128)(2,1)S(1)}, u32[]{:S(2)}, u32[]{:S(2)}) async-start(bf16[8,448,128]{2,1,0:T(8,128)(2,1)} %get-tuple-element.19), calls=%async_computation | async-start | bytes 1835008 | tf_op jit(solution)/shard_map/all_to_all | solution.py:273
  13.4 6.8 %collective-permute-start.1 = (bf16[1,64,256]{2,1,0:T(8,128)(2,1)S(1)}, bf16[1,64,256]{2,1,0:T(8,128)(2,1)S(1)}, u32[]{:S(2)}, u32[]{:S(2)}) collective-permute-start(bf16[1,64,256]{2,1,0:T(8,128)(2,1)S(1)} %get-tuple-element.40), channel_id=1, source_target_pairs={{16,0},{32,16},{48,32},{64,48},{80,64},{96,80},{112,96},{17,1},{33... | collective-permute-start | bytes 98312 | tf_op jit(solution)/shard_map/ppermute | solution.py:254
  14.7 6.9 %collective-permute-start = (bf16[1,64,256]{2,1,0:T(8,128)(2,1)S(1)}, bf16[1,64,256]{2,1,0:T(8,128)(2,1)S(1)}, u32[]{:S(2)}, u32[]{:S(2)}) collective-permute-start(bf16[1,64,256]{2,1,0:T(8,128)(2,1)S(1)} %get-tuple-element.41), channel_id=1, source_target_pairs={{0,16},{16,32},{32,48},{48,64},{64,80},{80,96},{96,112},{1,17},{17... | collective-permute-start | bytes 98312 | tf_op jit(solution)/shard_map/ppermute | solution.py:253
  27.7 29.1 %all-to-all-start.1 = ((bf16[8,480,128]{2,1,0:T(8,128)(2,1)}), bf16[8,480,128]{2,1,0:T(8,128)(2,1)S(1)}, u32[]{:S(2)}, u32[]{:S(2)}) async-start(bf16[8,480,128]{2,1,0:T(8,128)(2,1)} %get-tuple-element.24), calls=%async_computation.1 | async-start | bytes 1966080 | tf_op jit(solution)/shard_map/all_to_all | solution.py:277
  32.8 16.4 %collective-permute-start.2 = (bf16[18,8,256]{2,1,0:T(8,128)(2,1)S(1)}, bf16[18,8,256]{2,1,0:T(8,128)(2,1)S(1)}, u32[]{:S(2)}, u32[]{:S(2)}) collective-permute-start(bf16[18,8,256]{2,1,0:T(8,128)(2,1)S(1)} %pad_maximum_fusion), channel_id=1, source_target_pairs={{0,1},{1,2},{2,3},{3,4},{4,5},{5,6},{6,7},{7,8},{8,9},{9,10},{10,1... | collective-permute-start | bytes 221192 | tf_op jit(solution)/shard_map/ppermute | solution.py:289
  37.1 18.9 %collective-permute-start.5 = (bf16[8,176,128]{2,1,0:T(8,128)(2,1)S(1)}, bf16[8,176,128]{2,1,0:T(8,128)(2,1)S(1)}, u32[]{:S(2)}, u32[]{:S(2)}) collective-permute-start(bf16[8,176,128]{2,1,0:T(8,128)(2,1)S(1)} %get-tuple-element.36), channel_id=1, source_target_pairs={{1,0},{2,1},{3,2},{4,3},{5,4},{6,5},{7,6},{8,7},{9,8},{10,9},{11,1... | collective-permute-start | bytes 1081352 | tf_op jit(solution)/shard_map/ppermute | solution.py:292
  39.0 17.0 %collective-permute-start.4 = (bf16[8,176,128]{2,1,0:T(8,128)(2,1)S(1)}, bf16[8,176,128]{2,1,0:T(8,128)(2,1)S(1)}, u32[]{:S(2)}, u32[]{:S(2)}) collective-permute-start(bf16[8,176,128]{2,1,0:T(8,128)(2,1)S(1)} %get-tuple-element.37), channel_id=1, source_target_pairs={{0,1},{1,2},{2,3},{3,4},{4,5},{5,6},{6,7},{7,8},{8,9},{9,10},{10,1... | collective-permute-start | bytes 1081352 | tf_op jit(solution)/shard_map/ppermute | solution.py:291
  42.7 6.6 %collective-permute-start.3 = (bf16[18,8,256]{2,1,0:T(8,128)(2,1)S(1)}, bf16[18,8,256]{2,1,0:T(8,128)(2,1)S(1)}, u32[]{:S(2)}, u32[]{:S(2)}) collective-permute-start(bf16[18,8,256]{2,1,0:T(8,128)(2,1)S(1)} %pad_maximum_fusion.1), channel_id=1, source_target_pairs={{1,0},{2,1},{3,2},{4,3},{5,4},{6,5},{7,6},{8,7},{9,8},{10,9},{11,1... | collective-permute-start | bytes 221192 | tf_op jit(solution)/shard_map/ppermute | solution.py:290
  45.3 13.0 %collective-permute-start.8 = (bf16[8,96,128]{2,1,0:T(8,128)(2,1)}, bf16[8,96,128]{2,1,0:T(8,128)(2,1)S(1)}, u32[]{:S(2)}, u32[]{:S(2)}) collective-permute-start(bf16[8,96,128]{2,1,0:T(8,128)(2,1)} %slice.53), channel_id=1, source_target_pairs={{0,6},{2,0},{4,2},{6,4},{8,14},{10,8},{12,10},{14,12},{1,7},{3,1},... | collective-permute-start | bytes 589832 | tf_op jit(solution)/shard_map/ppermute | solution.py:279
  49.2 9.1 %collective-permute-start.7 = (bf16[8,96,128]{2,1,0:T(8,128)(2,1)}, bf16[8,96,128]{2,1,0:T(8,128)(2,1)S(1)}, u32[]{:S(2)}, u32[]{:S(2)}) collective-permute-start(bf16[8,96,128]{2,1,0:T(8,128)(2,1)} %slice.53), channel_id=1, source_target_pairs={{0,4},{2,6},{4,0},{6,2},{8,12},{10,14},{12,8},{14,10},{1,5},{3,7},... | collective-permute-start | bytes 589832 | tf_op jit(solution)/shard_map/ppermute | solution.py:279
  49.2 0.6 copy-start.9
  49.9 11.9 %collective-permute-start.6 = (bf16[8,96,128]{2,1,0:T(8,128)(2,1)}, bf16[8,96,128]{2,1,0:T(8,128)(2,1)S(1)}, u32[]{:S(2)}, u32[]{:S(2)}) collective-permute-start(bf16[8,96,128]{2,1,0:T(8,128)(2,1)} %slice.53), channel_id=1, source_target_pairs={{0,2},{2,4},{4,6},{6,0},{8,10},{10,12},{12,14},{14,8},{1,3},{3,5},... | collective-permute-start | bytes 589832 | tf_op jit(solution)/shard_map/ppermute | solution.py:279
  50.8 2.0 %copy-start = (bf16[3,3,3,256,256]{4,3,2,1,0:T(8,128)(2,1)S(1)}, bf16[3,3,3,256,256]{4,3,2,1,0:T(8,128)(2,1)}, u32[]{:S(2)}) copy-start(bf16[3,3,3,256,256]{4,3,2,1,0:T(8,128)(2,1)} %param.6) | copy-start | bytes 10616836
  54.2 1.8 %copy-start.2 = (bf16[9,768,256]{2,1,0:T(8,128)(2,1)}, bf16[9,768,256]{2,1,0:T(8,128)(2,1)S(1)}, u32[]{:S(2)}) copy-start(bf16[9,768,256]{2,1,0:T(8,128)(2,1)S(1)} %flip.1.w2_ref) | copy-start | bytes 10616836
  56.0 0.7 copy-start.7
  56.8 7.0 %copy-start.8 = (bf16[8,176,128]{2,1,0:T(8,128)(2,1)S(1)}, bf16[8,176,128]{2,1,0:T(8,128)(2,1)}, u32[]{:S(2)}) copy-start(bf16[8,176,128]{2,1,0:T(8,128)(2,1)} %copy-done.7) | copy-start | bytes 1081348
  63.6 3.8 %copy-start.1 = (bf16[3,3,3,256,256]{4,3,2,1,0:T(8,128)(2,1)S(1)}, bf16[3,3,3,256,256]{4,3,2,1,0:T(8,128)(2,1)}, u32[]{:S(2)}) copy-start(bf16[3,3,3,256,256]{4,3,2,1,0:T(8,128)(2,1)} %param.6) | copy-start | bytes 10616836
  63.6 3.8 %copy-start.10 = (bf16[18,8,256]{2,1,0:T(8,128)(2,1)S(1)}, bf16[18,8,256]{2,1,0:T(8,128)(2,1)}, u32[]{:S(2)}) copy-start(bf16[18,8,256]{2,1,0:T(8,128)(2,1)} %copy-done.9) | copy-start | bytes 221188
  63.6 3.8 %collective-permute-start.9 = (bf16[27,128,256]{2,1,0:T(8,128)(2,1)S(1)}, bf16[27,128,256]{2,1,0:T(8,128)(2,1)S(1)}, u32[]{:S(2)}, u32[]{:S(2)}) collective-permute-start(bf16[27,128,256]{2,1,0:T(8,128)(2,1)S(1)} %turn.1.mine_ref), channel_id=1, source_target_pairs={{0,1},{1,0},{2,3},{3,2},{4,5},{5,4},{6,7},{7,6},{8,9},{9,8},{10,11... | collective-permute-start | bytes 5308424 | tf_op jit(solution)/shard_map/ppermute | solution.py:324
  66.0 20.7 %copy-start.3 = (bf16[9,768,256]{2,1,0:T(8,128)(2,1)S(1)}, bf16[9,768,256]{2,1,0:T(8,128)(2,1)}, u32[]{:S(2)}) copy-start(bf16[9,768,256]{2,1,0:T(8,128)(2,1)} %copy-done.2) | copy-start | bytes 10616836
  86.2 5.0 %collective-permute-start.10 = (bf16[3584,256]{1,0:T(8,128)(2,1)S(1)}, bf16[3584,256]{1,0:T(8,128)(2,1)S(1)}, u32[]{:S(2)}, u32[]{:S(2)}) collective-permute-start(bf16[3584,256]{1,0:T(8,128)(2,1)S(1)} %get-tuple-element.30), channel_id=1, source_target_pairs={{0,1},{1,0},{2,3},{3,2},{4,5},{5,4},{6,7},{7,6},{8,9},{9,8},{10,11... | collective-permute-start | bytes 5505032 | tf_op jit(solution)/shard_map/ppermute | solution.py:347
  157.7 7.4 %collective-permute-start.11 = (bf16[3584,256]{1,0:T(8,128)(2,1)S(1)}, bf16[3584,256]{1,0:T(8,128)(2,1)S(1)}, u32[]{:S(2)}, u32[]{:S(2)}) collective-permute-start(bf16[3584,256]{1,0:T(8,128)(2,1)S(1)} %bitcast.18), channel_id=1, source_target_pairs={{0,1},{1,0},{2,3},{3,2},{4,5},{5,4},{6,7},{7,6},{8,9},{9,8},{10,11... | collective-permute-start | bytes 5505032 | tf_op jit(solution)/shard_map/ppermute | solution.py:366

commit v3 on v2

--- a/solution.py
+++ b/solution.py
@@ -273,7 +273,18 @@
     near = lax.all_to_all(packed, "chan", 0, 0, tiled=True)
 
     w2 = second_filters.reshape(9, 3 * C, C)
-    near, gxl, gxh, straight = lax.optimization_barrier((near, gxl, gxh, straight))
+    w2_back = pl.pallas_call(
+        flip_kernel,
+        out_shape=jax.ShapeDtypeStruct((9, 3 * C, C), BF),
+        in_specs=[VMEM],
+        out_specs=VMEM,
+        compiler_params=params(12),
+        cost_estimate=cost(1e9, 7 << 20),
+        name="flip",
+    )(w2)
+    near, gxl, gxh, straight, w2_back = lax.optimization_barrier(
+        (near, gxl, gxh, straight, w2_back)
+    )
     straight = lax.all_to_all(straight, "chan", 0, 0, tiled=True)
     quarters = [
         lax.ppermute(
@@ -284,24 +295,15 @@
         for d in range(1, 4)
     ]
 
+    low = lax.ppermute(near[:, 176:VOL], space, up)
+    high = lax.ppermute(near[:, :176], space, down)
+    low, high, gxl, gxh = lax.optimization_barrier((low, high, gxl, gxh))
+
     top = jnp.concatenate([gxl[:, 56:], og[:, 56:], gxh[:, 56:]], axis=0)
     bottom = jnp.concatenate([gxl[:, :8], og[:, :8], gxh[:, :8]], axis=0)
     gyl = lax.ppermute(top, space, up)
     gyh = lax.ppermute(bottom, space, down)
-    low = lax.ppermute(near[:, 176:VOL], space, up)
-    high = lax.ppermute(near[:, :176], space, down)
-    w2_back = pl.pallas_call(
-        flip_kernel,
-        out_shape=jax.ShapeDtypeStruct((9, 3 * C, C), BF),
-        in_specs=[VMEM],
-        out_specs=VMEM,
-        compiler_params=params(12),
-        cost_estimate=cost(1e9, 7 << 20),
-        name="flip",
-    )(w2)
-    w2_back, gyl, gyh, low, high, straight = lax.optimization_barrier(
-        (w2_back, gyl, gyh, low, high, straight)
-    )
+    gyl, gyh, low, high, straight = lax.optimization_barrier((gyl, gyh, low, high, straight))
     v3 = pl.pallas_call(
         unpack_kernel,
         out_shape=jax.ShapeDtypeStruct((22, 112, 3 * C), BF),

time: 168 us -> 164 us (0.976)
  waiting for transfers between devices: 14.8 us -> 10.6 us
  blocking collectives: 65.6 us -> 62.9 us
    ppermute x3, waiting for transfers between devices: 5.03 us -> 0.01 us  [local(): lax.ppermute(near[:, VOL:], 'slab', [(z + y, z + (y + d) % 4) for z in (0...]
    ppermute x1, waiting for transfers between devices: 0.01 us -> 3.8 us  [local(): gyl = lax.ppermute(top, space, up)]
    all_to_all x1, waiting for transfers between devices: 6.06 us -> 2.27 us  [local(): near = lax.all_to_all(packed, 'chan', 0, 0, tiled=True)]
    all_to_all x1, waiting for transfers between devices: 0.01 us -> 2.77 us  [local(): straight = lax.all_to_all(straight, 'chan', 0, 0, tiled=True)]
    all_to_all x1, blocking collectives: 35.8 us -> 33.2 us  [local(): shares = lax.all_to_all(both, CHIPS, 0, 0, tiled=True)]
    unnamed x22 -> x18, local copies, waits for them, and re-layouts: 7.21 us -> 6.49 us
  transfers between devices with their start and end apart: 14 -> 14, of which waited for: 6 -> 6; matrix products, arithmetic and copies ran while one was open for 0% -> 0% of each run, Pallas kernels for 6% -> 7%
where the time goes in v3:
time: 164 us; the launch traced here: 163 us
  blocking collectives  62.9 us (38%)
  starting transfers between devices  42.5 us (26%)
  Pallas kernels  36.8 us (22%)
  waiting for transfers between devices  10.6 us (6%)
  local copies, waits for them, and re-layouts  8.23 us (5%)
    all_to_all x1, blocking collectives, local(): shares = lax.all_to_all(both, CHIPS, 0, 0, tiled=True)  33.2 us
    all_to_all x1, blocking collectives, local(): ours = lax.all_to_all(spread, CHIPS, 0, 0, tiled=True).reshape(SLOT, C)  29.7 us
    pallas_call x1, Pallas kernels, local(): pl.pallas_call(layers_kernel, out_shape=(jax.ShapeDtypeStruct((SLOT, C),...  18.8 us
    all_to_all x1, starting transfers between devices, local(): near = lax.all_to_all(packed, 'chan', 0, 0, tiled=True)  8.17 us
    unnamed x18, local copies, waits for them, and re-layouts  6.49 us
    all_to_all x1, starting transfers between devices, local(): straight = lax.all_to_all(straight, 'chan', 0, 0, tiled=True)  5.85 us
    ppermute x1, starting transfers between devices, local(): gxl = lax.ppermute(og[BX - 1:], 'chan', xup)  5.49 us
    pallas_call x2, Pallas kernels, finish(): pl.pallas_call(functools.partial(finish_kernel, own), out_shape=jax.Shape...  5.13 us
  transfers between devices with their start and end apart: 14, of which 6 were waited for; matrix products, arithmetic and copies ran while one was open for 0% of the time, Pallas kernels for 7%

profile of v3, /device:TPU:1, one launch (start us, length us, event | category | flops | bytes accessed | tf_op | source)
XLA Modules:
  0.0 163.0 jit_solution(3131041576861486653)
XLA Ops:
  0.6 0.1 pad_add_fusion.place_ref
  0.7 0.0 copy-start.4
  0.7 1.0 copy-done.4
  1.8 0.0 copy-start.5
  1.8 1.0 copy-done.5
  2.8 0.0 copy-start.6
  2.8 2.5 %pack.1 = (bf16[8,448,128]{2,1,0:T(8,128)(2,1)}, bf16[8,480,128]{2,1,0:T(8,128)(2,1)}) custom-call(s32[4]{0:T(128)S(1)} %pad_add_fusion.place_ref, bf16[8,8,32,128]{3,2,1,0:T(8,128)(2,1)S(1)} %bitcast.22, bf16[27,32,256]{2,1,0:T(8,128)(2,1)S(1)} %bitcast.23), custom_call_target="tpu_custom_call" | custom-call | flops 92274688 | bytes 3145728 | tf_op jit(solution)/shard_map/pack/pallas_call | solution.py:256
  5.2 8.2 %all-to-all-start = ((bf16[8,448,128]{2,1,0:T(8,128)(2,1)}), bf16[8,448,128]{2,1,0:T(8,128)(2,1)S(1)}, u32[]{:S(2)}, u32[]{:S(2)}) async-start(bf16[8,448,128]{2,1,0:T(8,128)(2,1)} %get-tuple-element.23), calls=%async_computation | async-start | bytes 1835008 | tf_op jit(solution)/shard_map/all_to_all | solution.py:273
  13.4 0.0 copy-done.6
  13.4 1.3 collective-permute-start.1
  14.7 5.5 %collective-permute-start = (bf16[1,64,256]{2,1,0:T(8,128)(2,1)S(1)}, bf16[1,64,256]{2,1,0:T(8,128)(2,1)S(1)}, u32[]{:S(2)}, u32[]{:S(2)}) collective-permute-start(bf16[1,64,256]{2,1,0:T(8,128)(2,1)S(1)} %get-tuple-element.49), channel_id=1, source_target_pairs={{0,16},{16,32},{32,48},{48,64},{64,80},{80,96},{96,112},{1,17},{17... | collective-permute-start | bytes 98312 | tf_op jit(solution)/shard_map/ppermute | solution.py:253
  20.2 0.0 copy-start
  20.2 2.0 %copy-done = bf16[3,3,3,256,256]{4,3,2,1,0:T(8,128)(2,1)S(1)} copy-done((bf16[3,3,3,256,256]{4,3,2,1,0:T(8,128)(2,1)S(1)}, bf16[3,3,3,256,256]{4,3,2,1,0:T(8,128)(2,1)}, u32[]{:S(2)}) %copy-start) | copy-done | bytes 3538968
  22.2 1.4 flip.1.w2_ref
  23.6 0.0 copy-start.2
  23.6 1.8 %copy-done.2 = bf16[9,768,256]{2,1,0:T(8,128)(2,1)} copy-done((bf16[9,768,256]{2,1,0:T(8,128)(2,1)}, bf16[9,768,256]{2,1,0:T(8,128)(2,1)S(1)}, u32[]{:S(2)}) %copy-start.2) | copy-done | bytes 3538968
  25.4 0.0 collective-permute-done.1.gxh_ref
  25.4 0.0 collective-permute-done.gxl_ref
  25.4 2.3 %all-to-all-done.near_ref = bf16[8,448,128]{2,1,0:T(8,128)(2,1)S(1)} async-done(((bf16[8,448,128]{2,1,0:T(8,128)(2,1)}), bf16[8,448,128]{2,1,0:T(8,128)(2,1)S(1)}, u32[]{:S(2)}, u32[]{:S(2)}) %all-to-all-start) | async-done | bytes 917536 | tf_op jit(solution)/shard_map/all_to_all | solution.py:273
  27.7 0.9 fusion
  28.6 3.1 %collective-permute-start.3 = (bf16[8,176,128]{2,1,0:T(8,128)(2,1)}, bf16[8,176,128]{2,1,0:T(8,128)(2,1)S(1)}, u32[]{:S(2)}, u32[]{:S(2)}) collective-permute-start(bf16[8,176,128]{2,1,0:T(8,128)(2,1)} %get-tuple-element.44), channel_id=1, source_target_pairs={{1,0},{2,1},{3,2},{4,3},{5,4},{6,5},{7,6},{8,7},{9,8},{10,9},{11,1... | collective-permute-start | bytes 1081352 | tf_op jit(solution)/shard_map/ppermute | solution.py:299
  31.7 3.1 %collective-permute-start.2 = (bf16[8,176,128]{2,1,0:T(8,128)(2,1)}, bf16[8,176,128]{2,1,0:T(8,128)(2,1)}, u32[]{:S(2)}, u32[]{:S(2)}) collective-permute-start(bf16[8,176,128]{2,1,0:T(8,128)(2,1)} %get-tuple-element.45), channel_id=1, source_target_pairs={{0,1},{1,2},{2,3},{3,4},{4,5},{5,6},{6,7},{7,8},{8,9},{9,10},{10,1... | collective-permute-start | bytes 1081352 | tf_op jit(solution)/shard_map/ppermute | solution.py:298
  34.8 5.8 %all-to-all-start.1 = ((bf16[8,480,128]{2,1,0:T(8,128)(2,1)}), bf16[8,480,128]{2,1,0:T(8,128)(2,1)S(1)}, u32[]{:S(2)}, u32[]{:S(2)}) async-start(bf16[8,480,128]{2,1,0:T(8,128)(2,1)} %get-tuple-element.32), calls=%async_computation.1 | async-start | bytes 1966080 | tf_op jit(solution)/shard_map/all_to_all | solution.py:288
  40.7 0.7 slice.53
  41.4 3.6 %collective-permute-start.8 = (bf16[8,96,128]{2,1,0:T(8,128)(2,1)}, bf16[8,96,128]{2,1,0:T(8,128)(2,1)S(1)}, u32[]{:S(2)}, u32[]{:S(2)}) collective-permute-start(bf16[8,96,128]{2,1,0:T(8,128)(2,1)} %slice.53), channel_id=1, source_target_pairs={{0,6},{2,0},{4,2},{6,4},{8,14},{10,8},{12,10},{14,12},{1,7},{3,1},... | collective-permute-start | bytes 589832 | tf_op jit(solution)/shard_map/ppermute | solution.py:290
  45.0 0.0 collective-permute-start.7
  45.0 0.6 collective-permute-start.6
  45.6 0.0 collective-permute-done.3.high_ref
  45.6 0.0 collective-permute-done.2.low_ref
  45.6 3.4 %collective-permute-start.4 = (bf16[18,8,256]{2,1,0:T(8,128)(2,1)S(1)}, bf16[18,8,256]{2,1,0:T(8,128)(2,1)S(1)}, u32[]{:S(2)}, u32[]{:S(2)}) collective-permute-start(bf16[18,8,256]{2,1,0:T(8,128)(2,1)S(1)} %pad_maximum_fusion), channel_id=1, source_target_pairs={{0,1},{1,2},{2,3},{3,4},{4,5},{5,6},{6,7},{7,8},{8,9},{9,10},{10,1... | collective-permute-start | bytes 221192 | tf_op jit(solution)/shard_map/ppermute | solution.py:304
  49.1 1.9 %collective-permute-start.5 = (bf16[18,8,256]{2,1,0:T(8,128)(2,1)S(1)}, bf16[18,8,256]{2,1,0:T(8,128)(2,1)S(1)}, u32[]{:S(2)}, u32[]{:S(2)}) collective-permute-start(bf16[18,8,256]{2,1,0:T(8,128)(2,1)S(1)} %pad_maximum_fusion.1), channel_id=1, source_target_pairs={{1,0},{2,1},{3,2},{4,3},{5,4},{6,5},{7,6},{8,7},{9,8},{10,9},{11,1... | collective-permute-start | bytes 221192 | tf_op jit(solution)/shard_map/ppermute | solution.py:305
  51.0 3.8 %collective-permute-done.4.gyl_ref = bf16[18,8,256]{2,1,0:T(8,128)(2,1)S(1)} collective-permute-done((bf16[18,8,256]{2,1,0:T(8,128)(2,1)S(1)}, bf16[18,8,256]{2,1,0:T(8,128)(2,1)S(1)}, u32[]{:S(2)}, u32[]{:S(2)}) %collective-permute-start.4) | collective-permute-done | bytes 73760 | tf_op jit(solution)/shard_map/ppermute | solution.py:304
  54.8 0.2 collective-permute-done.5.gyh_ref
  55.1 0.0 copy-start.7
  55.1 0.6 copy-done.7
  55.7 2.8 %all-to-all-done.1.straight_ref = bf16[8,480,128]{2,1,0:T(8,128)(2,1)S(1)} async-done(((bf16[8,480,128]{2,1,0:T(8,128)(2,1)}), bf16[8,480,128]{2,1,0:T(8,128)(2,1)S(1)}, u32[]{:S(2)}, u32[]{:S(2)}) %all-to-all-start.1) | async-done | bytes 983072 | tf_op jit(solution)/shard_map/all_to_all | solution.py:288
  58.5 0.0 collective-permute-done.8.q3_ref
  58.5 0.0 collective-permute-done.7.q2_ref
  58.5 0.0 collective-permute-done.6.q1_ref
  58.5 1.8 %turn.1.mine_ref = bf16[27,128,256]{2,1,0:T(8,128)(2,1)S(1)} custom-call(s32[4]{0:T(128)S(1)} %pad_add_fusion.place_ref, bf16[8,448,128]{2,1,0:T(8,128)(2,1)S(1)} %all-to-all-done.near_ref, bf16[8,96,128]{2,1,0:T(8,128)(2,1)S(1)} %collective-permute-done.6.q1_ref, bf16[8,96,128]{2,1,0:T(8,128)(2,1)S(1)} %collective-permute-done.7.q2_ref, ...), custom_call_target="tpu_custom_call" | custom-call | flops 1000000000 | bytes 4194304 | tf_op jit(solution)/shard_map/turn/pallas_call | solution.py:317
  60.3 0.0 copy-start.1
  60.3 0.0 copy-start.8
  60.3 1.2 collective-permute-start.9
  61.6 2.7 %unpack.1.v3_ref = bf16[22,112,768]{2,1,0:T(8,128)(2,1)S(1)} custom-call(s32[4]{0:T(128)S(1)} %pad_add_fusion.place_ref, bf16[8,448,128]{2,1,0:T(8,128)(2,1)S(1)} %all-to-all-done.near_ref, bf16[8,176,128]{2,1,0:T(8,128)(2,1)} %collective-permute-done.2.low_ref, bf16[8,176,128]{2,1,0:T(8,128)(2,1)S(1)} %collective-permute-done.3.high_ref), custom_call_target="tpu_custom_call" | custom-call | flops 1500000000 | bytes 6291456 | tf_op jit(solution)/shard_map/unpack/pallas_call | solution.py:307
  64.2 0.0 copy-start.3
  64.2 0.6 collective-permute-done.9.other_ref
  64.9 0.0 copy-done.1
  64.9 0.0 copy-done.8
  64.9 18.8 %layers.1 = (bf16[3584,256]{1,0:T(8,128)(2,1)S(1)}, bf16[3584,256]{1,0:T(8,128)(2,1)S(1)}, bf16[18,80,768]{2,1,0:T(8,128)(2,1)S(1)}) custom-call(s32[4]{0:T(128)S(1)} %pad_add_fusion.place_ref, bf16[22,112,768]{2,1,0:T(8,128)(2,1)S(1)} %unpack.1.v3_ref, bf16[27,128,256]{2,1,0:T(8,128)(2,1)S(1)} %turn.1.mine_ref, ...), custom_call_target="tpu_custom_call" | custom-call | flops 16000000000 | bytes 20971520 | tf_op jit(solution)/shard_map/layers/pallas_call | solution.py:328
  83.7 0.7 collective-permute-start.10
  84.3 0.0 copy-done.3
  84.3 4.6 %back.1 = bf16[16,64,256]{2,1,0:T(8,128)(2,1)} custom-call(bf16[18,80,768]{2,1,0:T(8,128)(2,1)S(1)} %get-tuple-element.39.d3_ref, bf16[9,768,256]{2,1,0:T(8,128)(2,1)S(1)} %copy-done.3), custom_call_target="tpu_custom_call" | custom-call | flops 3600000000 | bytes 7340032 | tf_op jit(solution)/shard_map/back/pallas_call | solution.py:350
  88.9 0.0 collective-permute-done.10
  88.9 0.5 add_convert_fusion
  89.5 33.2 %all_to_all.20 = bf16[64,56,256]{2,1,0:T(8,128)(2,1)S(1)} all-to-all(bf16[64,56,256]{2,1,0:T(8,128)(2,1)S(1)} %bitcast.27), channel_id=1, replica_groups=mesh['chan'=8,'slab'=8,'core'=2] {'chan','slab'}, dimensions={0} | all-to-all | bytes 3670016 | tf_op jit(solution)/shard_map/all_to_all | solution.py:363
  122.6 0.3 convert_reduce_fusion
  122.9 0.1 broadcast_in_dim.2
  123.1 29.7 %all_to_all.21 = bf16[64,56,256]{2,1,0:T(8,128)(2,1)S(1)} all-to-all(bf16[64,56,256]{2,1,0:T(8,128)(2,1)S(1)} %broadcast_in_dim.2), channel_id=1, replica_groups=mesh['chan'=8,'slab'=8,'core'=2] {'chan','slab'}, dimensions={0} | all-to-all | bytes 3670016 | tf_op jit(solution)/shard_map/all_to_all | solution.py:367
  152.8 4.0 %collective-permute-start.11 = (bf16[3584,256]{1,0:T(8,128)(2,1)S(1)}, bf16[3584,256]{1,0:T(8,128)(2,1)S(1)}, u32[]{:S(2)}, u32[]{:S(2)}) collective-permute-start(bf16[3584,256]{1,0:T(8,128)(2,1)S(1)} %bitcast.18), channel_id=1, source_target_pairs={{0,1},{1,0},{2,3},{3,2},{4,5},{5,4},{6,7},{7,6},{8,9},{9,8},{10,11... | collective-permute-start | bytes 5505032 | tf_op jit(solution)/shard_map/ppermute | solution.py:368
  156.8 2.5 %finish.2.refs_0_ = f32[27,256,256]{2,1,0:T(8,128)} custom-call(s32[4]{0:T(128)S(1)} %pad_add_fusion.place_ref, bf16[3584,256]{1,0:T(8,128)(2,1)S(1)} %bitcast.19), custom_call_target="tpu_custom_call" | custom-call | flops 1000000000 | bytes 5242880 | tf_op jit(solution)/shard_map/finish/pallas_call | solution.py:372
  159.4 0.9 collective-permute-done.11.sums_ref
  160.3 2.6 %finish.3 = f32[27,256,256]{2,1,0:T(8,128)} custom-call(s32[4]{0:T(128)S(1)} %pad_add_fusion.place_ref, bf16[3584,256]{1,0:T(8,128)(2,1)S(1)} %collective-permute-done.11.sums_ref, f32[27,256,256]{2,1,0:T(8,128)} %finish.2.refs_0_), custom_call_target="tpu_custom_call", output_to_operand_aliasing={{}: (2, {})} | custom-call | flops 1000000000 | bytes 5242880 | tf_op jit(solution)/shard_map/finish/pallas_call | solution.py:372
  (6 shorter events, 0.1 us)
Async XLA Ops:
  0.7 1.0 copy-start.4
  1.8 1.0 copy-start.5
  2.8 10.6 %copy-start.6 = (bf16[16,8,8,256]{3,2,1,0:T(8,128)(2,1)S(1)}, bf16[16,8,8,256]{3,2,1,0:T(8,128)(2,1)}, u32[]{:S(2)}) copy-start(bf16[16,8,8,256]{3,2,1,0:T(8,128)(2,1)} %param.7) | copy-start | bytes 1572868
  5.2 22.5 %all-to-all-start = ((bf16[8,448,128]{2,1,0:T(8,128)(2,1)}), bf16[8,448,128]{2,1,0:T(8,128)(2,1)S(1)}, u32[]{:S(2)}, u32[]{:S(2)}) async-start(bf16[8,448,128]{2,1,0:T(8,128)(2,1)} %get-tuple-element.23), calls=%async_computation | async-start | bytes 1835008 | tf_op jit(solution)/shard_map/all_to_all | solution.py:273
  13.4 12.0 %collective-permute-start.1 = (bf16[1,64,256]{2,1,0:T(8,128)(2,1)S(1)}, bf16[1,64,256]{2,1,0:T(8,128)(2,1)S(1)}, u32[]{:S(2)}, u32[]{:S(2)}) collective-permute-start(bf16[1,64,256]{2,1,0:T(8,128)(2,1)S(1)} %get-tuple-element.48), channel_id=1, source_target_pairs={{16,0},{32,16},{48,32},{64,48},{80,64},{96,80},{112,96},{17,1},{33... | collective-permute-start | bytes 98312 | tf_op jit(solution)/shard_map/ppermute | solution.py:254
  14.7 10.7 %collective-permute-start = (bf16[1,64,256]{2,1,0:T(8,128)(2,1)S(1)}, bf16[1,64,256]{2,1,0:T(8,128)(2,1)S(1)}, u32[]{:S(2)}, u32[]{:S(2)}) collective-permute-start(bf16[1,64,256]{2,1,0:T(8,128)(2,1)S(1)} %get-tuple-element.49), channel_id=1, source_target_pairs={{0,16},{16,32},{32,48},{48,64},{64,80},{80,96},{96,112},{1,17},{17... | collective-permute-start | bytes 98312 | tf_op jit(solution)/shard_map/ppermute | solution.py:253
  20.2 2.0 %copy-start = (bf16[3,3,3,256,256]{4,3,2,1,0:T(8,128)(2,1)S(1)}, bf16[3,3,3,256,256]{4,3,2,1,0:T(8,128)(2,1)}, u32[]{:S(2)}) copy-start(bf16[3,3,3,256,256]{4,3,2,1,0:T(8,128)(2,1)} %param.6) | copy-start | bytes 10616836
  23.6 1.8 %copy-start.2 = (bf16[9,768,256]{2,1,0:T(8,128)(2,1)}, bf16[9,768,256]{2,1,0:T(8,128)(2,1)S(1)}, u32[]{:S(2)}) copy-start(bf16[9,768,256]{2,1,0:T(8,128)(2,1)S(1)} %flip.1.w2_ref) | copy-start | bytes 10616836
  28.6 17.0 %collective-permute-start.3 = (bf16[8,176,128]{2,1,0:T(8,128)(2,1)}, bf16[8,176,128]{2,1,0:T(8,128)(2,1)S(1)}, u32[]{:S(2)}, u32[]{:S(2)}) collective-permute-start(bf16[8,176,128]{2,1,0:T(8,128)(2,1)} %get-tuple-element.44), channel_id=1, source_target_pairs={{1,0},{2,1},{3,2},{4,3},{5,4},{6,5},{7,6},{8,7},{9,8},{10,9},{11,1... | collective-permute-start | bytes 1081352 | tf_op jit(solution)/shard_map/ppermute | solution.py:299
  31.7 13.9 %collective-permute-start.2 = (bf16[8,176,128]{2,1,0:T(8,128)(2,1)}, bf16[8,176,128]{2,1,0:T(8,128)(2,1)}, u32[]{:S(2)}, u32[]{:S(2)}) collective-permute-start(bf16[8,176,128]{2,1,0:T(8,128)(2,1)} %get-tuple-element.45), channel_id=1, source_target_pairs={{0,1},{1,2},{2,3},{3,4},{4,5},{5,6},{6,7},{7,8},{8,9},{9,10},{10,1... | collective-permute-start | bytes 1081352 | tf_op jit(solution)/shard_map/ppermute | solution.py:298
  34.8 23.6 %all-to-all-start.1 = ((bf16[8,480,128]{2,1,0:T(8,128)(2,1)}), bf16[8,480,128]{2,1,0:T(8,128)(2,1)S(1)}, u32[]{:S(2)}, u32[]{:S(2)}) async-start(bf16[8,480,128]{2,1,0:T(8,128)(2,1)} %get-tuple-element.32), calls=%async_computation.1 | async-start | bytes 1966080 | tf_op jit(solution)/shard_map/all_to_all | solution.py:288
  41.4 17.1 %collective-permute-start.8 = (bf16[8,96,128]{2,1,0:T(8,128)(2,1)}, bf16[8,96,128]{2,1,0:T(8,128)(2,1)S(1)}, u32[]{:S(2)}, u32[]{:S(2)}) collective-permute-start(bf16[8,96,128]{2,1,0:T(8,128)(2,1)} %slice.53), channel_id=1, source_target_pairs={{0,6},{2,0},{4,2},{6,4},{8,14},{10,8},{12,10},{14,12},{1,7},{3,1},... | collective-permute-start | bytes 589832 | tf_op jit(solution)/shard_map/ppermute | solution.py:290
  45.0 13.4 %collective-permute-start.7 = (bf16[8,96,128]{2,1,0:T(8,128)(2,1)}, bf16[8,96,128]{2,1,0:T(8,128)(2,1)S(1)}, u32[]{:S(2)}, u32[]{:S(2)}) collective-permute-start(bf16[8,96,128]{2,1,0:T(8,128)(2,1)} %slice.53), channel_id=1, source_target_pairs={{0,4},{2,6},{4,0},{6,2},{8,12},{10,14},{12,8},{14,10},{1,5},{3,7},... | collective-permute-start | bytes 589832 | tf_op jit(solution)/shard_map/ppermute | solution.py:290
  45.0 13.4 %collective-permute-start.6 = (bf16[8,96,128]{2,1,0:T(8,128)(2,1)}, bf16[8,96,128]{2,1,0:T(8,128)(2,1)S(1)}, u32[]{:S(2)}, u32[]{:S(2)}) collective-permute-start(bf16[8,96,128]{2,1,0:T(8,128)(2,1)} %slice.53), channel_id=1, source_target_pairs={{0,2},{2,4},{4,6},{6,0},{8,10},{10,12},{12,14},{14,8},{1,3},{3,5},... | collective-permute-start | bytes 589832 | tf_op jit(solution)/shard_map/ppermute | solution.py:290
  45.6 9.2 %collective-permute-start.4 = (bf16[18,8,256]{2,1,0:T(8,128)(2,1)S(1)}, bf16[18,8,256]{2,1,0:T(8,128)(2,1)S(1)}, u32[]{:S(2)}, u32[]{:S(2)}) collective-permute-start(bf16[18,8,256]{2,1,0:T(8,128)(2,1)S(1)} %pad_maximum_fusion), channel_id=1, source_target_pairs={{0,1},{1,2},{2,3},{3,4},{4,5},{5,6},{6,7},{7,8},{8,9},{9,10},{10,1... | collective-permute-start | bytes 221192 | tf_op jit(solution)/shard_map/ppermute | solution.py:304
  49.1 6.0 %collective-permute-start.5 = (bf16[18,8,256]{2,1,0:T(8,128)(2,1)S(1)}, bf16[18,8,256]{2,1,0:T(8,128)(2,1)S(1)}, u32[]{:S(2)}, u32[]{:S(2)}) collective-permute-start(bf16[18,8,256]{2,1,0:T(8,128)(2,1)S(1)} %pad_maximum_fusion.1), channel_id=1, source_target_pairs={{1,0},{2,1},{3,2},{4,3},{5,4},{6,5},{7,6},{8,7},{9,8},{10,9},{11,1... | collective-permute-start | bytes 221192 | tf_op jit(solution)/shard_map/ppermute | solution.py:305
  55.1 0.6 copy-start.7
  60.3 4.6 %copy-start.1 = (bf16[3,3,3,256,256]{4,3,2,1,0:T(8,128)(2,1)S(1)}, bf16[3,3,3,256,256]{4,3,2,1,0:T(8,128)(2,1)}, u32[]{:S(2)}) copy-start(bf16[3,3,3,256,256]{4,3,2,1,0:T(8,128)(2,1)} %param.6) | copy-start | bytes 10616836
  60.3 4.6 %copy-start.8 = (bf16[18,8,256]{2,1,0:T(8,128)(2,1)S(1)}, bf16[18,8,256]{2,1,0:T(8,128)(2,1)}, u32[]{:S(2)}) copy-start(bf16[18,8,256]{2,1,0:T(8,128)(2,1)} %copy-done.7) | copy-start | bytes 221188
  60.3 4.6 %collective-permute-start.9 = (bf16[27,128,256]{2,1,0:T(8,128)(2,1)S(1)}, bf16[27,128,256]{2,1,0:T(8,128)(2,1)S(1)}, u32[]{:S(2)}, u32[]{:S(2)}) collective-permute-start(bf16[27,128,256]{2,1,0:T(8,128)(2,1)S(1)} %turn.1.mine_ref), channel_id=1, source_target_pairs={{0,1},{1,0},{2,3},{3,2},{4,5},{5,4},{6,7},{7,6},{8,9},{9,8},{10,11... | collective-permute-start | bytes 5308424 | tf_op jit(solution)/shard_map/ppermute | solution.py:326
  64.2 20.1 %copy-start.3 = (bf16[9,768,256]{2,1,0:T(8,128)(2,1)S(1)}, bf16[9,768,256]{2,1,0:T(8,128)(2,1)}, u32[]{:S(2)}) copy-start(bf16[9,768,256]{2,1,0:T(8,128)(2,1)} %copy-done.2) | copy-start | bytes 10616836
  83.7 5.3 %collective-permute-start.10 = (bf16[3584,256]{1,0:T(8,128)(2,1)S(1)}, bf16[3584,256]{1,0:T(8,128)(2,1)S(1)}, u32[]{:S(2)}, u32[]{:S(2)}) collective-permute-start(bf16[3584,256]{1,0:T(8,128)(2,1)S(1)} %get-tuple-element.38), channel_id=1, source_target_pairs={{0,1},{1,0},{2,3},{3,2},{4,5},{5,4},{6,7},{7,6},{8,9},{9,8},{10,11... | collective-permute-start | bytes 5505032 | tf_op jit(solution)/shard_map/ppermute | solution.py:349
  152.8 7.4 %collective-permute-start.11 = (bf16[3584,256]{1,0:T(8,128)(2,1)S(1)}, bf16[3584,256]{1,0:T(8,128)(2,1)S(1)}, u32[]{:S(2)}, u32[]{:S(2)}) collective-permute-start(bf16[3584,256]{1,0:T(8,128)(2,1)S(1)} %bitcast.18), channel_id=1, source_target_pairs={{0,1},{1,0},{2,3},{3,2},{4,5},{5,4},{6,7},{7,6},{8,9},{9,8},{10,11... | collective-permute-start | bytes 5505032 | tf_op jit(solution)/shard_map/ppermute | solution.py:368

commit v4 on v3

--- a/solution.py
+++ b/solution.py
@@ -40,7 +40,7 @@
     return lax.dot_general(a, b, (((1,), (0,)), ((), ())), preferred_element_type=F32)
 
 
-def pack_kernel(place_ref, vol_ref, filters_ref, out_ref, straight_ref, wide_ref):
+def pack_kernel(place_ref, vol_ref, filters_ref, out_ref, wide_ref):
     row = lax.broadcasted_iota(jnp.int32, (176, 128), 0)
     col = lax.broadcasted_iota(jnp.int32, (176, 128), 1)
     c = sum((row >= 22 * n).astype(jnp.int32) for n in range(1, 8))
@@ -52,13 +52,18 @@
     lanes = pl.ds(pl.multiple_of(place_ref[2] * 128, 128), 128)
     mine = pl.ds(STRAIGHT + QUARTER * place_ref[3], QUARTER)
     quarter = filters_ref[mine, :, lanes].reshape(QUARTER * 32, 128)
-    straight = filters_ref[0:STRAIGHT, :, lanes].reshape(STRAIGHT * 32, 128)
     for c in range(8):
         for quad in range(2):
             part = wide_ref[quad, c * 176 : c * 176 + 176, :]
             out_ref[c, quad * 176 : quad * 176 + 176, :] = part.astype(BF)
         out_ref[c, VOL : VOL + QUARTER * 32, :] = quarter
-        straight_ref[c] = straight
+
+
+def straight_kernel(place_ref, filters_ref, out_ref):
+    lanes = pl.ds(pl.multiple_of(place_ref[2] * 128, 128), 128)
+    half = filters_ref[0:STRAIGHT, :, lanes].reshape(STRAIGHT * 32, 128)
+    for c in range(8):
+        out_ref[c] = half
 
 
 def neighbours(value):
@@ -253,23 +258,26 @@
     gxl = lax.ppermute(og[BX - 1 :], "chan", xup)
     gxh = lax.ppermute(og[:1], "chan", xdown)
 
-    packed, straight = pl.pallas_call(
+    w1 = jnp.transpose(first_filters, (0, 1, 2, 4, 3)).reshape(27, 32, C)
+    packed = pl.pallas_call(
         pack_kernel,
-        out_shape=(
-            jax.ShapeDtypeStruct((8, VOL + QUARTER * 32, 128), BF),
-            jax.ShapeDtypeStruct((8, STRAIGHT * 32, 128), BF),
-        ),
+        out_shape=jax.ShapeDtypeStruct((8, VOL + QUARTER * 32, 128), BF),
         in_specs=[SMEM, VMEM, VMEM],
-        out_specs=(VMEM, VMEM),
+        out_specs=VMEM,
         scratch_shapes=[pltpu.VMEM((2, 8 * 176, 128), F32)],
         compiler_params=params(16),
         cost_estimate=cost(16 * 176 * 128 * 256, 3 << 20),
         name="pack",
-    )(
-        place,
-        jnp.transpose(volume, (1, 2, 3, 0)),
-        jnp.transpose(first_filters, (0, 1, 2, 4, 3)).reshape(27, 32, C),
-    )
+    )(place, jnp.transpose(volume, (1, 2, 3, 0)), w1)
+    straight = pl.pallas_call(
+        straight_kernel,
+        out_shape=jax.ShapeDtypeStruct((8, STRAIGHT * 32, 128), BF),
+        in_specs=[SMEM, VMEM],
+        out_specs=VMEM,
+        compiler_params=params(8),
+        cost_estimate=cost(1e6, 2 << 20),
+        name="straight",
+    )(place, w1)
     near = lax.all_to_all(packed, "chan", 0, 0, tiled=True)
 
     w2 = second_filters.reshape(9, 3 * C, C)

time: 164 us -> 164 us (level)
  waiting for transfers between devices: 10.6 us -> 7.57 us
    all_to_all x1, waiting for transfers between devices: 2.77 us -> 0.78 us  [local(): straight = lax.all_to_all(straight, 'chan', 0, 0, tiled=True)]
    all_to_all x1, waiting for transfers between devices: 2.27 us -> 0.61 us  [local(): near = lax.all_to_all(packed, 'chan', 0, 0, tiled=True)]
    all_to_all x1, starting transfers between devices: 5.85 us -> 7.5 us  [local(): straight = lax.all_to_all(straight, 'chan', 0, 0, tiled=True)]
    pallas_call x1 -> x2, Pallas kernels: 2.46 us -> 3.73 us  [the longest x1 2.08 us: local(): pl.pallas_call(pack_kernel, out_shape=jax.ShapeDtypeStruct((8, VOL + QUAR...]
    unnamed x18 -> x20, local copies, waits for them, and re-layouts: 6.49 us -> 6.5 us
  transfers between devices with their start and end apart: 14 -> 14, of which waited for: 6 -> 7; matrix products, arithmetic and copies ran while one was open for 0% -> 0% of each run, Pallas kernels for 7% -> 8%
where the time goes in v4:
time: 164 us
  blocking collectives  64.2 us (39%)
  starting transfers between devices  43.4 us (26%)
  Pallas kernels  38.4 us (23%)
  local copies, waits for them, and re-layouts  8.24 us (5%)
  waiting for transfers between devices  7.57 us (5%)
    all_to_all x1, blocking collectives, local(): shares = lax.all_to_all(both, CHIPS, 0, 0, tiled=True)  34.5 us
    all_to_all x1, blocking collectives, local(): ours = lax.all_to_all(spread, CHIPS, 0, 0, tiled=True).reshape(SLOT, C)  29.8 us
    pallas_call x1, Pallas kernels, local(): pl.pallas_call(layers_kernel, out_shape=(jax.ShapeDtypeStruct((SLOT, C),...  18.8 us
    all_to_all x1, starting transfers between devices, local(): near = lax.all_to_all(packed, 'chan', 0, 0, tiled=True)  8.16 us
    all_to_all x1, starting transfers between devices, local(): straight = lax.all_to_all(straight, 'chan', 0, 0, tiled=True)  7.5 us
    unnamed x20, local copies, waits for them, and re-layouts  6.5 us
    ppermute x1, starting transfers between devices, local(): gxl = lax.ppermute(og[BX - 1:], 'chan', xup)  5.49 us
    pallas_call x2, Pallas kernels, finish(): pl.pallas_call(functools.partial(finish_kernel, own), out_shape=jax.Shape...  5.13 us
  transfers between devices with their start and end apart: 14, of which 7 were waited for; matrix products, arithmetic and copies ran while one was open for 0% of the time, Pallas kernels for 8%

profile of v4, /device:TPU:1, one launch (start us, length us, event | category | flops | bytes accessed | tf_op | source)
XLA Modules:
  0.0 163.7 jit_solution(259327849429322465)
XLA Ops:
  0.6 0.1 pad_add_fusion.place_ref
  0.7 0.0 copy-start.4
  0.7 1.0 copy-done.4
  1.7 0.0 copy-start.6
  1.7 1.0 copy-done.6
  2.8 0.0 copy-start.7
  2.8 2.1 %pack.1 = bf16[8,448,128]{2,1,0:T(8,128)(2,1)} custom-call(s32[4]{0:T(128)S(1)} %pad_add_fusion.place_ref, bf16[8,8,32,128]{3,2,1,0:T(8,128)(2,1)S(1)} %bitcast.24, bf16[27,32,256]{2,1,0:T(8,128)(2,1)S(1)} %bitcast.22), custom_call_target="tpu_custom_call" | custom-call | flops 92274688 | bytes 3145728 | tf_op jit(solution)/shard_map/pack/pallas_call | solution.py:262
  4.9 8.2 %all-to-all-start = ((bf16[8,448,128]{2,1,0:T(8,128)(2,1)}), bf16[8,448,128]{2,1,0:T(8,128)(2,1)S(1)}, u32[]{:S(2)}, u32[]{:S(2)}) async-start(bf16[8,448,128]{2,1,0:T(8,128)(2,1)} %pack.1), calls=%async_computation | async-start | bytes 1835008 | tf_op jit(solution)/shard_map/all_to_all | solution.py:281
  13.0 0.0 copy-done.7
  13.0 1.3 collective-permute-start.1
  14.3 5.5 %collective-permute-start = (bf16[1,64,256]{2,1,0:T(8,128)(2,1)S(1)}, bf16[1,64,256]{2,1,0:T(8,128)(2,1)S(1)}, u32[]{:S(2)}, u32[]{:S(2)}) collective-permute-start(bf16[1,64,256]{2,1,0:T(8,128)(2,1)S(1)} %get-tuple-element.45), channel_id=1, source_target_pairs={{0,16},{16,32},{32,48},{48,64},{64,80},{80,96},{96,112},{1,17},{17... | collective-permute-start | bytes 98312 | tf_op jit(solution)/shard_map/ppermute | solution.py:258
  19.8 0.0 copy-start
  19.9 2.0 %copy-done = bf16[3,3,3,256,256]{4,3,2,1,0:T(8,128)(2,1)S(1)} copy-done((bf16[3,3,3,256,256]{4,3,2,1,0:T(8,128)(2,1)S(1)}, bf16[3,3,3,256,256]{4,3,2,1,0:T(8,128)(2,1)}, u32[]{:S(2)}) %copy-start) | copy-done | bytes 3538968
  21.8 0.0 copy-start.5
  21.8 1.4 flip.1.w2_ref
  23.3 0.0 copy-start.2
  23.3 1.8 %copy-done.2 = bf16[9,768,256]{2,1,0:T(8,128)(2,1)} copy-done((bf16[9,768,256]{2,1,0:T(8,128)(2,1)}, bf16[9,768,256]{2,1,0:T(8,128)(2,1)S(1)}, u32[]{:S(2)}) %copy-start.2) | copy-done | bytes 3538968
  25.0 0.0 copy-done.5
  25.0 1.6 %straight.1 = bf16[8,480,128]{2,1,0:T(8,128)(2,1)} custom-call(s32[4]{0:T(128)S(1)} %pad_add_fusion.place_ref, bf16[27,32,256]{2,1,0:T(8,128)(2,1)S(1)} %bitcast.23), custom_call_target="tpu_custom_call" | custom-call | flops 1000000 | bytes 2097152 | tf_op jit(solution)/shard_map/straight/pallas_call | solution.py:272
  26.7 0.0 collective-permute-done.1.gxh_ref
  26.7 0.0 collective-permute-done.gxl_ref
  26.7 0.6 all-to-all-done.near_ref
  27.3 0.9 fusion
  28.2 3.1 %collective-permute-start.3 = (bf16[8,176,128]{2,1,0:T(8,128)(2,1)}, bf16[8,176,128]{2,1,0:T(8,128)(2,1)S(1)}, u32[]{:S(2)}, u32[]{:S(2)}) collective-permute-start(bf16[8,176,128]{2,1,0:T(8,128)(2,1)} %get-tuple-element.40), channel_id=1, source_target_pairs={{1,0},{2,1},{3,2},{4,3},{5,4},{6,5},{7,6},{8,7},{9,8},{10,9},{11,1... | collective-permute-start | bytes 1081352 | tf_op jit(solution)/shard_map/ppermute | solution.py:307
  31.4 3.1 %collective-permute-start.2 = (bf16[8,176,128]{2,1,0:T(8,128)(2,1)}, bf16[8,176,128]{2,1,0:T(8,128)(2,1)}, u32[]{:S(2)}, u32[]{:S(2)}) collective-permute-start(bf16[8,176,128]{2,1,0:T(8,128)(2,1)} %get-tuple-element.41), channel_id=1, source_target_pairs={{0,1},{1,2},{2,3},{3,4},{4,5},{5,6},{6,7},{7,8},{8,9},{9,10},{10,1... | collective-permute-start | bytes 1081352 | tf_op jit(solution)/shard_map/ppermute | solution.py:306
  34.5 7.5 %all-to-all-start.1 = ((bf16[8,480,128]{2,1,0:T(8,128)(2,1)}), bf16[8,480,128]{2,1,0:T(8,128)(2,1)S(1)}, u32[]{:S(2)}, u32[]{:S(2)}) async-start(bf16[8,480,128]{2,1,0:T(8,128)(2,1)} %straight.1), calls=%async_computation.1 | async-start | bytes 1966080 | tf_op jit(solution)/shard_map/all_to_all | solution.py:296
  42.0 0.7 slice.53
  42.7 3.6 %collective-permute-start.8 = (bf16[8,96,128]{2,1,0:T(8,128)(2,1)}, bf16[8,96,128]{2,1,0:T(8,128)(2,1)S(1)}, u32[]{:S(2)}, u32[]{:S(2)}) collective-permute-start(bf16[8,96,128]{2,1,0:T(8,128)(2,1)} %slice.53), channel_id=1, source_target_pairs={{0,6},{2,0},{4,2},{6,4},{8,14},{10,8},{12,10},{14,12},{1,7},{3,1},... | collective-permute-start | bytes 589832 | tf_op jit(solution)/shard_map/ppermute | solution.py:298
  46.3 0.0 collective-permute-start.7
  46.3 0.6 collective-permute-start.6
  46.9 0.0 collective-permute-done.3.high_ref
  46.9 0.0 collective-permute-done.2.low_ref
  46.9 3.4 %collective-permute-start.4 = (bf16[18,8,256]{2,1,0:T(8,128)(2,1)S(1)}, bf16[18,8,256]{2,1,0:T(8,128)(2,1)S(1)}, u32[]{:S(2)}, u32[]{:S(2)}) collective-permute-start(bf16[18,8,256]{2,1,0:T(8,128)(2,1)S(1)} %pad_maximum_fusion), channel_id=1, source_target_pairs={{0,1},{1,2},{2,3},{3,4},{4,5},{5,6},{6,7},{7,8},{8,9},{9,10},{10,1... | collective-permute-start | bytes 221192 | tf_op jit(solution)/shard_map/ppermute | solution.py:312
  50.4 1.9 %collective-permute-start.5 = (bf16[18,8,256]{2,1,0:T(8,128)(2,1)S(1)}, bf16[18,8,256]{2,1,0:T(8,128)(2,1)S(1)}, u32[]{:S(2)}, u32[]{:S(2)}) collective-permute-start(bf16[18,8,256]{2,1,0:T(8,128)(2,1)S(1)} %pad_maximum_fusion.1), channel_id=1, source_target_pairs={{1,0},{2,1},{3,2},{4,3},{5,4},{6,5},{7,6},{8,7},{9,8},{10,9},{11,1... | collective-permute-start | bytes 221192 | tf_op jit(solution)/shard_map/ppermute | solution.py:313
  52.3 3.8 %collective-permute-done.4.gyl_ref = bf16[18,8,256]{2,1,0:T(8,128)(2,1)S(1)} collective-permute-done((bf16[18,8,256]{2,1,0:T(8,128)(2,1)S(1)}, bf16[18,8,256]{2,1,0:T(8,128)(2,1)S(1)}, u32[]{:S(2)}, u32[]{:S(2)}) %collective-permute-start.4) | collective-permute-done | bytes 73760 | tf_op jit(solution)/shard_map/ppermute | solution.py:312
  56.1 0.2 collective-permute-done.5.gyh_ref
  56.3 0.6 copy-done.8
  57.0 0.8 all-to-all-done.1.straight_ref
  57.7 0.0 collective-permute-done.8.q3_ref
  57.7 0.0 collective-permute-done.7.q2_ref
  57.7 0.9 collective-permute-done.6.q1_ref
  58.6 1.8 %turn.1.mine_ref = bf16[27,128,256]{2,1,0:T(8,128)(2,1)S(1)} custom-call(s32[4]{0:T(128)S(1)} %pad_add_fusion.place_ref, bf16[8,448,128]{2,1,0:T(8,128)(2,1)S(1)} %all-to-all-done.near_ref, bf16[8,96,128]{2,1,0:T(8,128)(2,1)S(1)} %collective-permute-done.6.q1_ref, bf16[8,96,128]{2,1,0:T(8,128)(2,1)S(1)} %collective-permute-done.7.q2_ref, ...), custom_call_target="tpu_custom_call" | custom-call | flops 1000000000 | bytes 4194304 | tf_op jit(solution)/shard_map/turn/pallas_call | solution.py:325
  60.4 0.0 copy-start.1
  60.4 0.0 copy-start.9
  60.4 0.5 collective-permute-start.9
  60.9 2.9 %unpack.1.v3_ref = bf16[22,112,768]{2,1,0:T(8,128)(2,1)S(1)} custom-call(s32[4]{0:T(128)S(1)} %pad_add_fusion.place_ref, bf16[8,448,128]{2,1,0:T(8,128)(2,1)S(1)} %all-to-all-done.near_ref, bf16[8,176,128]{2,1,0:T(8,128)(2,1)} %collective-permute-done.2.low_ref, bf16[8,176,128]{2,1,0:T(8,128)(2,1)S(1)} %collective-permute-done.3.high_ref), custom_call_target="tpu_custom_call" | custom-call | flops 1500000000 | bytes 6291456 | tf_op jit(solution)/shard_map/unpack/pallas_call | solution.py:315
  63.8 0.0 copy-start.3
  63.9 0.4 collective-permute-done.9.other_ref
  64.2 0.0 copy-done.1
  64.2 0.0 copy-done.9
  64.2 18.8 %layers.1 = (bf16[3584,256]{1,0:T(8,128)(2,1)S(1)}, bf16[3584,256]{1,0:T(8,128)(2,1)S(1)}, bf16[18,80,768]{2,1,0:T(8,128)(2,1)S(1)}) custom-call(s32[4]{0:T(128)S(1)} %pad_add_fusion.place_ref, bf16[22,112,768]{2,1,0:T(8,128)(2,1)S(1)} %unpack.1.v3_ref, bf16[27,128,256]{2,1,0:T(8,128)(2,1)S(1)} %turn.1.mine_ref, ...), custom_call_target="tpu_custom_call" | custom-call | flops 16000000000 | bytes 20971520 | tf_op jit(solution)/shard_map/layers/pallas_call | solution.py:336
  83.0 0.7 collective-permute-start.10
  83.7 0.0 copy-done.3
  83.7 4.6 %back.1 = bf16[16,64,256]{2,1,0:T(8,128)(2,1)} custom-call(bf16[18,80,768]{2,1,0:T(8,128)(2,1)S(1)} %get-tuple-element.35.d3_ref, bf16[9,768,256]{2,1,0:T(8,128)(2,1)S(1)} %copy-done.3), custom_call_target="tpu_custom_call" | custom-call | flops 3600000000 | bytes 7340032 | tf_op jit(solution)/shard_map/back/pallas_call | solution.py:358
  88.3 0.0 collective-permute-done.10
  88.3 0.5 add_convert_fusion
  88.8 34.5 %all_to_all.20 = bf16[64,56,256]{2,1,0:T(8,128)(2,1)S(1)} all-to-all(bf16[64,56,256]{2,1,0:T(8,128)(2,1)S(1)} %bitcast.28), channel_id=1, replica_groups=mesh['chan'=8,'slab'=8,'core'=2] {'chan','slab'}, dimensions={0} | all-to-all | bytes 3670016 | tf_op jit(solution)/shard_map/all_to_all | solution.py:371
  123.3 0.3 convert_reduce_fusion
  123.6 0.1 broadcast_in_dim.2
  123.7 29.8 %all_to_all.21 = bf16[64,56,256]{2,1,0:T(8,128)(2,1)S(1)} all-to-all(bf16[64,56,256]{2,1,0:T(8,128)(2,1)S(1)} %broadcast_in_dim.2), channel_id=1, replica_groups=mesh['chan'=8,'slab'=8,'core'=2] {'chan','slab'}, dimensions={0} | all-to-all | bytes 3670016 | tf_op jit(solution)/shard_map/all_to_all | solution.py:375
  153.5 4.0 %collective-permute-start.11 = (bf16[3584,256]{1,0:T(8,128)(2,1)S(1)}, bf16[3584,256]{1,0:T(8,128)(2,1)S(1)}, u32[]{:S(2)}, u32[]{:S(2)}) collective-permute-start(bf16[3584,256]{1,0:T(8,128)(2,1)S(1)} %bitcast.18), channel_id=1, source_target_pairs={{0,1},{1,0},{2,3},{3,2},{4,5},{5,4},{6,7},{7,6},{8,9},{9,8},{10,11... | collective-permute-start | bytes 5505032 | tf_op jit(solution)/shard_map/ppermute | solution.py:376
  157.5 2.5 %finish.2.refs_0_ = f32[27,256,256]{2,1,0:T(8,128)} custom-call(s32[4]{0:T(128)S(1)} %pad_add_fusion.place_ref, bf16[3584,256]{1,0:T(8,128)(2,1)S(1)} %bitcast.19), custom_call_target="tpu_custom_call" | custom-call | flops 1000000000 | bytes 5242880 | tf_op jit(solution)/shard_map/finish/pallas_call | solution.py:380
  160.0 0.9 collective-permute-done.11.sums_ref
  160.9 2.6 %finish.3 = f32[27,256,256]{2,1,0:T(8,128)} custom-call(s32[4]{0:T(128)S(1)} %pad_add_fusion.place_ref, bf16[3584,256]{1,0:T(8,128)(2,1)S(1)} %collective-permute-done.11.sums_ref, f32[27,256,256]{2,1,0:T(8,128)} %finish.2.refs_0_), custom_call_target="tpu_custom_call", output_to_operand_aliasing={{}: (2, {})} | custom-call | flops 1000000000 | bytes 5242880 | tf_op jit(solution)/shard_map/finish/pallas_call | solution.py:380
  (7 shorter events, 0.1 us)
Async XLA Ops:
  0.7 1.0 copy-start.4
  1.7 1.0 copy-start.6
  2.8 10.2 %copy-start.7 = (bf16[16,8,8,256]{3,2,1,0:T(8,128)(2,1)S(1)}, bf16[16,8,8,256]{3,2,1,0:T(8,128)(2,1)}, u32[]{:S(2)}) copy-start(bf16[16,8,8,256]{3,2,1,0:T(8,128)(2,1)} %param.7) | copy-start | bytes 1572868
  4.9 22.5 %all-to-all-start = ((bf16[8,448,128]{2,1,0:T(8,128)(2,1)}), bf16[8,448,128]{2,1,0:T(8,128)(2,1)S(1)}, u32[]{:S(2)}, u32[]{:S(2)}) async-start(bf16[8,448,128]{2,1,0:T(8,128)(2,1)} %pack.1), calls=%async_computation | async-start | bytes 1835008 | tf_op jit(solution)/shard_map/all_to_all | solution.py:281
  13.0 13.7 %collective-permute-start.1 = (bf16[1,64,256]{2,1,0:T(8,128)(2,1)S(1)}, bf16[1,64,256]{2,1,0:T(8,128)(2,1)S(1)}, u32[]{:S(2)}, u32[]{:S(2)}) collective-permute-start(bf16[1,64,256]{2,1,0:T(8,128)(2,1)S(1)} %get-tuple-element.44), channel_id=1, source_target_pairs={{16,0},{32,16},{48,32},{64,48},{80,64},{96,80},{112,96},{17,1},{33... | collective-permute-start | bytes 98312 | tf_op jit(solution)/shard_map/ppermute | solution.py:259
  14.3 12.4 %collective-permute-start = (bf16[1,64,256]{2,1,0:T(8,128)(2,1)S(1)}, bf16[1,64,256]{2,1,0:T(8,128)(2,1)S(1)}, u32[]{:S(2)}, u32[]{:S(2)}) collective-permute-start(bf16[1,64,256]{2,1,0:T(8,128)(2,1)S(1)} %get-tuple-element.45), channel_id=1, source_target_pairs={{0,16},{16,32},{32,48},{48,64},{64,80},{80,96},{96,112},{1,17},{17... | collective-permute-start | bytes 98312 | tf_op jit(solution)/shard_map/ppermute | solution.py:258
  19.8 2.0 %copy-start = (bf16[3,3,3,256,256]{4,3,2,1,0:T(8,128)(2,1)S(1)}, bf16[3,3,3,256,256]{4,3,2,1,0:T(8,128)(2,1)}, u32[]{:S(2)}) copy-start(bf16[3,3,3,256,256]{4,3,2,1,0:T(8,128)(2,1)} %param.6) | copy-start | bytes 10616836
  21.8 3.2 %copy-start.5 = (bf16[3,3,3,256,32]{3,4,2,1,0:T(8,128)(2,1)S(1)}, bf16[3,3,3,256,32]{3,4,2,1,0:T(8,128)(2,1)}, u32[]{:S(2)}) copy-start(bf16[3,3,3,256,32]{3,4,2,1,0:T(8,128)(2,1)} %param.5) | copy-start | bytes 1327108
  23.3 1.8 %copy-start.2 = (bf16[9,768,256]{2,1,0:T(8,128)(2,1)}, bf16[9,768,256]{2,1,0:T(8,128)(2,1)S(1)}, u32[]{:S(2)}) copy-start(bf16[9,768,256]{2,1,0:T(8,128)(2,1)S(1)} %flip.1.w2_ref) | copy-start | bytes 10616836
  28.2 18.7 %collective-permute-start.3 = (bf16[8,176,128]{2,1,0:T(8,128)(2,1)}, bf16[8,176,128]{2,1,0:T(8,128)(2,1)S(1)}, u32[]{:S(2)}, u32[]{:S(2)}) collective-permute-start(bf16[8,176,128]{2,1,0:T(8,128)(2,1)} %get-tuple-element.40), channel_id=1, source_target_pairs={{1,0},{2,1},{3,2},{4,3},{5,4},{6,5},{7,6},{8,7},{9,8},{10,9},{11,1... | collective-permute-start | bytes 1081352 | tf_op jit(solution)/shard_map/ppermute | solution.py:307
  31.4 15.5 %collective-permute-start.2 = (bf16[8,176,128]{2,1,0:T(8,128)(2,1)}, bf16[8,176,128]{2,1,0:T(8,128)(2,1)}, u32[]{:S(2)}, u32[]{:S(2)}) collective-permute-start(bf16[8,176,128]{2,1,0:T(8,128)(2,1)} %get-tuple-element.41), channel_id=1, source_target_pairs={{0,1},{1,2},{2,3},{3,4},{4,5},{5,6},{6,7},{7,8},{8,9},{9,10},{10,1... | collective-permute-start | bytes 1081352 | tf_op jit(solution)/shard_map/ppermute | solution.py:306
  34.5 23.3 %all-to-all-start.1 = ((bf16[8,480,128]{2,1,0:T(8,128)(2,1)}), bf16[8,480,128]{2,1,0:T(8,128)(2,1)S(1)}, u32[]{:S(2)}, u32[]{:S(2)}) async-start(bf16[8,480,128]{2,1,0:T(8,128)(2,1)} %straight.1), calls=%async_computation.1 | async-start | bytes 1966080 | tf_op jit(solution)/shard_map/all_to_all | solution.py:296
  42.7 15.1 %collective-permute-start.8 = (bf16[8,96,128]{2,1,0:T(8,128)(2,1)}, bf16[8,96,128]{2,1,0:T(8,128)(2,1)S(1)}, u32[]{:S(2)}, u32[]{:S(2)}) collective-permute-start(bf16[8,96,128]{2,1,0:T(8,128)(2,1)} %slice.53), channel_id=1, source_target_pairs={{0,6},{2,0},{4,2},{6,4},{8,14},{10,8},{12,10},{14,12},{1,7},{3,1},... | collective-permute-start | bytes 589832 | tf_op jit(solution)/shard_map/ppermute | solution.py:298
  46.3 11.5 %collective-permute-start.7 = (bf16[8,96,128]{2,1,0:T(8,128)(2,1)}, bf16[8,96,128]{2,1,0:T(8,128)(2,1)S(1)}, u32[]{:S(2)}, u32[]{:S(2)}) collective-permute-start(bf16[8,96,128]{2,1,0:T(8,128)(2,1)} %slice.53), channel_id=1, source_target_pairs={{0,4},{2,6},{4,0},{6,2},{8,12},{10,14},{12,8},{14,10},{1,5},{3,7},... | collective-permute-start | bytes 589832 | tf_op jit(solution)/shard_map/ppermute | solution.py:298
  46.3 12.3 %collective-permute-start.6 = (bf16[8,96,128]{2,1,0:T(8,128)(2,1)}, bf16[8,96,128]{2,1,0:T(8,128)(2,1)S(1)}, u32[]{:S(2)}, u32[]{:S(2)}) collective-permute-start(bf16[8,96,128]{2,1,0:T(8,128)(2,1)} %slice.53), channel_id=1, source_target_pairs={{0,2},{2,4},{4,6},{6,0},{8,10},{10,12},{12,14},{14,8},{1,3},{3,5},... | collective-permute-start | bytes 589832 | tf_op jit(solution)/shard_map/ppermute | solution.py:298
  46.9 9.2 %collective-permute-start.4 = (bf16[18,8,256]{2,1,0:T(8,128)(2,1)S(1)}, bf16[18,8,256]{2,1,0:T(8,128)(2,1)S(1)}, u32[]{:S(2)}, u32[]{:S(2)}) collective-permute-start(bf16[18,8,256]{2,1,0:T(8,128)(2,1)S(1)} %pad_maximum_fusion), channel_id=1, source_target_pairs={{0,1},{1,2},{2,3},{3,4},{4,5},{5,6},{6,7},{7,8},{8,9},{9,10},{10,1... | collective-permute-start | bytes 221192 | tf_op jit(solution)/shard_map/ppermute | solution.py:312
  50.4 6.0 %collective-permute-start.5 = (bf16[18,8,256]{2,1,0:T(8,128)(2,1)S(1)}, bf16[18,8,256]{2,1,0:T(8,128)(2,1)S(1)}, u32[]{:S(2)}, u32[]{:S(2)}) collective-permute-start(bf16[18,8,256]{2,1,0:T(8,128)(2,1)S(1)} %pad_maximum_fusion.1), channel_id=1, source_target_pairs={{1,0},{2,1},{3,2},{4,3},{5,4},{6,5},{7,6},{8,7},{9,8},{10,9},{11,1... | collective-permute-start | bytes 221192 | tf_op jit(solution)/shard_map/ppermute | solution.py:313
  56.3 0.6 copy-start.8
  60.4 3.8 %copy-start.1 = (bf16[3,3,3,256,256]{4,3,2,1,0:T(8,128)(2,1)S(1)}, bf16[3,3,3,256,256]{4,3,2,1,0:T(8,128)(2,1)}, u32[]{:S(2)}) copy-start(bf16[3,3,3,256,256]{4,3,2,1,0:T(8,128)(2,1)} %param.6) | copy-start | bytes 10616836
  60.4 3.8 %copy-start.9 = (bf16[18,8,256]{2,1,0:T(8,128)(2,1)S(1)}, bf16[18,8,256]{2,1,0:T(8,128)(2,1)}, u32[]{:S(2)}) copy-start(bf16[18,8,256]{2,1,0:T(8,128)(2,1)} %copy-done.8) | copy-start | bytes 221188
  60.4 3.8 %collective-permute-start.9 = (bf16[27,128,256]{2,1,0:T(8,128)(2,1)S(1)}, bf16[27,128,256]{2,1,0:T(8,128)(2,1)S(1)}, u32[]{:S(2)}, u32[]{:S(2)}) collective-permute-start(bf16[27,128,256]{2,1,0:T(8,128)(2,1)S(1)} %turn.1.mine_ref), channel_id=1, source_target_pairs={{0,1},{1,0},{2,3},{3,2},{4,5},{5,4},{6,7},{7,6},{8,9},{9,8},{10,11... | collective-permute-start | bytes 5308424 | tf_op jit(solution)/shard_map/ppermute | solution.py:334
  63.8 19.9 %copy-start.3 = (bf16[9,768,256]{2,1,0:T(8,128)(2,1)S(1)}, bf16[9,768,256]{2,1,0:T(8,128)(2,1)}, u32[]{:S(2)}) copy-start(bf16[9,768,256]{2,1,0:T(8,128)(2,1)} %copy-done.2) | copy-start | bytes 10616836
  83.0 5.3 %collective-permute-start.10 = (bf16[3584,256]{1,0:T(8,128)(2,1)S(1)}, bf16[3584,256]{1,0:T(8,128)(2,1)S(1)}, u32[]{:S(2)}, u32[]{:S(2)}) collective-permute-start(bf16[3584,256]{1,0:T(8,128)(2,1)S(1)} %get-tuple-element.34), channel_id=1, source_target_pairs={{0,1},{1,0},{2,3},{3,2},{4,5},{5,4},{6,7},{7,6},{8,9},{9,8},{10,11... | collective-permute-start | bytes 5505032 | tf_op jit(solution)/shard_map/ppermute | solution.py:357
  153.5 7.4 %collective-permute-start.11 = (bf16[3584,256]{1,0:T(8,128)(2,1)S(1)}, bf16[3584,256]{1,0:T(8,128)(2,1)S(1)}, u32[]{:S(2)}, u32[]{:S(2)}) collective-permute-start(bf16[3584,256]{1,0:T(8,128)(2,1)S(1)} %bitcast.18), channel_id=1, source_target_pairs={{0,1},{1,0},{2,3},{3,2},{4,5},{5,4},{6,7},{7,6},{8,9},{9,8},{10,11... | collective-permute-start | bytes 5505032 | tf_op jit(solution)/shard_map/ppermute | solution.py:376

commit v5 on v3

--- a/solution.py
+++ b/solution.py
@@ -114,25 +114,25 @@
     chan, space, core = place_ref[0], place_ref[1], place_ref[2]
 
     def first(i, carry):
-        x0 = i * 5
+        x0 = i * 10
         for s in range(9):
-            part = v3_ref[pl.ds(x0 + s // 3, 5), (s % 3) * 8 : (s % 3) * 8 + 96, :]
+            part = v3_ref[pl.ds(x0 + s // 3, 10), (s % 3) * 8 : (s % 3) * 8 + 96, :]
             w = [h[3 * s + k] for k in range(3) for h in (mine_ref, other_ref)]
-            part = dot_n(part.reshape(480, 3 * C), jnp.concatenate(w, axis=0))
+            part = dot_n(part.reshape(960, 3 * C), jnp.concatenate(w, axis=0))
             if s == 0:
                 acc_ref[...] = part
             else:
                 acc_ref[...] += part
         v = acc_ref[...]
         act = (v / (1.0 + jnp.exp(-v))).astype(BF)
-        wide = act.astype(F32).reshape(60, NZ, C)
+        wide = act.astype(F32).reshape(120, NZ, C)
         before, after = neighbours(wide)
-        a3_ref[pl.ds(x0, 5), :, 0:C] = before.reshape(5, 96, C)
-        a3_ref[pl.ds(x0, 5), :, C : 2 * C] = act.reshape(5, 96, C)
-        a3_ref[pl.ds(x0, 5), :, 2 * C : 3 * C] = after.reshape(5, 96, C)
-        return carry
-
-    lax.fori_loop(0, 4, first, 0)
+        a3_ref[pl.ds(x0, 10), :, 0:C] = before.reshape(10, 96, C)
+        a3_ref[pl.ds(x0, 10), :, C : 2 * C] = act.reshape(10, 96, C)
+        a3_ref[pl.ds(x0, 10), :, 2 * C : 3 * C] = after.reshape(10, 96, C)
+        return carry
+
+    lax.fori_loop(0, 2, first, 0)
 
     @pl.when(chan == 0)
     def _():
@@ -157,25 +157,25 @@
     og_ref[:, 72:80, :] = gyh_ref[...]
 
     def second(i, carry):
-        x0 = i * 6
+        x0 = i * 9
         for s in range(9):
-            part = a3_ref[pl.ds(x0 + s // 3, 6), (s % 3) * 8 : (s % 3) * 8 + 80, :]
-            part = dot_n(part.reshape(480, 3 * C), w2_ref[s])
+            part = a3_ref[pl.ds(x0 + s // 3, 9), (s % 3) * 8 : (s % 3) * 8 + 80, :]
+            part = dot_n(part.reshape(720, 3 * C), w2_ref[s])
             if s == 0:
-                acc_ref[...] = part
+                acc_ref[0:720] = part
             else:
-                acc_ref[...] += part
-        v = acc_ref[...]
+                acc_ref[0:720] += part
+        v = acc_ref[0:720]
         sig = 1.0 / (1.0 + jnp.exp(-v))
-        og = og_ref[pl.ds(x0, 6)].reshape(480, C).astype(F32)
+        og = og_ref[pl.ds(x0, 9)].reshape(720, C).astype(F32)
         delta = (og * sig * (1.0 + v * (1.0 - sig))).astype(BF)
-        before, after = neighbours(delta.astype(F32).reshape(60, NZ, C))
-        d3_ref[pl.ds(x0, 6), :, 0:C] = after.reshape(6, 80, C)
-        d3_ref[pl.ds(x0, 6), :, C : 2 * C] = delta.reshape(6, 80, C)
-        d3_ref[pl.ds(x0, 6), :, 2 * C : 3 * C] = before.reshape(6, 80, C)
-        return carry
-
-    lax.fori_loop(0, 3, second, 0)
+        before, after = neighbours(delta.astype(F32).reshape(90, NZ, C))
+        d3_ref[pl.ds(x0, 9), :, 0:C] = after.reshape(9, 80, C)
+        d3_ref[pl.ds(x0, 9), :, C : 2 * C] = delta.reshape(9, 80, C)
+        d3_ref[pl.ds(x0, 9), :, 2 * C : 3 * C] = before.reshape(9, 80, C)
+        return carry
+
+    lax.fori_loop(0, 2, second, 0)
 
     dt_ref[...] = d3_ref[1:17, 8:72, C : 2 * C].reshape(1024, C).T
     for s in range(9):
@@ -336,7 +336,7 @@
         out_specs=(VMEM, VMEM, VMEM),
         scratch_shapes=[
             pltpu.VMEM((20, 96, 3 * C), BF),
-            pltpu.VMEM((480, C), F32),
+            pltpu.VMEM((960, C), F32),
             pltpu.VMEM((18, 80, C), BF),
             pltpu.VMEM((C, 1024), BF),
             pltpu.VMEM((2 * SLOT, C), BF),

time: 164 us -> 163 us (level)
  no operation moved by 1% of the time
where the time goes in v5:
time: 163 us; the launch traced here: 162 us
  blocking collectives  62.9 us (39%)
  starting transfers between devices  42.3 us (26%)
  Pallas kernels  36.5 us (22%)
  waiting for transfers between devices  10.6 us (7%)
  local copies, waits for them, and re-layouts  8.23 us (5%)
    all_to_all x1, blocking collectives, local(): shares = lax.all_to_all(both, CHIPS, 0, 0, tiled=True)  33.2 us
    all_to_all x1, blocking collectives, local(): ours = lax.all_to_all(spread, CHIPS, 0, 0, tiled=True).reshape(SLOT, C)  29.7 us
    pallas_call x1, Pallas kernels, local(): pl.pallas_call(layers_kernel, out_shape=(jax.ShapeDtypeStruct((SLOT, C),...  18.4 us
    all_to_all x1, starting transfers between devices, local(): near = lax.all_to_all(packed, 'chan', 0, 0, tiled=True)  8.17 us
    unnamed x18, local copies, waits for them, and re-layouts  6.49 us
    all_to_all x1, starting transfers between devices, local(): straight = lax.all_to_all(straight, 'chan', 0, 0, tiled=True)  5.85 us
    ppermute x1, starting transfers between devices, local(): gxl = lax.ppermute(og[BX - 1:], 'chan', xup)  5.49 us
    pallas_call x2, Pallas kernels, finish(): pl.pallas_call(functools.partial(finish_kernel, own), out_shape=jax.Shape...  5.13 us
  transfers between devices with their start and end apart: 14, of which 6 were waited for; matrix products, arithmetic and copies ran while one was open for 0% of the time, Pallas kernels for 7%

profile of v5, /device:TPU:1, one launch (start us, length us, event | category | flops | bytes accessed | tf_op | source)
XLA Modules:
  0.0 162.4 jit_solution(10377383671191869610)
XLA Ops:
  0.6 0.1 pad_add_fusion.place_ref
  0.7 0.0 copy-start.4
  0.7 1.0 copy-done.4
  1.8 0.0 copy-start.5
  1.8 1.0 copy-done.5
  2.8 0.0 copy-start.6
  2.8 2.5 %pack.1 = (bf16[8,448,128]{2,1,0:T(8,128)(2,1)}, bf16[8,480,128]{2,1,0:T(8,128)(2,1)}) custom-call(s32[4]{0:T(128)S(1)} %pad_add_fusion.place_ref, bf16[8,8,32,128]{3,2,1,0:T(8,128)(2,1)S(1)} %bitcast.22, bf16[27,32,256]{2,1,0:T(8,128)(2,1)S(1)} %bitcast.23), custom_call_target="tpu_custom_call" | custom-call | flops 92274688 | bytes 3145728 | tf_op jit(solution)/shard_map/pack/pallas_call | solution.py:256
  5.2 8.2 %all-to-all-start = ((bf16[8,448,128]{2,1,0:T(8,128)(2,1)}), bf16[8,448,128]{2,1,0:T(8,128)(2,1)S(1)}, u32[]{:S(2)}, u32[]{:S(2)}) async-start(bf16[8,448,128]{2,1,0:T(8,128)(2,1)} %get-tuple-element.23), calls=%async_computation | async-start | bytes 1835008 | tf_op jit(solution)/shard_map/all_to_all | solution.py:273
  13.4 0.0 copy-done.6
  13.4 1.3 collective-permute-start.1
  14.7 5.5 %collective-permute-start = (bf16[1,64,256]{2,1,0:T(8,128)(2,1)S(1)}, bf16[1,64,256]{2,1,0:T(8,128)(2,1)S(1)}, u32[]{:S(2)}, u32[]{:S(2)}) collective-permute-start(bf16[1,64,256]{2,1,0:T(8,128)(2,1)S(1)} %get-tuple-element.49), channel_id=1, source_target_pairs={{0,16},{16,32},{32,48},{48,64},{64,80},{80,96},{96,112},{1,17},{17... | collective-permute-start | bytes 98312 | tf_op jit(solution)/shard_map/ppermute | solution.py:253
  20.2 0.0 copy-start
  20.2 2.0 %copy-done = bf16[3,3,3,256,256]{4,3,2,1,0:T(8,128)(2,1)S(1)} copy-done((bf16[3,3,3,256,256]{4,3,2,1,0:T(8,128)(2,1)S(1)}, bf16[3,3,3,256,256]{4,3,2,1,0:T(8,128)(2,1)}, u32[]{:S(2)}) %copy-start) | copy-done | bytes 3538968
  22.2 1.4 flip.1.w2_ref
  23.6 0.0 copy-start.2
  23.6 1.8 %copy-done.2 = bf16[9,768,256]{2,1,0:T(8,128)(2,1)} copy-done((bf16[9,768,256]{2,1,0:T(8,128)(2,1)}, bf16[9,768,256]{2,1,0:T(8,128)(2,1)S(1)}, u32[]{:S(2)}) %copy-start.2) | copy-done | bytes 3538968
  25.4 0.0 collective-permute-done.1.gxh_ref
  25.4 0.0 collective-permute-done.gxl_ref
  25.4 2.3 %all-to-all-done.near_ref = bf16[8,448,128]{2,1,0:T(8,128)(2,1)S(1)} async-done(((bf16[8,448,128]{2,1,0:T(8,128)(2,1)}), bf16[8,448,128]{2,1,0:T(8,128)(2,1)S(1)}, u32[]{:S(2)}, u32[]{:S(2)}) %all-to-all-start) | async-done | bytes 917536 | tf_op jit(solution)/shard_map/all_to_all | solution.py:273
  27.7 0.9 fusion
  28.6 3.1 %collective-permute-start.3 = (bf16[8,176,128]{2,1,0:T(8,128)(2,1)}, bf16[8,176,128]{2,1,0:T(8,128)(2,1)S(1)}, u32[]{:S(2)}, u32[]{:S(2)}) collective-permute-start(bf16[8,176,128]{2,1,0:T(8,128)(2,1)} %get-tuple-element.44), channel_id=1, source_target_pairs={{1,0},{2,1},{3,2},{4,3},{5,4},{6,5},{7,6},{8,7},{9,8},{10,9},{11,1... | collective-permute-start | bytes 1081352 | tf_op jit(solution)/shard_map/ppermute | solution.py:299
  31.7 3.1 %collective-permute-start.2 = (bf16[8,176,128]{2,1,0:T(8,128)(2,1)}, bf16[8,176,128]{2,1,0:T(8,128)(2,1)}, u32[]{:S(2)}, u32[]{:S(2)}) collective-permute-start(bf16[8,176,128]{2,1,0:T(8,128)(2,1)} %get-tuple-element.45), channel_id=1, source_target_pairs={{0,1},{1,2},{2,3},{3,4},{4,5},{5,6},{6,7},{7,8},{8,9},{9,10},{10,1... | collective-permute-start | bytes 1081352 | tf_op jit(solution)/shard_map/ppermute | solution.py:298
  34.8 5.8 %all-to-all-start.1 = ((bf16[8,480,128]{2,1,0:T(8,128)(2,1)}), bf16[8,480,128]{2,1,0:T(8,128)(2,1)S(1)}, u32[]{:S(2)}, u32[]{:S(2)}) async-start(bf16[8,480,128]{2,1,0:T(8,128)(2,1)} %get-tuple-element.32), calls=%async_computation.1 | async-start | bytes 1966080 | tf_op jit(solution)/shard_map/all_to_all | solution.py:288
  40.7 0.7 slice.53
  41.4 3.6 %collective-permute-start.8 = (bf16[8,96,128]{2,1,0:T(8,128)(2,1)}, bf16[8,96,128]{2,1,0:T(8,128)(2,1)S(1)}, u32[]{:S(2)}, u32[]{:S(2)}) collective-permute-start(bf16[8,96,128]{2,1,0:T(8,128)(2,1)} %slice.53), channel_id=1, source_target_pairs={{0,6},{2,0},{4,2},{6,4},{8,14},{10,8},{12,10},{14,12},{1,7},{3,1},... | collective-permute-start | bytes 589832 | tf_op jit(solution)/shard_map/ppermute | solution.py:290
  45.0 0.0 collective-permute-start.7
  45.0 0.6 collective-permute-start.6
  45.6 0.0 collective-permute-done.3.high_ref
  45.6 0.0 collective-permute-done.2.low_ref
  45.6 3.4 %collective-permute-start.4 = (bf16[18,8,256]{2,1,0:T(8,128)(2,1)S(1)}, bf16[18,8,256]{2,1,0:T(8,128)(2,1)S(1)}, u32[]{:S(2)}, u32[]{:S(2)}) collective-permute-start(bf16[18,8,256]{2,1,0:T(8,128)(2,1)S(1)} %pad_maximum_fusion), channel_id=1, source_target_pairs={{0,1},{1,2},{2,3},{3,4},{4,5},{5,6},{6,7},{7,8},{8,9},{9,10},{10,1... | collective-permute-start | bytes 221192 | tf_op jit(solution)/shard_map/ppermute | solution.py:304
  49.1 1.9 %collective-permute-start.5 = (bf16[18,8,256]{2,1,0:T(8,128)(2,1)S(1)}, bf16[18,8,256]{2,1,0:T(8,128)(2,1)S(1)}, u32[]{:S(2)}, u32[]{:S(2)}) collective-permute-start(bf16[18,8,256]{2,1,0:T(8,128)(2,1)S(1)} %pad_maximum_fusion.1), channel_id=1, source_target_pairs={{1,0},{2,1},{3,2},{4,3},{5,4},{6,5},{7,6},{8,7},{9,8},{10,9},{11,1... | collective-permute-start | bytes 221192 | tf_op jit(solution)/shard_map/ppermute | solution.py:305
  51.0 3.8 %collective-permute-done.4.gyl_ref = bf16[18,8,256]{2,1,0:T(8,128)(2,1)S(1)} collective-permute-done((bf16[18,8,256]{2,1,0:T(8,128)(2,1)S(1)}, bf16[18,8,256]{2,1,0:T(8,128)(2,1)S(1)}, u32[]{:S(2)}, u32[]{:S(2)}) %collective-permute-start.4) | collective-permute-done | bytes 73760 | tf_op jit(solution)/shard_map/ppermute | solution.py:304
  54.8 0.2 collective-permute-done.5.gyh_ref
  55.1 0.0 copy-start.7
  55.1 0.6 copy-done.7
  55.7 2.8 %all-to-all-done.1.straight_ref = bf16[8,480,128]{2,1,0:T(8,128)(2,1)S(1)} async-done(((bf16[8,480,128]{2,1,0:T(8,128)(2,1)}), bf16[8,480,128]{2,1,0:T(8,128)(2,1)S(1)}, u32[]{:S(2)}, u32[]{:S(2)}) %all-to-all-start.1) | async-done | bytes 983072 | tf_op jit(solution)/shard_map/all_to_all | solution.py:288
  58.5 0.0 collective-permute-done.8.q3_ref
  58.5 0.0 collective-permute-done.7.q2_ref
  58.5 0.0 collective-permute-done.6.q1_ref
  58.5 1.8 %turn.1.mine_ref = bf16[27,128,256]{2,1,0:T(8,128)(2,1)S(1)} custom-call(s32[4]{0:T(128)S(1)} %pad_add_fusion.place_ref, bf16[8,448,128]{2,1,0:T(8,128)(2,1)S(1)} %all-to-all-done.near_ref, bf16[8,96,128]{2,1,0:T(8,128)(2,1)S(1)} %collective-permute-done.6.q1_ref, bf16[8,96,128]{2,1,0:T(8,128)(2,1)S(1)} %collective-permute-done.7.q2_ref, ...), custom_call_target="tpu_custom_call" | custom-call | flops 1000000000 | bytes 4194304 | tf_op jit(solution)/shard_map/turn/pallas_call | solution.py:317
  60.3 0.0 copy-start.1
  60.3 0.0 copy-start.8
  60.3 1.2 collective-permute-start.9
  61.6 2.7 %unpack.1.v3_ref = bf16[22,112,768]{2,1,0:T(8,128)(2,1)S(1)} custom-call(s32[4]{0:T(128)S(1)} %pad_add_fusion.place_ref, bf16[8,448,128]{2,1,0:T(8,128)(2,1)S(1)} %all-to-all-done.near_ref, bf16[8,176,128]{2,1,0:T(8,128)(2,1)} %collective-permute-done.2.low_ref, bf16[8,176,128]{2,1,0:T(8,128)(2,1)S(1)} %collective-permute-done.3.high_ref), custom_call_target="tpu_custom_call" | custom-call | flops 1500000000 | bytes 6291456 | tf_op jit(solution)/shard_map/unpack/pallas_call | solution.py:307
  64.2 0.0 copy-start.3
  64.2 0.6 collective-permute-done.9.other_ref
  64.9 0.0 copy-done.1
  64.9 0.0 copy-done.8
  64.9 18.4 %layers.1 = (bf16[3584,256]{1,0:T(8,128)(2,1)S(1)}, bf16[3584,256]{1,0:T(8,128)(2,1)S(1)}, bf16[18,80,768]{2,1,0:T(8,128)(2,1)S(1)}) custom-call(s32[4]{0:T(128)S(1)} %pad_add_fusion.place_ref, bf16[22,112,768]{2,1,0:T(8,128)(2,1)S(1)} %unpack.1.v3_ref, bf16[27,128,256]{2,1,0:T(8,128)(2,1)S(1)} %turn.1.mine_ref, ...), custom_call_target="tpu_custom_call" | custom-call | flops 16000000000 | bytes 20971520 | tf_op jit(solution)/shard_map/layers/pallas_call | solution.py:328
  83.3 0.5 collective-permute-start.10
  83.8 0.0 copy-done.3
  83.8 4.6 %back.1 = bf16[16,64,256]{2,1,0:T(8,128)(2,1)} custom-call(bf16[18,80,768]{2,1,0:T(8,128)(2,1)S(1)} %get-tuple-element.39.d3_ref, bf16[9,768,256]{2,1,0:T(8,128)(2,1)S(1)} %copy-done.3), custom_call_target="tpu_custom_call" | custom-call | flops 3600000000 | bytes 7340032 | tf_op jit(solution)/shard_map/back/pallas_call | solution.py:350
  88.4 0.0 collective-permute-done.10
  88.4 0.5 add_convert_fusion
  88.9 33.2 %all_to_all.20 = bf16[64,56,256]{2,1,0:T(8,128)(2,1)S(1)} all-to-all(bf16[64,56,256]{2,1,0:T(8,128)(2,1)S(1)} %bitcast.27), channel_id=1, replica_groups=mesh['chan'=8,'slab'=8,'core'=2] {'chan','slab'}, dimensions={0} | all-to-all | bytes 3670016 | tf_op jit(solution)/shard_map/all_to_all | solution.py:363
  122.1 0.3 convert_reduce_fusion
  122.4 0.1 broadcast_in_dim.2
  122.5 29.7 %all_to_all.21 = bf16[64,56,256]{2,1,0:T(8,128)(2,1)S(1)} all-to-all(bf16[64,56,256]{2,1,0:T(8,128)(2,1)S(1)} %broadcast_in_dim.2), channel_id=1, replica_groups=mesh['chan'=8,'slab'=8,'core'=2] {'chan','slab'}, dimensions={0} | all-to-all | bytes 3670016 | tf_op jit(solution)/shard_map/all_to_all | solution.py:367
  152.2 4.0 %collective-permute-start.11 = (bf16[3584,256]{1,0:T(8,128)(2,1)S(1)}, bf16[3584,256]{1,0:T(8,128)(2,1)S(1)}, u32[]{:S(2)}, u32[]{:S(2)}) collective-permute-start(bf16[3584,256]{1,0:T(8,128)(2,1)S(1)} %bitcast.18), channel_id=1, source_target_pairs={{0,1},{1,0},{2,3},{3,2},{4,5},{5,4},{6,7},{7,6},{8,9},{9,8},{10,11... | collective-permute-start | bytes 5505032 | tf_op jit(solution)/shard_map/ppermute | solution.py:368
  156.3 2.5 %finish.2.refs_0_ = f32[27,256,256]{2,1,0:T(8,128)} custom-call(s32[4]{0:T(128)S(1)} %pad_add_fusion.place_ref, bf16[3584,256]{1,0:T(8,128)(2,1)S(1)} %bitcast.19), custom_call_target="tpu_custom_call" | custom-call | flops 1000000000 | bytes 5242880 | tf_op jit(solution)/shard_map/finish/pallas_call | solution.py:372
  158.8 0.9 collective-permute-done.11.sums_ref
  159.7 2.6 %finish.3 = f32[27,256,256]{2,1,0:T(8,128)} custom-call(s32[4]{0:T(128)S(1)} %pad_add_fusion.place_ref, bf16[3584,256]{1,0:T(8,128)(2,1)S(1)} %collective-permute-done.11.sums_ref, f32[27,256,256]{2,1,0:T(8,128)} %finish.2.refs_0_), custom_call_target="tpu_custom_call", output_to_operand_aliasing={{}: (2, {})} | custom-call | flops 1000000000 | bytes 5242880 | tf_op jit(solution)/shard_map/finish/pallas_call | solution.py:372
  (6 shorter events, 0.1 us)
Async XLA Ops:
  0.7 1.0 copy-start.4
  1.8 1.0 copy-start.5
  2.8 10.6 %copy-start.6 = (bf16[16,8,8,256]{3,2,1,0:T(8,128)(2,1)S(1)}, bf16[16,8,8,256]{3,2,1,0:T(8,128)(2,1)}, u32[]{:S(2)}) copy-start(bf16[16,8,8,256]{3,2,1,0:T(8,128)(2,1)} %param.7) | copy-start | bytes 1572868
  5.2 22.5 %all-to-all-start = ((bf16[8,448,128]{2,1,0:T(8,128)(2,1)}), bf16[8,448,128]{2,1,0:T(8,128)(2,1)S(1)}, u32[]{:S(2)}, u32[]{:S(2)}) async-start(bf16[8,448,128]{2,1,0:T(8,128)(2,1)} %get-tuple-element.23), calls=%async_computation | async-start | bytes 1835008 | tf_op jit(solution)/shard_map/all_to_all | solution.py:273
  13.4 12.0 %collective-permute-start.1 = (bf16[1,64,256]{2,1,0:T(8,128)(2,1)S(1)}, bf16[1,64,256]{2,1,0:T(8,128)(2,1)S(1)}, u32[]{:S(2)}, u32[]{:S(2)}) collective-permute-start(bf16[1,64,256]{2,1,0:T(8,128)(2,1)S(1)} %get-tuple-element.48), channel_id=1, source_target_pairs={{16,0},{32,16},{48,32},{64,48},{80,64},{96,80},{112,96},{17,1},{33... | collective-permute-start | bytes 98312 | tf_op jit(solution)/shard_map/ppermute | solution.py:254
  14.7 10.7 %collective-permute-start = (bf16[1,64,256]{2,1,0:T(8,128)(2,1)S(1)}, bf16[1,64,256]{2,1,0:T(8,128)(2,1)S(1)}, u32[]{:S(2)}, u32[]{:S(2)}) collective-permute-start(bf16[1,64,256]{2,1,0:T(8,128)(2,1)S(1)} %get-tuple-element.49), channel_id=1, source_target_pairs={{0,16},{16,32},{32,48},{48,64},{64,80},{80,96},{96,112},{1,17},{17... | collective-permute-start | bytes 98312 | tf_op jit(solution)/shard_map/ppermute | solution.py:253
  20.2 2.0 %copy-start = (bf16[3,3,3,256,256]{4,3,2,1,0:T(8,128)(2,1)S(1)}, bf16[3,3,3,256,256]{4,3,2,1,0:T(8,128)(2,1)}, u32[]{:S(2)}) copy-start(bf16[3,3,3,256,256]{4,3,2,1,0:T(8,128)(2,1)} %param.6) | copy-start | bytes 10616836
  23.6 1.8 %copy-start.2 = (bf16[9,768,256]{2,1,0:T(8,128)(2,1)}, bf16[9,768,256]{2,1,0:T(8,128)(2,1)S(1)}, u32[]{:S(2)}) copy-start(bf16[9,768,256]{2,1,0:T(8,128)(2,1)S(1)} %flip.1.w2_ref) | copy-start | bytes 10616836
  28.6 17.0 %collective-permute-start.3 = (bf16[8,176,128]{2,1,0:T(8,128)(2,1)}, bf16[8,176,128]{2,1,0:T(8,128)(2,1)S(1)}, u32[]{:S(2)}, u32[]{:S(2)}) collective-permute-start(bf16[8,176,128]{2,1,0:T(8,128)(2,1)} %get-tuple-element.44), channel_id=1, source_target_pairs={{1,0},{2,1},{3,2},{4,3},{5,4},{6,5},{7,6},{8,7},{9,8},{10,9},{11,1... | collective-permute-start | bytes 1081352 | tf_op jit(solution)/shard_map/ppermute | solution.py:299
  31.7 13.9 %collective-permute-start.2 = (bf16[8,176,128]{2,1,0:T(8,128)(2,1)}, bf16[8,176,128]{2,1,0:T(8,128)(2,1)}, u32[]{:S(2)}, u32[]{:S(2)}) collective-permute-start(bf16[8,176,128]{2,1,0:T(8,128)(2,1)} %get-tuple-element.45), channel_id=1, source_target_pairs={{0,1},{1,2},{2,3},{3,4},{4,5},{5,6},{6,7},{7,8},{8,9},{9,10},{10,1... | collective-permute-start | bytes 1081352 | tf_op jit(solution)/shard_map/ppermute | solution.py:298
  34.8 23.6 %all-to-all-start.1 = ((bf16[8,480,128]{2,1,0:T(8,128)(2,1)}), bf16[8,480,128]{2,1,0:T(8,128)(2,1)S(1)}, u32[]{:S(2)}, u32[]{:S(2)}) async-start(bf16[8,480,128]{2,1,0:T(8,128)(2,1)} %get-tuple-element.32), calls=%async_computation.1 | async-start | bytes 1966080 | tf_op jit(solution)/shard_map/all_to_all | solution.py:288
  41.4 17.1 %collective-permute-start.8 = (bf16[8,96,128]{2,1,0:T(8,128)(2,1)}, bf16[8,96,128]{2,1,0:T(8,128)(2,1)S(1)}, u32[]{:S(2)}, u32[]{:S(2)}) collective-permute-start(bf16[8,96,128]{2,1,0:T(8,128)(2,1)} %slice.53), channel_id=1, source_target_pairs={{0,6},{2,0},{4,2},{6,4},{8,14},{10,8},{12,10},{14,12},{1,7},{3,1},... | collective-permute-start | bytes 589832 | tf_op jit(solution)/shard_map/ppermute | solution.py:290
  45.0 13.4 %collective-permute-start.7 = (bf16[8,96,128]{2,1,0:T(8,128)(2,1)}, bf16[8,96,128]{2,1,0:T(8,128)(2,1)S(1)}, u32[]{:S(2)}, u32[]{:S(2)}) collective-permute-start(bf16[8,96,128]{2,1,0:T(8,128)(2,1)} %slice.53), channel_id=1, source_target_pairs={{0,4},{2,6},{4,0},{6,2},{8,12},{10,14},{12,8},{14,10},{1,5},{3,7},... | collective-permute-start | bytes 589832 | tf_op jit(solution)/shard_map/ppermute | solution.py:290
  45.0 13.4 %collective-permute-start.6 = (bf16[8,96,128]{2,1,0:T(8,128)(2,1)}, bf16[8,96,128]{2,1,0:T(8,128)(2,1)S(1)}, u32[]{:S(2)}, u32[]{:S(2)}) collective-permute-start(bf16[8,96,128]{2,1,0:T(8,128)(2,1)} %slice.53), channel_id=1, source_target_pairs={{0,2},{2,4},{4,6},{6,0},{8,10},{10,12},{12,14},{14,8},{1,3},{3,5},... | collective-permute-start | bytes 589832 | tf_op jit(solution)/shard_map/ppermute | solution.py:290
  45.6 9.2 %collective-permute-start.4 = (bf16[18,8,256]{2,1,0:T(8,128)(2,1)S(1)}, bf16[18,8,256]{2,1,0:T(8,128)(2,1)S(1)}, u32[]{:S(2)}, u32[]{:S(2)}) collective-permute-start(bf16[18,8,256]{2,1,0:T(8,128)(2,1)S(1)} %pad_maximum_fusion), channel_id=1, source_target_pairs={{0,1},{1,2},{2,3},{3,4},{4,5},{5,6},{6,7},{7,8},{8,9},{9,10},{10,1... | collective-permute-start | bytes 221192 | tf_op jit(solution)/shard_map/ppermute | solution.py:304
  49.1 6.0 %collective-permute-start.5 = (bf16[18,8,256]{2,1,0:T(8,128)(2,1)S(1)}, bf16[18,8,256]{2,1,0:T(8,128)(2,1)S(1)}, u32[]{:S(2)}, u32[]{:S(2)}) collective-permute-start(bf16[18,8,256]{2,1,0:T(8,128)(2,1)S(1)} %pad_maximum_fusion.1), channel_id=1, source_target_pairs={{1,0},{2,1},{3,2},{4,3},{5,4},{6,5},{7,6},{8,7},{9,8},{10,9},{11,1... | collective-permute-start | bytes 221192 | tf_op jit(solution)/shard_map/ppermute | solution.py:305
  55.1 0.6 copy-start.7
  60.3 4.6 %copy-start.1 = (bf16[3,3,3,256,256]{4,3,2,1,0:T(8,128)(2,1)S(1)}, bf16[3,3,3,256,256]{4,3,2,1,0:T(8,128)(2,1)}, u32[]{:S(2)}) copy-start(bf16[3,3,3,256,256]{4,3,2,1,0:T(8,128)(2,1)} %param.6) | copy-start | bytes 10616836
  60.3 4.6 %copy-start.8 = (bf16[18,8,256]{2,1,0:T(8,128)(2,1)S(1)}, bf16[18,8,256]{2,1,0:T(8,128)(2,1)}, u32[]{:S(2)}) copy-start(bf16[18,8,256]{2,1,0:T(8,128)(2,1)} %copy-done.7) | copy-start | bytes 221188
  60.3 4.6 %collective-permute-start.9 = (bf16[27,128,256]{2,1,0:T(8,128)(2,1)S(1)}, bf16[27,128,256]{2,1,0:T(8,128)(2,1)S(1)}, u32[]{:S(2)}, u32[]{:S(2)}) collective-permute-start(bf16[27,128,256]{2,1,0:T(8,128)(2,1)S(1)} %turn.1.mine_ref), channel_id=1, source_target_pairs={{0,1},{1,0},{2,3},{3,2},{4,5},{5,4},{6,7},{7,6},{8,9},{9,8},{10,11... | collective-permute-start | bytes 5308424 | tf_op jit(solution)/shard_map/ppermute | solution.py:326
  64.2 19.5 %copy-start.3 = (bf16[9,768,256]{2,1,0:T(8,128)(2,1)S(1)}, bf16[9,768,256]{2,1,0:T(8,128)(2,1)}, u32[]{:S(2)}) copy-start(bf16[9,768,256]{2,1,0:T(8,128)(2,1)} %copy-done.2) | copy-start | bytes 10616836
  83.3 5.1 %collective-permute-start.10 = (bf16[3584,256]{1,0:T(8,128)(2,1)S(1)}, bf16[3584,256]{1,0:T(8,128)(2,1)S(1)}, u32[]{:S(2)}, u32[]{:S(2)}) collective-permute-start(bf16[3584,256]{1,0:T(8,128)(2,1)S(1)} %get-tuple-element.38), channel_id=1, source_target_pairs={{0,1},{1,0},{2,3},{3,2},{4,5},{5,4},{6,7},{7,6},{8,9},{9,8},{10,11... | collective-permute-start | bytes 5505032 | tf_op jit(solution)/shard_map/ppermute | solution.py:349
  152.2 7.4 %collective-permute-start.11 = (bf16[3584,256]{1,0:T(8,128)(2,1)S(1)}, bf16[3584,256]{1,0:T(8,128)(2,1)S(1)}, u32[]{:S(2)}, u32[]{:S(2)}) collective-permute-start(bf16[3584,256]{1,0:T(8,128)(2,1)S(1)} %bitcast.18), channel_id=1, source_target_pairs={{0,1},{1,0},{2,3},{3,2},{4,5},{5,4},{6,7},{7,6},{8,9},{9,8},{10,11... | collective-permute-start | bytes 5505032 | tf_op jit(solution)/shard_map/ppermute | solution.py:368
